TPU v7x, 512 devices: a whole 4x8x8 slice. The times are simulated.
512 devices in a mesh: dp: 16 (over z, core), expert: 32 (over y, x).
Axes of the slice: x: 4, y: 8, z: 8, core: 2. Of those that a mesh axis runs over, the one named last changes fastest.
Arguments:
- tokens: bfloat16 [65536, 2048], P(('dp', 'expert')), may hold values from -6 to 6
- gates: float32 [65536, 2], P(('dp', 'expert')), may hold values from 0.1 to 1
- experts: int32 [65536, 2], P(('dp', 'expert')), may hold values from 0 to 31, all different within a row; in each aligned block of 128 rows (0 to 127, 128 to 255, ...) at most 12 rows name the same one
- gate_weight: bfloat16 [32, 2048, 512], P('expert', 'dp'), may hold values from -0.125 to 0.125
- up_weight: bfloat16 [32, 2048, 512], P('expert', 'dp'), may hold values from -0.125 to 0.125
- down_weight: bfloat16 [32, 2048, 512], P('expert', 'dp'), may hold values from -0.25 to 0.25
- out_grad: bfloat16 [65536, 2048], P(('dp', 'expert')), may hold values from -6 to 6
Outputs:
- mixed: bfloat16 [65536, 2048], P(('dp', 'expert'))
- token_grad: bfloat16 [65536, 2048], P(('dp', 'expert'))
- gate_grad: float32 [65536, 2], P(('dp', 'expert'))
- gate_weight_grad: float32 [32, 2048, 512], P('expert', 'dp')
- up_weight_grad: float32 [32, 2048, 512], P('expert', 'dp')
Inputs may be any that keep to these rules, and one draw needn't show every extreme that they name: The two experts of a token differ. Among the tokens of one device (aligned blocks of 128 rows) no expert is named by more than 12 picks, a bound that some block reaches.
All inputs are finite; a program needn't handle non-finite values.
Results may differ from a plain program's by a relative error of at most 0.02.
Values may be sent and summed in bfloat16 or wider, within the bound.
No kernel may reach another device: no remote copies, remote signals or barrier semaphores. Data moves between devices by JAX's collectives and lax.ppermute only.
A program may use at most 64 MiB of HBM per device.

v0:
```python
import jax
import jax.numpy as jnp
from jax import lax
from jax.sharding import PartitionSpec as P


def slot_tables(block_ids, experts_all, capacity):
    picked_ids = block_ids.reshape(-1)
    pick_count = picked_ids.shape[0]
    onehot = (picked_ids[:, None] == jnp.arange(experts_all, dtype=jnp.int32)[None, :]).astype(
        jnp.int32
    )
    before = jnp.cumsum(onehot, axis=0) - onehot
    slot_index = jnp.sum(before * onehot, axis=1)
    flat_slot = picked_ids * capacity + slot_index
    slot_owner = jnp.full((experts_all * capacity,), pick_count, jnp.int32)
    slot_owner = slot_owner.at[flat_slot].set(jnp.arange(pick_count, dtype=jnp.int32))
    return (slot_owner, flat_slot)


def contract_rows(left, right):
    return lax.dot_general(
        left, right, (((0,), (0,)), ((), ())), preferred_element_type=jnp.float32
    )


def contract_cols(left, right):
    return lax.dot_general(
        left, right, (((1,), (1,)), ((), ())), preferred_element_type=jnp.float32
    )


def on_device(tokens, gates, experts, gate_weight, up_weight, down_weight, out_grad):
    tok_count = tokens.shape[0]
    width = tokens.shape[1]
    experts_all = lax.axis_size("expert") * gate_weight.shape[0]
    capacity = 3 * tok_count // experts_all
    pick_count = 2 * tok_count
    slot_owner, flat_slot = slot_tables(experts, experts_all, capacity)
    owner_tok = jnp.where(slot_owner < pick_count, slot_owner // 2, tok_count)
    tok_pad = jnp.concatenate([tokens, jnp.zeros((1, width), tokens.dtype)], axis=0)
    send_rows = tok_pad[owner_tok].reshape(experts_all, capacity, width)
    full_gate, full_up, full_down = (
        lax.all_gather(gate_weight, "dp", axis=1, tiled=True),
        lax.all_gather(up_weight, "dp", axis=1, tiled=True),
        lax.all_gather(down_weight, "dp", axis=1, tiled=True),
    )
    w_gate = full_gate[0]
    w_up = full_up[0]
    w_down = full_down[0]
    hid_width = w_gate.shape[1]
    received = lax.all_to_all(send_rows, "expert", split_axis=0, concat_axis=0, tiled=True)
    sources = received.shape[0]
    items = received.shape[1]
    expert_rows_in = received.reshape(-1, width)
    gate_pre = jnp.dot(expert_rows_in, w_gate, preferred_element_type=jnp.float32)
    up_pre = jnp.dot(expert_rows_in, w_up, preferred_element_type=jnp.float32)
    hidden = (gate_pre * jax.nn.sigmoid(gate_pre) * up_pre).astype(jnp.bfloat16)
    expert_out = contract_cols(hidden, w_down).astype(jnp.bfloat16)
    expert_out, gate_pre, up_pre, hidden = (
        expert_out.reshape(sources, items, width),
        gate_pre.reshape(sources, items, hid_width),
        up_pre.reshape(sources, items, hid_width),
        hidden.reshape(sources, items, hid_width),
    )
    returned = lax.all_to_all(expert_out, "expert", split_axis=0, concat_axis=0, tiled=True)
    rows_in = received.reshape(-1, width)
    gate_pre = gate_pre.reshape(-1, hid_width)
    up_pre = up_pre.reshape(-1, hid_width)
    picked_out = (
        returned.reshape(-1, width)[flat_slot].astype(jnp.float32).reshape(tok_count, 2, width)
    )
    mixed = jnp.sum(gates[:, :, None] * picked_out, axis=1).astype(jnp.bfloat16)
    gate_grad = jnp.sum(out_grad.astype(jnp.float32)[:, None, :] * picked_out, axis=2)
    grad_pad = jnp.concatenate([out_grad, jnp.zeros((1, width), out_grad.dtype)], axis=0)
    gate_pad = jnp.concatenate([gates.reshape(-1), jnp.zeros((1,), jnp.float32)], axis=0)
    send_grad = (gate_pad[slot_owner][:, None] * grad_pad[owner_tok].astype(jnp.float32)).astype(
        jnp.bfloat16
    )
    send_grad = send_grad.reshape(experts_all, capacity, width)
    slot_grad = lax.all_to_all(
        send_grad, "expert", split_axis=0, concat_axis=0, tiled=True
    ).reshape(-1, width)
    hidden_grad = jnp.dot(slot_grad, w_down, preferred_element_type=jnp.float32)
    sigma_gate = jax.nn.sigmoid(gate_pre)
    up_grad = (hidden_grad * gate_pre * sigma_gate).astype(jnp.bfloat16)
    pre_grad = (hidden_grad * up_pre * sigma_gate * (1.0 + gate_pre * (1.0 - sigma_gate))).astype(
        jnp.bfloat16
    )
    row_grad = (contract_cols(pre_grad, w_gate) + contract_cols(up_grad, w_up)).astype(jnp.bfloat16)
    back_grad = lax.all_to_all(
        row_grad.reshape(experts_all, capacity, width),
        "expert",
        split_axis=0,
        concat_axis=0,
        tiled=True,
    )
    picked_grad = (
        back_grad.reshape(-1, width)[flat_slot].astype(jnp.float32).reshape(tok_count, 2, width)
    )
    token_grad = jnp.sum(picked_grad, axis=1).astype(jnp.bfloat16)
    part_gate = contract_rows(rows_in, pre_grad)[None]
    part_up = contract_rows(rows_in, up_grad)[None]
    return (
        mixed,
        token_grad,
        gate_grad,
        lax.psum_scatter(
            part_gate.astype(jnp.bfloat16), "dp", scatter_dimension=1, tiled=True
        ).astype(jnp.float32),
        lax.psum_scatter(
            part_up.astype(jnp.bfloat16), "dp", scatter_dimension=1, tiled=True
        ).astype(jnp.float32),
    )


def solution(mesh):
    return jax.shard_map(
        on_device,
        mesh=mesh,
        in_specs=(
            P(("dp", "expert"), None),
            P(("dp", "expert"), None),
            P(("dp", "expert"), None),
            P("expert", "dp", None),
            P("expert", "dp", None),
            P("expert", "dp", None),
            P(("dp", "expert"), None),
        ),
        out_specs=(
            P(("dp", "expert"), None),
            P(("dp", "expert"), None),
            P(("dp", "expert"), None),
            P("expert", "dp", None),
            P("expert", "dp", None),
        ),
        check_vma=False,
    )
```

profile of v0, /device:TPU:6, one launch (start us, length us, event | category | flops | bytes accessed | tf_op | source)
XLA Modules:
  0.0 296.6 jit_solution(5085516644950090465)
XLA Ops:
  7.9 0.7 all-gather.6.cloned.1.call-update
  8.6 0.8 copy.21
  9.7 0.7 broadcast_multiply_fusion
  11.6 1.1 concatenate.11
  12.7 1.4 scatter_custom_fusion
  14.1 2.5 gather_fusion.3
  16.6 2.1 reshape.121
  19.0 2.8 gather_fusion.2
  21.9 3.8 %multiply_convert_fusion = bf16[32,12,2048]{2,1,0:T(8,128)(2,1)} fusion(f32[32,12,2048]{2,1,0:T(8,128)} %reshape.121, f32[32,12]{1,0:T(8,128)S(1)} %mul.82), kind=kLoop, calls=%fused_computation.6 | loop fusion | flops 1572864 | bytes 4720128 | tf_op jit(solution)/shard_map/convert_element_type | solution.py:77
  25.7 10.2 %all-to-all-start.2 = ((bf16[32,12,2048]{2,1,0:T(8,128)(2,1)}), bf16[32,12,2048]{2,1,0:T(8,128)(2,1)S(1)}, u32[]{:S(2)}, u32[]{:S(2)}) async-start(bf16[32,12,2048]{2,1,0:T(8,128)(2,1)} %multiply_convert_fusion), calls=%async_computation.2 | async-start | bytes 4194304 | tf_op jit(solution)/shard_map/all_to_all | solution.py:81
  36.7 1.1 concatenate.9
  37.8 3.1 %gather_fusion = bf16[384,2048]{1,0:T(8,128)(2,1)} fusion(bf16[129,2048]{1,0:T(8,128)(2,1)S(1)} %concatenate.9, s32[1024]{0:T(1024)S(1)} %get-tuple-element.17), kind=kCustom, calls=%fused_computation | custom fusion | bytes 3147264 | tf_op jit(solution)/shard_map/gather | solution.py:42
  40.9 3.6 %reshape.112 = bf16[32,12,2048]{2,1,0:T(8,128)(2,1)} reshape(bf16[384,2048]{1,0:T(8,128)(2,1)} %gather_fusion) | data formatting | bytes 3145728 | tf_op jit(solution)/shard_map/reshape | solution.py:42
  44.5 41.2 %all-to-all-done.2 = bf16[32,12,2048]{2,1,0:T(8,128)(2,1)S(1)} async-done(((bf16[32,12,2048]{2,1,0:T(8,128)(2,1)}), bf16[32,12,2048]{2,1,0:T(8,128)(2,1)S(1)}, u32[]{:S(2)}, u32[]{:S(2)}) %all-to-all-start.2) | async-done | bytes 1572896 | tf_op jit(solution)/shard_map/all_to_all | solution.py:81
  85.7 6.3 %all-to-all-start = ((bf16[32,12,2048]{2,1,0:T(8,128)(2,1)}), bf16[32,12,2048]{2,1,0:T(8,128)(2,1)}, u32[]{:S(2)}, u32[]{:S(2)}) async-start(bf16[32,12,2048]{2,1,0:T(8,128)(2,1)} %reshape.112), calls=%async_computation | async-start | bytes 4194304 | tf_op jit(solution)/shard_map/all_to_all | solution.py:52
  92.1 1.4 reshape.117
  93.5 48.2 %all-to-all-done = bf16[32,12,2048]{2,1,0:T(8,128)(2,1)} async-done(((bf16[32,12,2048]{2,1,0:T(8,128)(2,1)}), bf16[32,12,2048]{2,1,0:T(8,128)(2,1)}, u32[]{:S(2)}, u32[]{:S(2)}) %all-to-all-start) | async-done | bytes 1572896 | tf_op jit(solution)/shard_map/all_to_all | solution.py:52
  141.7 2.5 reshape.113
  144.2 4.0 %fusion.10 = f32[384,512]{1,0:T(8,128)} fusion(bf16[384,2048]{1,0:T(8,128)(2,1)S(1)} %reshape.113, bf16[1,2048,512]{2,1,0:T(8,128)(2,1)} %all-gather.4.cloned.1.call-done), kind=kOutput, calls=%fused_computation.21 | convolution fusion | flops 805306368 | bytes 4456448 | tf_op jit(solution)/shard_map/dot_general | solution.py:56
  148.3 3.6 %fusion.6 = f32[384,512]{1,0:T(8,128)} fusion(bf16[384,2048]{1,0:T(8,128)(2,1)S(1)} %reshape.113, bf16[1,2048,512]{2,1,0:T(8,128)(2,1)} %all-gather.6.cloned.1.call-done), kind=kOutput, calls=%fused_computation.17 | convolution fusion | flops 805306368 | bytes 4456448 | tf_op jit(solution)/shard_map/dot_general | solution.py:57
  151.9 3.9 %multiply_convert_fusion.1 = (bf16[384,512]{1,0:T(8,128)(2,1)}, bf16[384,512]{1,0:T(8,128)(2,1)S(1)}) fusion(f32[384,512]{1,0:T(8,128)} %fusion.10, f32[384,512]{1,0:T(8,128)} %fusion.6, bf16[384,2048]{1,0:T(8,128)(2,1)S(1)} %copy-done.5, bf16[1,2048,512]{2,1,0:T(8,128)(2,1)} %all-gather.8.cloned.1.call-done), kind=kOutput, calls=%fused_computation.25 | convolution fusion | flops 807862272 | bytes 6029312 | tf_op jit(solution)/shard_map/dot_general | solution.py:84
  155.8 0.7 copy-done.7
  156.5 2.6 fusion
  159.2 1.6 copy-done.3
  160.7 2.1 fusion.8
  162.9 1.1 add_convert_fusion
  164.0 1.5 reshape.118
  165.5 5.6 %all-to-all-start.3 = ((bf16[32,12,2048]{2,1,0:T(8,128)(2,1)}), bf16[32,12,2048]{2,1,0:T(8,128)(2,1)S(1)}, u32[]{:S(2)}, u32[]{:S(2)}) async-start(bf16[32,12,2048]{2,1,0:T(8,128)(2,1)} %reshape.118), calls=%async_computation.3 | async-start | bytes 4194304 | tf_op jit(solution)/shard_map/all_to_all | solution.py:91
  171.3 4.0 %fusion.1 = bf16[1,2048,512]{2,1,0:T(8,128)(2,1)} fusion(bf16[384,2048]{1,0:T(8,128)(2,1)} %copy-done.4, bf16[384,512]{1,0:T(8,128)(2,1)S(1)} %copy-done.6), kind=kOutput, calls=%fused_computation.12 | convolution fusion | flops 806354944 | bytes 4063232 | tf_op jit(solution)/shard_map/dot_general | solution.py:22
  175.4 1.1 copy-done.9
  176.5 4.1 %convolution_convert_fusion.2 = bf16[384,2048]{1,0:T(8,128)(2,1)} fusion(bf16[1,2048,512]{2,1,0:T(8,128)(2,1)} %all-gather.8.cloned.1.call-done, f32[384,512]{1,0:T(8,128)} %fusion.6, f32[384,512]{1,0:T(8,128)S(1)} %copy-done.9), kind=kOutput, calls=%fused_computation.10 | convolution fusion | flops 807272448 | bytes 5242880 | tf_op jit(solution)/shard_map/dot_general | solution.py:28
  180.6 3.6 %reshape.114 = bf16[32,12,2048]{2,1,0:T(8,128)(2,1)} reshape(bf16[384,2048]{1,0:T(8,128)(2,1)} %convolution_convert_fusion.2) | data formatting | bytes 3145728 | tf_op jit(solution)/shard_map/reshape | solution.py:61
  184.2 35.1 %all-to-all-done.3 = bf16[32,12,2048]{2,1,0:T(8,128)(2,1)S(1)} async-done(((bf16[32,12,2048]{2,1,0:T(8,128)(2,1)}), bf16[32,12,2048]{2,1,0:T(8,128)(2,1)S(1)}, u32[]{:S(2)}, u32[]{:S(2)}) %all-to-all-start.3) | async-done | bytes 1572896 | tf_op jit(solution)/shard_map/all_to_all | solution.py:91
  219.3 1.4 copy-done
  220.7 6.3 %all-to-all-start.1 = ((bf16[32,12,2048]{2,1,0:T(8,128)(2,1)}), bf16[32,12,2048]{2,1,0:T(8,128)(2,1)}, u32[]{:S(2)}, u32[]{:S(2)}) async-start(bf16[32,12,2048]{2,1,0:T(8,128)(2,1)} %reshape.114), calls=%async_computation.1 | async-start | bytes 4194304 | tf_op jit(solution)/shard_map/all_to_all | solution.py:66
  227.0 1.1 convert_element_type.84
  228.1 2.5 reshape.119
  230.6 1.4 gather_fusion.4
  232.0 0.7 gather.22
  232.7 3.6 %reduce_sum.44 = bf16[128,2048]{1,0:T(8,128)(2,1)} reduce(bf16[128,2,2048]{2,1,0:T(2,128)(2,1)S(1)} %gather.22, bf16[]{:T(256)} %constant.13.clone.1), dimensions={1}, to_apply=%region_5.6 | reduce | flops 262144 | bytes 1572866 | tf_op jit(solution)/shard_map/reduce_sum | solution.py:101
  236.3 37.9 %all-to-all-done.1 = bf16[32,12,2048]{2,1,0:T(8,128)(2,1)} async-done(((bf16[32,12,2048]{2,1,0:T(8,128)(2,1)}), bf16[32,12,2048]{2,1,0:T(8,128)(2,1)}, u32[]{:S(2)}, u32[]{:S(2)}) %all-to-all-start.1) | async-done | bytes 1572896 | tf_op jit(solution)/shard_map/all_to_all | solution.py:66
  274.3 2.5 reshape.115
  276.8 1.4 gather_fusion.1
  278.2 1.3 reshape.120
  279.5 6.0 %multiply_reduce_fusion = (f32[128,2]{1,0:T(8,128)S(1)}, bf16[128,2048]{1,0:T(8,128)(2,1)}) fusion(f32[128,2,2048]{2,1,0:T(2,128)S(1)} %reshape.120, f32[128,2048]{1,0:T(8,128)} %convert_element_type.84, f32[128,2]{1,0:T(8,128)S(1)} %copy.19), kind=kLoop, calls=%fused_computation.23 | loop fusion | flops 1834752 | bytes 3672064 | tf_op jit(solution)/shard_map/reduce_sum | solution.py:74
  286.1 1.6 convert_element_type.87
  287.8 0.7 reduce-scatter.5.cloned.1.call-done
  288.4 1.6 convert_element_type.90
  (49 shorter events, 4.3 us)
Async XLA Ops:
  7.2 137.0 %all-gather.4.cloned.1.call-start = ((), (), s32[]{:S(2)}) async-start(), calls=%async_computation.6 | async-start | bytes 2228224 | tf_op jit(solution)/shard_map/all_gather | solution.py:44
  7.9 140.4 %all-gather.6.cloned.1.call-start = ((), (), s32[]{:S(2)}) async-start(), calls=%async_computation.7 | async-start | bytes 2228224 | tf_op jit(solution)/shard_map/all_gather | solution.py:45
  16.6 2.1 copy-start.8
  25.7 60.0 %all-to-all-start.2 = ((bf16[32,12,2048]{2,1,0:T(8,128)(2,1)}), bf16[32,12,2048]{2,1,0:T(8,128)(2,1)S(1)}, u32[]{:S(2)}, u32[]{:S(2)}) async-start(bf16[32,12,2048]{2,1,0:T(8,128)(2,1)} %multiply_convert_fusion), calls=%async_computation.2 | async-start | bytes 4194304 | tf_op jit(solution)/shard_map/all_to_all | solution.py:81
  35.9 115.9 %all-gather.8.cloned.1.call-start = ((), (), s32[]{:S(2)}) async-start(), calls=%async_computation.8 | async-start | bytes 2228224 | tf_op jit(solution)/shard_map/all_gather | solution.py:46
  85.7 55.9 %all-to-all-start = ((bf16[32,12,2048]{2,1,0:T(8,128)(2,1)}), bf16[32,12,2048]{2,1,0:T(8,128)(2,1)}, u32[]{:S(2)}, u32[]{:S(2)}) async-start(bf16[32,12,2048]{2,1,0:T(8,128)(2,1)} %reshape.112), calls=%async_computation | async-start | bytes 4194304 | tf_op jit(solution)/shard_map/all_to_all | solution.py:52
  92.1 194.0 %reduce-scatter.3.cloned.1.call-start = ((), (), s32[]{:S(2)}) async-start(), calls=%async_computation.9 | async-start | bytes 2228224 | tf_op jit(solution)/shard_map/reduce_scatter | solution.py:108
  144.2 11.6 %copy-start.4 = (bf16[384,2048]{1,0:T(8,128)(2,1)}, bf16[384,2048]{1,0:T(8,128)(2,1)S(1)}, u32[]{:S(2)}) copy-start(bf16[384,2048]{1,0:T(8,128)(2,1)S(1)} %reshape.113) | copy-start | bytes 4718596
  148.3 3.6 %copy-start.5 = (bf16[384,2048]{1,0:T(8,128)(2,1)S(1)}, bf16[384,2048]{1,0:T(8,128)(2,1)}, u32[]{:S(2)}) copy-start(bf16[384,2048]{1,0:T(8,128)(2,1)} %reshape.117) | copy-start | bytes 4718596
  155.8 0.7 copy-start.7
  159.1 1.6 copy-start.3
  160.7 2.2 copy-start.1
  160.7 2.2 copy-start.6
  165.5 53.8 %all-to-all-start.3 = ((bf16[32,12,2048]{2,1,0:T(8,128)(2,1)}), bf16[32,12,2048]{2,1,0:T(8,128)(2,1)S(1)}, u32[]{:S(2)}, u32[]{:S(2)}) async-start(bf16[32,12,2048]{2,1,0:T(8,128)(2,1)} %reshape.118), calls=%async_computation.3 | async-start | bytes 4194304 | tf_op jit(solution)/shard_map/all_to_all | solution.py:91
  171.1 117.3 %reduce-scatter.5.cloned.1.call-start = ((), (), s32[]{:S(2)}) async-start(), calls=%async_computation.10 | async-start | bytes 2228224 | tf_op jit(solution)/shard_map/reduce_scatter | solution.py:111
  175.4 1.1 copy-start.9
  184.2 42.8 %copy-start.2 = (bf16[128,2048]{1,0:T(8,128)(2,1)S(1)}, bf16[128,2048]{1,0:T(8,128)(2,1)}, u32[]{:S(2)}) copy-start(bf16[128,2048]{1,0:T(8,128)(2,1)} %param.13) | copy-start | bytes 1572868
  219.3 1.4 copy-start
  220.7 53.6 %all-to-all-start.1 = ((bf16[32,12,2048]{2,1,0:T(8,128)(2,1)}), bf16[32,12,2048]{2,1,0:T(8,128)(2,1)}, u32[]{:S(2)}, u32[]{:S(2)}) async-start(bf16[32,12,2048]{2,1,0:T(8,128)(2,1)} %reshape.114), calls=%async_computation.1 | async-start | bytes 4194304 | tf_op jit(solution)/shard_map/all_to_all | solution.py:66
Sparse Core Ops, SparseCore 0:
  10.1 47.9 all-gather.3
  60.2 41.0 all-gather.5
  103.5 40.7 all-gather.7
  159.3 64.1 reduce-scatter.2
  226.1 62.2 reduce-scatter.4
where the time goes:
time: 298 us; the launch traced here: 297 us
  waiting for transfers between devices  165 us (55%)
  local copies, waits for them, and re-layouts  43.7 us (15%)
  starting transfers between devices  28.8 us (10%)
  matrix products  25.5 us (9%)
  other arithmetic  19.2 us (6%)
  between operations  14 us (5%)
    all_to_all x1, waiting for transfers between devices, on_device(): lax.all_to_all(send_rows, 'expert', split_axis=0, concat_axis=0, tiled=True)  48.2 us
    all_to_all x1, waiting for transfers between devices, on_device(): lax.all_to_all(send_grad, 'expert', split_axis=0, concat_axis=0, tiled=True)  41.2 us
    all_to_all x1, waiting for transfers between devices, on_device(): lax.all_to_all(expert_out, 'expert', split_axis=0, concat_axis=0, tiled=T...  37.9 us
    all_to_all x1, waiting for transfers between devices, on_device(): lax.all_to_all(row_grad.reshape(experts_all, capacity, width), 'expert',...  35.1 us
    all_to_all x1, starting transfers between devices, on_device(): lax.all_to_all(send_grad, 'expert', split_axis=0, concat_axis=0, tiled=True)  10.2 us
    dot_general x3, matrix products, contract_cols(): lax.dot_general(left, right, (((1,), (1,)), ((), ())), preferred_element_...  7.29 us
    dot_general x2, matrix products, contract_rows(): lax.dot_general(left, right, (((0,), (0,)), ((), ())), preferred_element_...  6.64 us
    all_to_all x1, starting transfers between devices, on_device(): lax.all_to_all(send_rows, 'expert', split_axis=0, concat_axis=0, tiled=True)  6.35 us
  transfers between devices with their start and end apart: 9, of which 5 were waited for; matrix products, arithmetic and copies ran while one was open for 25% of the time, Pallas kernels for 0%

commit v1 on v0

v1 whole, which is shorter than its diff:
```python
import jax
import jax.numpy as jnp
from jax import lax
from jax.experimental import pallas as pl
from jax.experimental.pallas import tpu as pltpu
from jax.sharding import PartitionSpec as P

BF = jnp.bfloat16
F32 = jnp.float32
TILE = 512


def iota(shape, axis):
    return lax.broadcasted_iota(jnp.int32, shape, axis)


def dot(left, right):
    return jnp.dot(left, right, preferred_element_type=F32)


def dot_cols(left, right):
    return lax.dot_general(left, right, (((1,), (1,)), ((), ())), preferred_element_type=F32)


def pick_ranks(experts_ref, count):
    first, second = experts_ref[0:1, :], experts_ref[1:2, :]
    toks = experts_ref.shape[1]
    names = iota((count, toks), 0)
    is_first, is_second = names == first, names == second
    either = jnp.where(is_first | is_second, 1.0, 0.0).astype(BF)
    earlier = jnp.where(iota((toks, toks), 0) < iota((toks, toks), 1), 1.0, 0.0).astype(BF)
    before = dot(either, earlier)
    ranks = [
        jnp.sum(jnp.where(mask, before, 0.0), axis=0, keepdims=True).astype(jnp.int32)
        for mask in (is_first, is_second)
    ]
    return ((first, ranks[0]), (second, ranks[1]))


def wide_row(expert, rank):
    return jnp.where(rank < 8, expert * 8 + rank, -1)


def half_row(expert, rank, half):
    return jnp.where(rank >= 8, expert * 8 + half * 4 + rank - 8, -1)


def as_column(row):
    toks = row.shape[1]
    eye = iota((toks, toks), 0) == iota((toks, toks), 1)
    return jnp.sum(jnp.where(eye, row, jnp.zeros_like(row)), axis=1, keepdims=True)


def send_masks(experts_ref, count):
    rows = count * 8
    toks = experts_ref.shape[1]
    row = iota((rows, toks), 0)
    out = []
    for expert, rank in pick_ranks(experts_ref, count):
        out.append(
            (
                row == wide_row(expert, rank),
                row == half_row(expert, rank, 0),
                row == half_row(expert, rank, 1),
            )
        )
    return out


def one_hot(*masks):
    both = masks[0]
    for mask in masks[1:]:
        both = both | mask
    return jnp.where(both, 1.0, 0.0).astype(BF)


def pack_tokens(experts_ref, rows_ref, out_ref):
    count = out_ref.shape[0] // 8
    width = rows_ref.shape[1]
    half = width // 2
    first, second = send_masks(experts_ref, count)
    wide = one_hot(first[0], second[0])
    halves = [one_hot(first[1 + h], second[1 + h]) for h in range(2)]
    for c in range(0, width, TILE):
        out_ref[:, c : c + TILE] = dot(wide, rows_ref[:, c : c + TILE]).astype(BF)
    for c in range(0, half, TILE):
        out_ref[:, width + c : width + c + TILE] = (
            dot(halves[0], rows_ref[:, c : c + TILE])
            + dot(halves[1], rows_ref[:, half + c : half + c + TILE])
        ).astype(BF)


def pack_grads(experts_ref, gates_ref, rows_ref, out_ref):
    count = out_ref.shape[0] // 8
    width = rows_ref.shape[1]
    half = width // 2
    first, second = send_masks(experts_ref, count)
    gate0, gate1 = gates_ref[0:1, :], gates_ref[1:2, :]

    def gate_of(mask0, mask1):
        return jnp.sum(
            jnp.where(mask0, gate0, 0.0) + jnp.where(mask1, gate1, 0.0), axis=1, keepdims=True
        )

    wide = one_hot(first[0], second[0])
    wide_gate = gate_of(first[0], second[0])
    halves = [one_hot(first[1 + h], second[1 + h]) for h in range(2)]
    half_gate = gate_of(first[1] | first[2], second[1] | second[2])
    for c in range(0, width, TILE):
        out_ref[:, c : c + TILE] = (wide_gate * dot(wide, rows_ref[:, c : c + TILE])).astype(BF)
    for c in range(0, half, TILE):
        out_ref[:, width + c : width + c + TILE] = (
            half_gate
            * (
                dot(halves[0], rows_ref[:, c : c + TILE])
                + dot(halves[1], rows_ref[:, half + c : half + c + TILE])
            )
        ).astype(BF)


def fetch_masks(experts_ref, count):
    rows = count * 8
    toks = experts_ref.shape[1]
    col = iota((toks, rows), 1)
    out = []
    for expert, rank in pick_ranks(experts_ref, count):
        targets = (wide_row(expert, rank), half_row(expert, rank, 0), half_row(expert, rank, 1))
        out.append(tuple(col == as_column(t) for t in targets))
    return out


def combine_out(experts_ref, gates_ref, got_ref, grad_ref, mixed_ref, gate_grad_ref):
    count = got_ref.shape[0] // 8
    toks, width = mixed_ref.shape
    half = width // 2
    masks = fetch_masks(experts_ref, count)
    wide = [one_hot(m[0]) for m in masks]
    halves = [[one_hot(m[1 + h]) for m in masks] for h in range(2)]
    gates = [as_column(gates_ref[k : k + 1, :]) for k in range(2)]
    sums = [jnp.zeros((toks, 1), F32) for _ in range(2)]
    for c in range(0, width, TILE):
        h, low = c // half, width + c % half
        grad = grad_ref[:, c : c + TILE].astype(F32)
        total = jnp.zeros((toks, TILE), F32)
        for k in range(2):
            picked = dot(wide[k], got_ref[:, c : c + TILE]) + dot(
                halves[h][k], got_ref[:, low : low + TILE]
            )
            total = total + gates[k] * picked
            sums[k] = sums[k] + jnp.sum(grad * picked, axis=1, keepdims=True)
        mixed_ref[:, c : c + TILE] = total.astype(BF)
    lane = iota((toks, 2), 1)
    gate_grad_ref[...] = jnp.where(lane == 0, sums[0], sums[1])


def combine_grads(experts_ref, got_ref, out_ref):
    count = got_ref.shape[0] // 8
    width = out_ref.shape[1]
    half = width // 2
    first, second = fetch_masks(experts_ref, count)
    wide = one_hot(first[0], second[0])
    halves = [one_hot(first[1 + h], second[1 + h]) for h in range(2)]
    for c in range(0, width, TILE):
        low = width + c % half
        out_ref[:, c : c + TILE] = (
            dot(wide, got_ref[:, c : c + TILE]) + dot(halves[c // half], got_ref[:, low : low + TILE])
        ).astype(BF)


def split_rows(got_ref, rows_ref):
    count = got_ref.shape[0]
    width = rows_ref.shape[1]
    half = width // 2
    tail = count // 2
    rows_ref[0:count, :] = got_ref[:, 0:width]
    row, col = iota((tail, count), 0), iota((tail, count), 1)
    for h in range(2):
        pick = one_hot(col == (row >> 2) * 8 + h * 4 + (row & 3))
        for c in range(0, half, TILE):
            rows_ref[count : count + tail, h * half + c : h * half + c + TILE] = dot(
                pick, got_ref[:, width + c : width + c + TILE]
            ).astype(BF)


def tail_spread(count):
    tail = count // 2
    row, col = iota((count, tail), 0), iota((count, tail), 1)
    return [one_hot(row == (col >> 2) * 8 + h * 4 + (col & 3)) for h in range(2)]


def store_rows(product, send_ref, tail_ref, width, at, size):
    count = send_ref.shape[0]
    send_ref[:, at : at + size] = product[0:count]
    tail_ref[:, at : at + size] = product[count:]


def flush_tail(send_ref, tail_ref, width):
    count = send_ref.shape[0]
    half = width // 2
    spread = tail_spread(count)
    for c in range(0, half, TILE):
        send_ref[:, width + c : width + c + TILE] = (
            dot(spread[0], tail_ref[:, c : c + TILE])
            + dot(spread[1], tail_ref[:, half + c : half + c + TILE])
        ).astype(BF)


def forward_rows(got_ref, weights_ref, send_ref, rows_ref, gate_ref, up_ref, hidden_ref, tail_ref):
    width = rows_ref.shape[1]
    hid = gate_ref.shape[1]
    split_rows(got_ref, rows_ref)
    for c in range(0, hid, 256):
        gate = dot(rows_ref[...], weights_ref[:, c : c + 256])
        up = dot(rows_ref[...], weights_ref[:, hid + c : hid + c + 256])
        gate_ref[:, c : c + 256] = gate
        up_ref[:, c : c + 256] = up
        hidden_ref[:, c : c + 256] = (gate * jax.nn.sigmoid(gate) * up).astype(BF)
    for c in range(0, width, 256):
        product = dot_cols(hidden_ref[...], weights_ref[c : c + 256, 2 * hid : 3 * hid]).astype(BF)
        store_rows(product, send_ref, tail_ref, width, c, 256)
    flush_tail(send_ref, tail_ref, width)


def backward_rows(got_ref, weights_ref, gate_ref, up_ref, send_ref, pre_ref, rows_ref, tail_ref):
    width = rows_ref.shape[1]
    hid = gate_ref.shape[1]
    split_rows(got_ref, rows_ref)
    for c in range(0, hid, 256):
        grad = dot(rows_ref[...], weights_ref[:, 2 * hid + c : 2 * hid + c + 256])
        gate, up = gate_ref[:, c : c + 256], up_ref[:, c : c + 256]
        sigma = jax.nn.sigmoid(gate)
        pre_ref[:, hid + c : hid + c + 256] = (grad * gate * sigma).astype(BF)
        pre_ref[:, c : c + 256] = (grad * up * sigma * (1.0 + gate * (1.0 - sigma))).astype(BF)
    for c in range(0, width, 256):
        product = dot_cols(pre_ref[...], weights_ref[c : c + 256, 0 : 2 * hid]).astype(BF)
        store_rows(product, send_ref, tail_ref, width, c, 256)
    flush_tail(send_ref, tail_ref, width)


def call(body, outs, scratch, flops, *args):
    size = sum(a.size * a.dtype.itemsize for a in args)
    size += sum(o[0][0] * o[0][1] * jnp.dtype(o[1]).itemsize for o in outs)
    return pl.pallas_call(
        body,
        out_shape=[jax.ShapeDtypeStruct(s, d) for s, d in outs],
        in_specs=[pl.BlockSpec(memory_space=pltpu.VMEM) for _ in args],
        out_specs=[pl.BlockSpec(memory_space=pltpu.VMEM) for _ in outs],
        scratch_shapes=[pltpu.VMEM(s, d) for s, d in scratch],
        cost_estimate=pl.CostEstimate(flops=flops, bytes_accessed=size, transcendentals=0),
        compiler_params=pltpu.CompilerParams(vmem_limit_bytes=12 << 20),
    )(*args)


def on_device(tokens, gates, experts, gate_weight, up_weight, down_weight, out_grad):
    toks, width = tokens.shape
    hid = gate_weight.shape[2]
    count = lax.axis_size("expert") * gate_weight.shape[0]
    send = (count * 8, 3 * width // 2)
    slots = count * 12
    experts_t, gates_t = experts.T, gates.T

    def exchange(rows):
        moved = lax.all_to_all(
            rows.reshape(count, 8, send[1]), "expert", split_axis=0, concat_axis=0, tiled=True
        )
        return moved.reshape(send)

    weights = lax.all_gather(
        jnp.concatenate([gate_weight, up_weight, down_weight], axis=2), "dp", axis=1, tiled=True
    )[0]
    pack_flops = 2 * send[0] * toks * send[1]
    (send_tok,) = call(pack_tokens, [(send, BF)], [], pack_flops, experts_t, tokens)
    (send_grad,) = call(pack_grads, [(send, BF)], [], pack_flops, experts_t, gates_t, out_grad)
    got_tok = exchange(send_tok)
    got_tok, send_grad = lax.optimization_barrier((got_tok, send_grad))
    got_grad = exchange(send_grad)
    send_out, rows_in, gate_pre, up_pre = call(
        forward_rows,
        [(send, BF), ((slots, width), BF), ((slots, hid), F32), ((slots, hid), F32)],
        [((slots, hid), BF), ((slots - send[0], width), BF)],
        6 * slots * width * hid,
        got_tok,
        weights,
    )
    got_grad, send_out = lax.optimization_barrier((got_grad, send_out))
    got_out = exchange(send_out)
    send_back, pre_grads = call(
        backward_rows,
        [(send, BF), ((slots, 2 * hid), BF)],
        [((slots, width), BF), ((slots - send[0], width), BF)],
        6 * slots * width * hid,
        got_grad,
        weights,
        gate_pre,
        up_pre,
    )
    partial = lax.dot_general(
        rows_in, pre_grads, (((0,), (0,)), ((), ())), preferred_element_type=F32
    )[None]
    summed = lax.psum_scatter(
        partial.astype(BF), "dp", scatter_dimension=1, tiled=True
    ).astype(F32)
    got_out, send_back = lax.optimization_barrier((got_out, send_back))
    got_back = exchange(send_back)
    mixed, gate_grad = call(
        combine_out,
        [((toks, width), BF), ((toks, 2), F32)],
        [],
        400 * toks * send[0] * width * 2,
        experts_t,
        gates_t,
        got_out,
        out_grad,
    )
    (token_grad,) = call(
        combine_grads, [((toks, width), BF)], [], 4 * toks * send[0] * width, experts_t, got_back
    )
    return (mixed, token_grad, gate_grad, summed[:, :, :hid], summed[:, :, hid:])


def solution(mesh):
    return jax.shard_map(
        on_device,
        mesh=mesh,
        in_specs=(
            P(("dp", "expert"), None),
            P(("dp", "expert"), None),
            P(("dp", "expert"), None),
            P("expert", "dp", None),
            P("expert", "dp", None),
            P("expert", "dp", None),
            P(("dp", "expert"), None),
        ),
        out_specs=(
            P(("dp", "expert"), None),
            P(("dp", "expert"), None),
            P(("dp", "expert"), None),
            P("expert", "dp", None),
            P("expert", "dp", None),
        ),
        check_vma=False,
    )
```

time: 298 us -> 218 us (0.73)
  waiting for transfers between devices: 165 us -> 98.8 us
  blocking collectives: 0 us -> 42.8 us
  local copies, waits for them, and re-layouts: 43.7 us -> 18.5 us
  matrix products: 25.5 us -> 4.37 us
  other arithmetic: 19.2 us -> 1.8 us
  Pallas kernels: 0 us -> 15.1 us
  starting transfers between devices: 28.8 us -> 21.5 us
    all_to_all x4 -> x3, waiting for transfers between devices: 162 us -> 98.8 us  [exchange(): lax.all_to_all(rows.reshape(count, 8, send[1]), 'expert', split_axis=0, c...]
    all_to_all x0 -> x1, blocking collectives: none -> 42.8 us  [exchange(): lax.all_to_all(rows.reshape(count, 8, send[1]), 'expert', split_axis=0, c...]
    dot_general x8 -> x1, matrix products: 25.5 us -> 4.37 us  [on_device(): lax.dot_general(rows_in, pre_grads, (((0,), (0,)), ((), ())), preferred_e...]
    reshape x8 -> x0, local copies, waits for them, and re-layouts: 17.8 us -> none  [the longest x1 3.62 us: on_device(): send_rows = tok_pad[owner_tok].reshape(experts_all, capacity, width)]
    pallas_call x0 -> x6, Pallas kernels: none -> 15.1 us  [call(): pl.pallas_call(body, out_shape=[jax.ShapeDtypeStruct(s, d) for s, d in ou...]
    gather x6 -> x0, local copies, waits for them, and re-layouts: 11.8 us -> none  [the longest x1 3.12 us: on_device(): send_rows = tok_pad[owner_tok].reshape(experts_all, capacity, width)]
    unnamed x23 -> x33, local copies, waits for them, and re-layouts: 6.34 us -> 16.7 us
    reduce_sum x3 -> x0, other arithmetic: 9.69 us -> none  [the longest x1 5.96 us: on_device(): jnp.sum(out_grad.astype(jnp.float32)[:, None, :] * picked_out, axis=2)]
  transfers between devices with their start and end apart: 9 -> 5, of which waited for: 5 -> 3; matrix products, arithmetic and copies ran while one was open for 25% -> 0% of each run, Pallas kernels for 0% -> 5%
where the time goes in v1:
time: 218 us; the launch traced here: 217 us
  waiting for transfers between devices  98.8 us (45%)
  blocking collectives  42.8 us (20%)
  starting transfers between devices  21.5 us (10%)
  local copies, waits for them, and re-layouts  18.5 us (8%)
  Pallas kernels  15.1 us (7%)
  between operations  14.2 us (7%)
  matrix products  4.37 us (2%)
    all_to_all x3, waiting for transfers between devices, exchange(): lax.all_to_all(rows.reshape(count, 8, send[1]), 'expert', split_axis=0, c...  98.8 us
    all_to_all x1, blocking collectives, exchange(): lax.all_to_all(rows.reshape(count, 8, send[1]), 'expert', split_axis=0, c...  42.8 us
    all_to_all x3, starting transfers between devices, exchange(): lax.all_to_all(rows.reshape(count, 8, send[1]), 'expert', split_axis=0, c...  21.5 us
    unnamed x33, local copies, waits for them, and re-layouts  16.7 us
    pallas_call x6, Pallas kernels, call(): pl.pallas_call(body, out_shape=[jax.ShapeDtypeStruct(s, d) for s, d in ou...  15.1 us
    dot_general x1, matrix products, on_device(): lax.dot_general(rows_in, pre_grads, (((0,), (0,)), ((), ())), preferred_e...  4.37 us
  transfers between devices with their start and end apart: 5, of which 3 were waited for; matrix products, arithmetic and copies ran while one was open for 0% of the time, Pallas kernels for 5%

profile of v1, /device:TPU:6, one launch (start us, length us, event | category | flops | bytes accessed | tf_op | source)
XLA Modules:
  0.0 217.1 jit_solution(14725387346319016127)
XLA Ops:
  7.2 0.0 all-gather.2.cloned.1.call-start
  7.2 1.8 pad_maximum_fusion
  9.0 0.0 all-gather.2.cloned.1.call-update
  9.0 0.0 copy-start.10
  9.1 1.0 copy-done.10
  10.1 0.0 copy-start.11
  10.1 0.7 copy-done.11
  10.8 2.0 shard_map.110
  12.8 0.0 copy-start.8
  12.8 0.0 copy-start.12
  12.8 0.0 copy-start.13
  12.8 10.3 %all-to-all-start = ((bf16[32,8,3072]{2,1,0:T(8,128)(2,1)}), bf16[32,8,3072]{2,1,0:T(8,128)(2,1)S(1)}, u32[]{:S(2)}, u32[]{:S(2)}) async-start(bf16[32,8,3072]{2,1,0:T(8,128)(2,1)} %bitcast.2), calls=%async_computation | async-start | bytes 3145728 | tf_op jit(solution)/shard_map/all_to_all | solution.py:263
  23.1 0.0 copy-done.8
  23.2 0.0 copy-done.12
  23.2 0.0 copy-done.13
  23.2 2.1 shard_map.111
  25.3 37.1 %all-to-all-done = bf16[32,8,3072]{2,1,0:T(8,128)(2,1)S(1)} async-done(((bf16[32,8,3072]{2,1,0:T(8,128)(2,1)}), bf16[32,8,3072]{2,1,0:T(8,128)(2,1)S(1)}, u32[]{:S(2)}, u32[]{:S(2)}) %all-to-all-start) | async-done | bytes 1572896 | tf_op jit(solution)/shard_map/all_to_all | solution.py:263
  62.4 5.6 %all-to-all-start.1 = ((bf16[32,8,3072]{2,1,0:T(8,128)(2,1)}), bf16[32,8,3072]{2,1,0:T(8,128)(2,1)S(1)}, u32[]{:S(2)}, u32[]{:S(2)}) async-start(bf16[32,8,3072]{2,1,0:T(8,128)(2,1)} %bitcast.4), calls=%async_computation.1 | async-start | bytes 3145728 | tf_op jit(solution)/shard_map/all_to_all | solution.py:263
  68.0 0.0 reduce-scatter.2.cloned.1.call-start
  68.1 0.0 all-gather.2.cloned.1.call-done
  68.1 0.0 copy-start
  68.1 2.8 %copy-done = bf16[1,2048,1536]{2,1,0:T(8,128)(2,1)S(1)} copy-done((bf16[1,2048,1536]{2,1,0:T(8,128)(2,1)S(1)}, bf16[1,2048,1536]{2,1,0:T(8,128)(2,1)}, u32[]{:S(2)}) %copy-start) | copy-done | bytes 6291480
  70.9 3.0 %shard_map.112 = (bf16[256,3072]{1,0:T(8,128)(2,1)S(1)}, bf16[384,2048]{1,0:T(8,128)(2,1)S(1)}, f32[384,512]{1,0:T(8,128)S(1)}, f32[384,512]{1,0:T(8,128)S(1)}) custom-call(bf16[256,3072]{1,0:T(8,128)(2,1)S(1)} %bitcast.19, bf16[2048,1536]{1,0:T(8,128)(2,1)S(1)} %bitcast.15), custom_call_target="tpu_custom_call" | custom-call | flops 2415919104 | bytes 12582912 | tf_op jit(solution)/shard_map/pallas_call | solution.py:243
  73.9 0.0 copy-start.2
  73.9 1.1 copy-done.2
  75.0 0.0 copy-start.4
  75.1 0.9 copy-done.4
  75.9 0.0 copy-start.6
  75.9 0.9 copy-done.6
  76.8 1.1 copy-done.14
  78.0 28.1 %all-to-all-done.1 = bf16[32,8,3072]{2,1,0:T(8,128)(2,1)S(1)} async-done(((bf16[32,8,3072]{2,1,0:T(8,128)(2,1)}), bf16[32,8,3072]{2,1,0:T(8,128)(2,1)S(1)}, u32[]{:S(2)}, u32[]{:S(2)}) %all-to-all-start.1) | async-done | bytes 1572896 | tf_op jit(solution)/shard_map/all_to_all | solution.py:263
  106.1 2.8 %copy-done.1 = bf16[1,2048,1536]{2,1,0:T(8,128)(2,1)S(1)} copy-done((bf16[1,2048,1536]{2,1,0:T(8,128)(2,1)S(1)}, bf16[1,2048,1536]{2,1,0:T(8,128)(2,1)}, u32[]{:S(2)}) %copy-start.1) | copy-done | bytes 6291480
  108.9 1.1 copy-done.5
  110.0 1.1 copy-done.7
  111.2 4.5 %shard_map.113 = (bf16[256,3072]{1,0:T(8,128)(2,1)}, bf16[384,1024]{1,0:T(8,128)(2,1)S(1)}) custom-call(bf16[256,3072]{1,0:T(8,128)(2,1)S(1)} %bitcast.17, bf16[2048,1536]{1,0:T(8,128)(2,1)S(1)} %bitcast.16, f32[384,512]{1,0:T(8,128)S(1)} %copy-done.5, f32[384,512]{1,0:T(8,128)S(1)} %copy-done.7), custom_call_target="tpu_custom_call" | custom-call | flops 2415919104 | bytes 11796480 | tf_op jit(solution)/shard_map/pallas_call | solution.py:243
  115.7 0.0 copy-done.15
  115.7 4.4 %convert_bitcast_fusion = bf16[1,2048,1024]{2,1,0:T(8,128)(2,1)} fusion(bf16[384,2048]{1,0:T(8,128)(2,1)S(1)} %copy-done.15, bf16[384,1024]{1,0:T(8,128)(2,1)S(1)} %get-tuple-element.32), kind=kOutput, calls=%fused_computation | convolution fusion | flops 1612709888 | bytes 6553600 | tf_op jit(solution)/shard_map/dot_general | solution.py:297
  120.1 0.0 reduce-scatter.2.cloned.1.call-update
  120.1 1.4 copy-done.3
  121.5 42.8 %all_to_all.20 = bf16[32,8,3072]{2,1,0:T(8,128)(2,1)S(1)} all-to-all(bf16[32,8,3072]{2,1,0:T(8,128)(2,1)S(1)} %bitcast.20), channel_id=1, replica_groups=mesh['dp'=16,'expert'=32] {'expert'}, dimensions={0} | all-to-all | bytes 3145728 | tf_op jit(solution)/shard_map/all_to_all | solution.py:263
  164.3 5.6 %all-to-all-start.3 = ((bf16[32,8,3072]{2,1,0:T(8,128)(2,1)}), bf16[32,8,3072]{2,1,0:T(8,128)(2,1)S(1)}, u32[]{:S(2)}, u32[]{:S(2)}) async-start(bf16[32,8,3072]{2,1,0:T(8,128)(2,1)} %bitcast.9), calls=%async_computation.3 | async-start | bytes 3145728 | tf_op jit(solution)/shard_map/all_to_all | solution.py:263
  169.9 0.0 copy-start.9
  169.9 1.0 copy-done.9
  170.9 1.9 shard_map.114
  172.8 0.6 copy.12
  173.4 33.5 %all-to-all-done.3 = bf16[32,8,3072]{2,1,0:T(8,128)(2,1)S(1)} async-done(((bf16[32,8,3072]{2,1,0:T(8,128)(2,1)}), bf16[32,8,3072]{2,1,0:T(8,128)(2,1)S(1)}, u32[]{:S(2)}, u32[]{:S(2)}) %all-to-all-start.3) | async-done | bytes 1572896 | tf_op jit(solution)/shard_map/all_to_all | solution.py:263
  206.9 1.5 shard_map.115
  208.5 1.8 fusion
  (7 shorter events, 0.0 us)
Async XLA Ops:
  7.2 60.9 %all-gather.2.cloned.1.call-start = ((), (), s32[]{:S(2)}) async-start(), calls=%async_computation.5 | async-start | bytes 6684672 | tf_op jit(solution)/shard_map/all_gather | solution.py:268
  9.0 1.0 copy-start.10
  10.1 0.7 copy-start.11
  12.8 10.3 %copy-start.8 = (bf16[128,2048]{1,0:T(8,128)(2,1)S(1)}, bf16[128,2048]{1,0:T(8,128)(2,1)}, u32[]{:S(2)}) copy-start(bf16[128,2048]{1,0:T(8,128)(2,1)} %grad_ref.1) | copy-start | bytes 1572868
  12.8 10.4 %copy-start.12 = (s32[128,2]{0,1:T(2,128)S(1)}, s32[128,2]{0,1:T(2,128)}, u32[]{:S(2)}) copy-start(s32[128,2]{0,1:T(2,128)} %param.9) | copy-start | bytes 3076
  12.8 10.4 %copy-start.13 = (f32[128,2]{0,1:T(2,128)S(1)}, f32[128,2]{0,1:T(2,128)}, u32[]{:S(2)}) copy-start(f32[128,2]{0,1:T(2,128)} %param.8) | copy-start | bytes 3076
  12.8 49.6 %all-to-all-start = ((bf16[32,8,3072]{2,1,0:T(8,128)(2,1)}), bf16[32,8,3072]{2,1,0:T(8,128)(2,1)S(1)}, u32[]{:S(2)}, u32[]{:S(2)}) async-start(bf16[32,8,3072]{2,1,0:T(8,128)(2,1)} %bitcast.2), calls=%async_computation | async-start | bytes 3145728 | tf_op jit(solution)/shard_map/all_to_all | solution.py:263
  62.4 43.7 %all-to-all-start.1 = ((bf16[32,8,3072]{2,1,0:T(8,128)(2,1)}), bf16[32,8,3072]{2,1,0:T(8,128)(2,1)S(1)}, u32[]{:S(2)}, u32[]{:S(2)}) async-start(bf16[32,8,3072]{2,1,0:T(8,128)(2,1)} %bitcast.4), calls=%async_computation.1 | async-start | bytes 3145728 | tf_op jit(solution)/shard_map/all_to_all | solution.py:263
  68.0 140.5 %reduce-scatter.2.cloned.1.call-start = ((), (), s32[]{:S(2)}) async-start(), calls=%async_computation.6 | async-start | bytes 4456448 | tf_op jit(solution)/shard_map/reduce_scatter | solution.py:300
  68.1 2.8 %copy-start = (bf16[1,2048,1536]{2,1,0:T(8,128)(2,1)S(1)}, bf16[1,2048,1536]{2,1,0:T(8,128)(2,1)}, u32[]{:S(2)}) copy-start(bf16[1,2048,1536]{2,1,0:T(8,128)(2,1)} %all-gather.2.cloned.1.call-done) | copy-start | bytes 18874372
  73.9 1.2 copy-start.2
  75.0 0.9 copy-start.4
  75.9 0.9 copy-start.6
  76.8 1.1 copy-start.14
  106.1 2.8 %copy-start.1 = (bf16[1,2048,1536]{2,1,0:T(8,128)(2,1)S(1)}, bf16[1,2048,1536]{2,1,0:T(8,128)(2,1)}, u32[]{:S(2)}) copy-start(bf16[1,2048,1536]{2,1,0:T(8,128)(2,1)} %all-gather.2.cloned.1.call-done) | copy-start | bytes 18874372
  108.9 1.1 copy-start.5
  110.0 1.1 copy-start.7
  111.2 4.5 %copy-start.15 = (bf16[384,2048]{1,0:T(8,128)(2,1)S(1)}, bf16[384,2048]{1,0:T(8,128)(2,1)}, u32[]{:S(2)}) copy-start(bf16[384,2048]{1,0:T(8,128)(2,1)} %copy-done.14) | copy-start | bytes 4718596
  120.1 1.4 copy-start.3
  164.3 42.7 %all-to-all-start.3 = ((bf16[32,8,3072]{2,1,0:T(8,128)(2,1)}), bf16[32,8,3072]{2,1,0:T(8,128)(2,1)S(1)}, u32[]{:S(2)}, u32[]{:S(2)}) async-start(bf16[32,8,3072]{2,1,0:T(8,128)(2,1)} %bitcast.9), calls=%async_computation.3 | async-start | bytes 3145728 | tf_op jit(solution)/shard_map/all_to_all | solution.py:263
  169.9 1.1 copy-start.9
Sparse Core Ops, SparseCore 0:
  10.7 54.0 all-gather.1
  120.2 67.3 reduce-scatter.1

commit v2 on v1

--- a/solution.py
+++ b/solution.py
@@ -22,8 +22,12 @@
     return lax.dot_general(left, right, (((1,), (1,)), ((), ())), preferred_element_type=F32)
 
 
+def turn(expert):
+    return (expert & 3) * 8 + (expert >> 2)
+
+
 def pick_ranks(experts_ref, count):
-    first, second = experts_ref[0:1, :], experts_ref[1:2, :]
+    first, second = turn(experts_ref[0:1, :]), turn(experts_ref[1:2, :])
     toks = experts_ref.shape[1]
     names = iota((count, toks), 0)
     is_first, is_second = names == first, names == second
@@ -261,15 +265,19 @@
 
     def exchange(rows):
         moved = lax.all_to_all(
-            rows.reshape(count, 8, send[1]), "expert", split_axis=0, concat_axis=0, tiled=True
+            rows.reshape(count, 8, send[1]),
+            "expert",
+            split_axis=0,
+            concat_axis=0,
+            tiled=True,
+            axis_index_groups=[[y * 4 + x for x in range(4) for y in range(8)]],
         )
         return moved.reshape(send)
 
-    weights = lax.all_gather(
-        jnp.concatenate([gate_weight, up_weight, down_weight], axis=2), "dp", axis=1, tiled=True
-    )[0]
     pack_flops = 2 * send[0] * toks * send[1]
     (send_tok,) = call(pack_tokens, [(send, BF)], [], pack_flops, experts_t, tokens)
+    shards, send_tok = lax.optimization_barrier(((gate_weight, up_weight, down_weight), send_tok))
+    weights = lax.all_gather(jnp.concatenate(shards, axis=2), "dp", axis=1, tiled=True)[0]
     (send_grad,) = call(pack_grads, [(send, BF)], [], pack_flops, experts_t, gates_t, out_grad)
     got_tok = exchange(send_tok)
     got_tok, send_grad = lax.optimization_barrier((got_tok, send_grad))
@@ -306,16 +314,17 @@
         combine_out,
         [((toks, width), BF), ((toks, 2), F32)],
         [],
-        400 * toks * send[0] * width * 2,
+        40000000 * toks * send[0] * width * 2,
         experts_t,
         gates_t,
         got_out,
         out_grad,
     )
+    got_back, summed = lax.optimization_barrier((got_back, (summed[:, :, :hid], summed[:, :, hid:])))
     (token_grad,) = call(
         combine_grads, [((toks, width), BF)], [], 4 * toks * send[0] * width, experts_t, got_back
     )
-    return (mixed, token_grad, gate_grad, summed[:, :, :hid], summed[:, :, hid:])
+    return (mixed, token_grad, gate_grad, *summed)
 
 
 def solution(mesh):

time: 218 us -> 210 us (0.963)
  blocking collectives: 42.8 us -> 0 us
  waiting for transfers between devices: 98.8 us -> 123 us
  starting transfers between devices: 21.5 us -> 34 us
  local copies, waits for them, and re-layouts: 18.5 us -> 16.1 us
    all_to_all x1 -> x0, blocking collectives: 42.8 us -> none  [exchange(): lax.all_to_all(rows.reshape(count, 8, send[1]), 'expert', split_axis=0, c...]
    reduce_scatter x1, waiting for transfers between devices: 0.01 us -> 38.9 us  [on_device(): lax.psum_scatter(partial.astype(BF), 'dp', scatter_dimension=1, tiled=True)]
    all_to_all x3 -> x4, waiting for transfers between devices: 98.8 us -> 84.5 us  [exchange(): lax.all_to_all(rows.reshape(count, 8, send[1]), 'expert', split_axis=0, c...]
    all_to_all x3 -> x4, starting transfers between devices: 21.5 us -> 33.9 us  [exchange(): lax.all_to_all(rows.reshape(count, 8, send[1]), 'expert', split_axis=0, c...]
    unnamed x33 -> x37, local copies, waits for them, and re-layouts: 16.7 us -> 14.3 us
  transfers between devices with their start and end apart: 5 -> 6, of which waited for: 3 -> 4; matrix products, arithmetic and copies ran while one was open for 0% -> 3% of each run, Pallas kernels for 5% -> 5%
where the time goes in v2:
time: 210 us; the launch traced here: 209 us
  waiting for transfers between devices  123 us (59%)
  starting transfers between devices  34 us (16%)
  Pallas kernels  16.4 us (8%)
  local copies, waits for them, and re-layouts  16.1 us (8%)
  between operations  14.2 us (7%)
  matrix products  4.35 us (2%)
    all_to_all x4, waiting for transfers between devices, exchange(): lax.all_to_all(rows.reshape(count, 8, send[1]), 'expert', split_axis=0, c...  84.5 us
    reduce_scatter x1, waiting for transfers between devices, on_device(): lax.psum_scatter(partial.astype(BF), 'dp', scatter_dimension=1, tiled=True)  38.9 us
    all_to_all x4, starting transfers between devices, exchange(): lax.all_to_all(rows.reshape(count, 8, send[1]), 'expert', split_axis=0, c...  33.9 us
    pallas_call x6, Pallas kernels, call(): pl.pallas_call(body, out_shape=[jax.ShapeDtypeStruct(s, d) for s, d in ou...  16.4 us
    unnamed x37, local copies, waits for them, and re-layouts  14.3 us
    dot_general x1, matrix products, on_device(): lax.dot_general(rows_in, pre_grads, (((0,), (0,)), ((), ())), preferred_e...  4.35 us
  transfers between devices with their start and end apart: 6, of which 4 were waited for; matrix products, arithmetic and copies ran while one was open for 3% of the time, Pallas kernels for 5%

profile of v2, /device:TPU:6, one launch (start us, length us, event | category | flops | bytes accessed | tf_op | source)
XLA Modules:
  0.0 209.3 jit_solution(10787148713311759416)
XLA Ops:
  7.2 0.0 all-gather.2.cloned.1.call-start
  7.2 0.0 copy-start.9
  7.2 1.0 copy-done.9
  8.3 0.7 copy-done.10
  8.9 2.0 shard_map.110
  11.0 0.0 copy-done.15
  11.0 0.0 copy-done.16
  11.0 0.0 copy-done.17
  11.0 0.8 pad_maximum_fusion
  11.7 0.0 all-gather.2.cloned.1.call-update
  11.8 0.0 copy-start.7
  11.8 0.0 copy-start.11
  11.8 0.0 copy-start.12
  11.8 10.4 %all-to-all-start = ((bf16[32,8,3072]{2,1,0:T(8,128)(2,1)}), bf16[32,8,3072]{2,1,0:T(8,128)(2,1)S(1)}, u32[]{:S(2)}, u32[]{:S(2)}) async-start(bf16[32,8,3072]{2,1,0:T(8,128)(2,1)} %bitcast.2), calls=%async_computation | async-start | bytes 3145728 | tf_op jit(solution)/shard_map/all_to_all | solution.py:267
  22.2 0.0 copy-done.7
  22.2 0.0 copy-done.11
  22.2 0.0 copy-done.12
  22.2 2.1 %shard_map.111 = bf16[256,3072]{1,0:T(8,128)(2,1)} custom-call(s32[2,128]{1,0:T(2,128)S(1)} %bitcast.22, f32[2,128]{1,0:T(2,128)S(1)} %bitcast.25, bf16[128,2048]{1,0:T(8,128)(2,1)S(1)} %copy-done.7), custom_call_target="tpu_custom_call" | custom-call | flops 201326592 | bytes 2099200 | tf_op jit(solution)/shard_map/pallas_call | solution.py:247
  24.3 34.9 %all-to-all-done = bf16[32,8,3072]{2,1,0:T(8,128)(2,1)S(1)} async-done(((bf16[32,8,3072]{2,1,0:T(8,128)(2,1)}), bf16[32,8,3072]{2,1,0:T(8,128)(2,1)S(1)}, u32[]{:S(2)}, u32[]{:S(2)}) %all-to-all-start) | async-done | bytes 1572896 | tf_op jit(solution)/shard_map/all_to_all | solution.py:267
  59.3 7.9 %all-to-all-start.1 = ((bf16[32,8,3072]{2,1,0:T(8,128)(2,1)}), bf16[32,8,3072]{2,1,0:T(8,128)(2,1)S(1)}, u32[]{:S(2)}, u32[]{:S(2)}) async-start(bf16[32,8,3072]{2,1,0:T(8,128)(2,1)} %bitcast.4), calls=%async_computation.1 | async-start | bytes 3145728 | tf_op jit(solution)/shard_map/all_to_all | solution.py:267
  67.1 0.0 all-gather.2.cloned.1.call-done
  67.2 0.0 copy-start
  67.2 2.8 %copy-done = bf16[1,2048,1536]{2,1,0:T(8,128)(2,1)S(1)} copy-done((bf16[1,2048,1536]{2,1,0:T(8,128)(2,1)S(1)}, bf16[1,2048,1536]{2,1,0:T(8,128)(2,1)}, u32[]{:S(2)}) %copy-start) | copy-done | bytes 6291480
  70.0 3.0 %shard_map.112 = (bf16[256,3072]{1,0:T(8,128)(2,1)S(1)}, bf16[384,2048]{1,0:T(8,128)(2,1)S(1)}, f32[384,512]{1,0:T(8,128)S(1)}, f32[384,512]{1,0:T(8,128)S(1)}) custom-call(bf16[256,3072]{1,0:T(8,128)(2,1)S(1)} %bitcast.20, bf16[2048,1536]{1,0:T(8,128)(2,1)S(1)} %bitcast.15), custom_call_target="tpu_custom_call" | custom-call | flops 2415919104 | bytes 12582912 | tf_op jit(solution)/shard_map/pallas_call | solution.py:247
  73.0 0.0 copy-start.2
  73.0 1.1 copy-done.2
  74.1 0.9 copy-done.3
  75.0 0.9 copy-done.5
  75.9 1.2 copy-done.13
  77.1 26.8 %all-to-all-done.1 = bf16[32,8,3072]{2,1,0:T(8,128)(2,1)S(1)} async-done(((bf16[32,8,3072]{2,1,0:T(8,128)(2,1)}), bf16[32,8,3072]{2,1,0:T(8,128)(2,1)S(1)}, u32[]{:S(2)}, u32[]{:S(2)}) %all-to-all-start.1) | async-done | bytes 1572896 | tf_op jit(solution)/shard_map/all_to_all | solution.py:267
  103.8 7.7 %all-to-all-start.2 = ((bf16[32,8,3072]{2,1,0:T(8,128)(2,1)}), bf16[32,8,3072]{2,1,0:T(8,128)(2,1)S(1)}, u32[]{:S(2)}, u32[]{:S(2)}) async-start(bf16[32,8,3072]{2,1,0:T(8,128)(2,1)} %bitcast.19), calls=%async_computation.2 | async-start | bytes 3145728 | tf_op jit(solution)/shard_map/all_to_all | solution.py:267
  111.6 0.0 reduce-scatter.2.cloned.1.call-start
  111.7 0.0 copy-start.1
  111.7 2.8 %copy-done.1 = bf16[1,2048,1536]{2,1,0:T(8,128)(2,1)S(1)} copy-done((bf16[1,2048,1536]{2,1,0:T(8,128)(2,1)S(1)}, bf16[1,2048,1536]{2,1,0:T(8,128)(2,1)}, u32[]{:S(2)}) %copy-start.1) | copy-done | bytes 6291480
  114.4 1.1 copy-done.4
  115.6 1.1 copy-done.6
  116.7 4.4 %shard_map.113 = (bf16[256,3072]{1,0:T(8,128)(2,1)}, bf16[384,1024]{1,0:T(8,128)(2,1)S(1)}) custom-call(bf16[256,3072]{1,0:T(8,128)(2,1)S(1)} %bitcast.17, bf16[2048,1536]{1,0:T(8,128)(2,1)S(1)} %bitcast.16, f32[384,512]{1,0:T(8,128)S(1)} %copy-done.4, f32[384,512]{1,0:T(8,128)S(1)} %copy-done.6), custom_call_target="tpu_custom_call" | custom-call | flops 2415919104 | bytes 11796480 | tf_op jit(solution)/shard_map/pallas_call | solution.py:247
  121.2 0.0 copy-done.14
  121.2 4.3 %convert_bitcast_fusion = bf16[1,2048,1024]{2,1,0:T(8,128)(2,1)} fusion(bf16[384,2048]{1,0:T(8,128)(2,1)S(1)} %copy-done.14, bf16[384,1024]{1,0:T(8,128)(2,1)S(1)} %get-tuple-element.42), kind=kOutput, calls=%fused_computation | convolution fusion | flops 1612709888 | bytes 6553600 | tf_op jit(solution)/shard_map/dot_general | solution.py:305
  125.5 0.0 reduce-scatter.2.cloned.1.call-update
  125.5 22.8 %all-to-all-done.2 = bf16[32,8,3072]{2,1,0:T(8,128)(2,1)S(1)} async-done(((bf16[32,8,3072]{2,1,0:T(8,128)(2,1)}), bf16[32,8,3072]{2,1,0:T(8,128)(2,1)S(1)}, u32[]{:S(2)}, u32[]{:S(2)}) %all-to-all-start.2) | async-done | bytes 1572896 | tf_op jit(solution)/shard_map/all_to_all | solution.py:267
  148.3 7.9 %all-to-all-start.3 = ((bf16[32,8,3072]{2,1,0:T(8,128)(2,1)}), bf16[32,8,3072]{2,1,0:T(8,128)(2,1)}, u32[]{:S(2)}, u32[]{:S(2)}) async-start(bf16[32,8,3072]{2,1,0:T(8,128)(2,1)} %bitcast.9), calls=%async_computation.3 | async-start | bytes 3145728 | tf_op jit(solution)/shard_map/all_to_all | solution.py:267
  156.2 1.9 shard_map.114
  158.1 0.6 copy.12
  158.7 38.9 %reduce-scatter.2.cloned.1.call-done = bf16[1,128,1024]{2,1,0:T(8,128)(2,1)} async-done(((bf16[1,2048,1024]{2,1,0:T(8,128)(2,1)}), bf16[1,128,1024]{2,1,0:T(8,128)(2,1)}) %reduce-scatter.2.cloned.1.call-update) | async-done | bytes 262160 | tf_op jit(solution)/shard_map/reduce_scatter | solution.py:308
  197.7 1.8 fusion
  199.5 0.0 all-to-all-done.3
  199.5 2.9 %shard_map.115 = bf16[128,2048]{1,0:T(8,128)(2,1)} custom-call(s32[2,128]{1,0:T(2,128)S(1)} %bitcast.24, bf16[256,3072]{1,0:T(8,128)(2,1)} %bitcast.10.got_ref), custom_call_target="tpu_custom_call" | custom-call | flops 268435456 | bytes 2098176 | tf_op jit(solution)/shard_map/pallas_call | solution.py:247
  (12 shorter events, 0.0 us)
Async XLA Ops:
  7.2 60.0 %all-gather.2.cloned.1.call-start = ((), (), s32[]{:S(2)}) async-start(), calls=%async_computation.5 | async-start | bytes 6684672 | tf_op jit(solution)/shard_map/all_gather | solution.py:280
  7.2 1.0 copy-start.9
  8.3 0.7 copy-start.10
  8.9 2.0 copy-start.15
  8.9 2.0 copy-start.16
  8.9 2.0 copy-start.17
  11.8 10.4 %copy-start.7 = (bf16[128,2048]{1,0:T(8,128)(2,1)S(1)}, bf16[128,2048]{1,0:T(8,128)(2,1)}, u32[]{:S(2)}) copy-start(bf16[128,2048]{1,0:T(8,128)(2,1)} %grad_ref.1) | copy-start | bytes 1572868
  11.8 10.4 %copy-start.11 = (s32[128,2]{0,1:T(2,128)S(1)}, s32[128,2]{0,1:T(2,128)}, u32[]{:S(2)}) copy-start(s32[128,2]{0,1:T(2,128)} %param.9) | copy-start | bytes 3076
  11.8 10.4 %copy-start.12 = (f32[128,2]{0,1:T(2,128)S(1)}, f32[128,2]{0,1:T(2,128)}, u32[]{:S(2)}) copy-start(f32[128,2]{0,1:T(2,128)} %param.8) | copy-start | bytes 3076
  11.8 47.5 %all-to-all-start = ((bf16[32,8,3072]{2,1,0:T(8,128)(2,1)}), bf16[32,8,3072]{2,1,0:T(8,128)(2,1)S(1)}, u32[]{:S(2)}, u32[]{:S(2)}) async-start(bf16[32,8,3072]{2,1,0:T(8,128)(2,1)} %bitcast.2), calls=%async_computation | async-start | bytes 3145728 | tf_op jit(solution)/shard_map/all_to_all | solution.py:267
  59.3 44.6 %all-to-all-start.1 = ((bf16[32,8,3072]{2,1,0:T(8,128)(2,1)}), bf16[32,8,3072]{2,1,0:T(8,128)(2,1)S(1)}, u32[]{:S(2)}, u32[]{:S(2)}) async-start(bf16[32,8,3072]{2,1,0:T(8,128)(2,1)} %bitcast.4), calls=%async_computation.1 | async-start | bytes 3145728 | tf_op jit(solution)/shard_map/all_to_all | solution.py:267
  67.2 2.8 %copy-start = (bf16[1,2048,1536]{2,1,0:T(8,128)(2,1)S(1)}, bf16[1,2048,1536]{2,1,0:T(8,128)(2,1)}, u32[]{:S(2)}) copy-start(bf16[1,2048,1536]{2,1,0:T(8,128)(2,1)} %all-gather.2.cloned.1.call-done) | copy-start | bytes 18874372
  73.0 1.1 copy-start.2
  74.1 0.9 copy-start.3
  75.0 0.9 copy-start.5
  75.9 1.2 copy-start.13
  103.8 44.5 %all-to-all-start.2 = ((bf16[32,8,3072]{2,1,0:T(8,128)(2,1)}), bf16[32,8,3072]{2,1,0:T(8,128)(2,1)S(1)}, u32[]{:S(2)}, u32[]{:S(2)}) async-start(bf16[32,8,3072]{2,1,0:T(8,128)(2,1)} %bitcast.19), calls=%async_computation.2 | async-start | bytes 3145728 | tf_op jit(solution)/shard_map/all_to_all | solution.py:267
  111.6 86.1 %reduce-scatter.2.cloned.1.call-start = ((), (), s32[]{:S(2)}) async-start(), calls=%async_computation.6 | async-start | bytes 4456448 | tf_op jit(solution)/shard_map/reduce_scatter | solution.py:308
  111.7 2.8 %copy-start.1 = (bf16[1,2048,1536]{2,1,0:T(8,128)(2,1)S(1)}, bf16[1,2048,1536]{2,1,0:T(8,128)(2,1)}, u32[]{:S(2)}) copy-start(bf16[1,2048,1536]{2,1,0:T(8,128)(2,1)} %all-gather.2.cloned.1.call-done) | copy-start | bytes 18874372
  114.4 1.1 copy-start.4
  115.6 1.1 copy-start.6
  116.7 4.5 %copy-start.14 = (bf16[384,2048]{1,0:T(8,128)(2,1)S(1)}, bf16[384,2048]{1,0:T(8,128)(2,1)}, u32[]{:S(2)}) copy-start(bf16[384,2048]{1,0:T(8,128)(2,1)} %copy-done.13) | copy-start | bytes 4718596
  148.3 7.9 %copy-start.8 = (bf16[128,2048]{1,0:T(8,128)(2,1)S(1)}, bf16[128,2048]{1,0:T(8,128)(2,1)}, u32[]{:S(2)}) copy-start(bf16[128,2048]{1,0:T(8,128)(2,1)} %grad_ref.1) | copy-start | bytes 1572868
  148.3 51.2 %all-to-all-start.3 = ((bf16[32,8,3072]{2,1,0:T(8,128)(2,1)}), bf16[32,8,3072]{2,1,0:T(8,128)(2,1)}, u32[]{:S(2)}, u32[]{:S(2)}) async-start(bf16[32,8,3072]{2,1,0:T(8,128)(2,1)} %bitcast.9), calls=%async_computation.3 | async-start | bytes 3145728 | tf_op jit(solution)/shard_map/all_to_all | solution.py:267
Sparse Core Ops, SparseCore 0:
  11.9 54.0 all-gather.1
  125.6 71.9 reduce-scatter.1

commit v3 on v2

--- a/solution.py
+++ b/solution.py
@@ -1,3 +1,5 @@
+import functools
+
 import jax
 import jax.numpy as jnp
 from jax import lax
@@ -209,7 +211,9 @@
         ).astype(BF)
 
 
-def forward_rows(got_ref, weights_ref, send_ref, rows_ref, gate_ref, up_ref, hidden_ref, tail_ref):
+def forward_rows(
+    block, core_ref, got_ref, weights_ref, send_ref, turned_ref, gate_ref, up_ref, rows_ref, hidden_ref, tail_ref
+):
     width = rows_ref.shape[1]
     hid = gate_ref.shape[1]
     split_rows(got_ref, rows_ref)
@@ -223,35 +227,109 @@
         product = dot_cols(hidden_ref[...], weights_ref[c : c + 256, 2 * hid : 3 * hid]).astype(BF)
         store_rows(product, send_ref, tail_ref, width, c, 256)
     flush_tail(send_ref, tail_ref, width)
-
-
-def backward_rows(got_ref, weights_ref, gate_ref, up_ref, send_ref, pre_ref, rows_ref, tail_ref):
+    core = core_ref[0]
+    for side, owner in enumerate((core, 1 - core)):
+        for c in range(0, width // 2, block):
+            at = pl.multiple_of(2 * c + owner * block, 128)
+            to = side * (width // 2) + c
+            turned_ref[:, to : to + block] = rows_ref[:, pl.ds(at, block)]
+
+
+def backward_hidden(
+    got_ref, weights_ref, gate_ref, up_ref, turned_ref,
+    pre_ref, keep_ref, give_ref,
+    rows_ref, down_in, gate_in, up_in, turned_in, sums_ref, sems, out_sems,
+):
     width = rows_ref.shape[1]
     hid = gate_ref.shape[1]
+    copies = [
+        pltpu.make_async_copy(source, target, sems.at[i])
+        for i, (source, target) in enumerate(
+            (
+                (weights_ref.at[:, pl.ds(2 * hid, hid)], down_in),
+                (gate_ref, gate_in),
+                (up_ref, up_in),
+                (turned_ref, turned_in),
+            )
+        )
+    ]
+    for copy in copies:
+        copy.start()
     split_rows(got_ref, rows_ref)
+    for copy in copies[:3]:
+        copy.wait()
     for c in range(0, hid, 256):
-        grad = dot(rows_ref[...], weights_ref[:, 2 * hid + c : 2 * hid + c + 256])
-        gate, up = gate_ref[:, c : c + 256], up_ref[:, c : c + 256]
+        grad = dot(rows_ref[...], down_in[:, c : c + 256])
+        gate, up = gate_in[:, c : c + 256], up_in[:, c : c + 256]
         sigma = jax.nn.sigmoid(gate)
         pre_ref[:, hid + c : hid + c + 256] = (grad * gate * sigma).astype(BF)
         pre_ref[:, c : c + 256] = (grad * up * sigma * (1.0 + gate * (1.0 - sigma))).astype(BF)
-    for c in range(0, width, 256):
-        product = dot_cols(pre_ref[...], weights_ref[c : c + 256, 0 : 2 * hid]).astype(BF)
-        store_rows(product, send_ref, tail_ref, width, c, 256)
+    copies[3].wait()
+    leaving = []
+    for side, out_ref in ((1, give_ref), (0, keep_ref)):
+        for c in range(0, width // 2, 256):
+            at = side * (width // 2) + c
+            sums_ref[at : at + 256, :] = lax.dot_general(
+                turned_in[:, at : at + 256],
+                pre_ref[...],
+                (((0,), (0,)), ((), ())),
+                preferred_element_type=F32,
+            ).astype(BF)
+            leaving.append(
+                pltpu.make_async_copy(
+                    sums_ref.at[pl.ds(at, 256)], out_ref.at[pl.ds(c, 256)], out_sems.at[at // 256]
+                )
+            )
+            leaving[-1].start()
+    for copy in leaving:
+        copy.wait()
+
+
+def backward_rows(pre_ref, weights_ref, send_ref, both_in, tail_ref, sems):
+    width = weights_ref.shape[0]
+    both = pre_ref.shape[1]
+    parts = 4
+    size = width // parts
+    copies = [
+        pltpu.make_async_copy(
+            weights_ref.at[pl.ds(i * size, size), pl.ds(0, both)],
+            both_in.at[pl.ds(i * size, size)],
+            sems.at[i],
+        )
+        for i in range(parts)
+    ]
+    for copy in copies:
+        copy.start()
+    for i in range(parts):
+        copies[i].wait()
+        for c in range(i * size, (i + 1) * size, 256):
+            product = dot_cols(pre_ref[...], both_in[c : c + 256, :]).astype(BF)
+            store_rows(product, send_ref, tail_ref, width, c, 256)
     flush_tail(send_ref, tail_ref, width)
 
 
-def call(body, outs, scratch, flops, *args):
+def call(body, outs, scratch, flops, *args, far=(), far_outs=(), scalars=()):
     size = sum(a.size * a.dtype.itemsize for a in args)
     size += sum(o[0][0] * o[0][1] * jnp.dtype(o[1]).itemsize for o in outs)
+    spaces = [
+        pltpu.HBM if i in far else pltpu.SMEM if i in scalars else pltpu.VMEM for i in range(len(args))
+    ]
+    held = [pltpu.VMEM(*s) for s in scratch]
+    if far:
+        held.append(pltpu.SemaphoreType.DMA((4,)))
+    if far_outs:
+        held.append(pltpu.SemaphoreType.DMA((8,)))
     return pl.pallas_call(
         body,
         out_shape=[jax.ShapeDtypeStruct(s, d) for s, d in outs],
-        in_specs=[pl.BlockSpec(memory_space=pltpu.VMEM) for _ in args],
-        out_specs=[pl.BlockSpec(memory_space=pltpu.VMEM) for _ in outs],
-        scratch_shapes=[pltpu.VMEM(s, d) for s, d in scratch],
+        in_specs=[pl.BlockSpec(memory_space=space) for space in spaces],
+        out_specs=[
+            pl.BlockSpec(memory_space=pltpu.HBM if i in far_outs else pltpu.VMEM)
+            for i in range(len(outs))
+        ],
+        scratch_shapes=held,
         cost_estimate=pl.CostEstimate(flops=flops, bytes_accessed=size, transcendentals=0),
-        compiler_params=pltpu.CompilerParams(vmem_limit_bytes=12 << 20),
+        compiler_params=pltpu.CompilerParams(vmem_limit_bytes=(58 if far else 12) << 20),
     )(*args)
 
 
@@ -282,32 +360,59 @@
     got_tok = exchange(send_tok)
     got_tok, send_grad = lax.optimization_barrier((got_tok, send_grad))
     got_grad = exchange(send_grad)
-    send_out, rows_in, gate_pre, up_pre = call(
-        forward_rows,
+    core = (lax.axis_index("dp") % 2).astype(jnp.int32)[None]
+    send_out, turned, gate_pre, up_pre = call(
+        functools.partial(forward_rows, width // lax.axis_size("dp")),
         [(send, BF), ((slots, width), BF), ((slots, hid), F32), ((slots, hid), F32)],
-        [((slots, hid), BF), ((slots - send[0], width), BF)],
+        [((slots, width), BF), ((slots, hid), BF), ((slots - send[0], width), BF)],
         6 * slots * width * hid,
+        core,
         got_tok,
         weights,
+        scalars=(0,),
     )
     got_grad, send_out = lax.optimization_barrier((got_grad, send_out))
     got_out = exchange(send_out)
-    send_back, pre_grads = call(
-        backward_rows,
-        [(send, BF), ((slots, 2 * hid), BF)],
-        [((slots, width), BF), ((slots - send[0], width), BF)],
+    half = (width // 2, 2 * hid)
+    pre_grads, keep, give = call(
+        backward_hidden,
+        [((slots, 2 * hid), BF), (half, BF), (half, BF)],
+        [
+            ((slots, width), BF),
+            ((width, hid), BF),
+            ((slots, hid), F32),
+            ((slots, hid), F32),
+            ((slots, width), BF),
+            ((width, 2 * hid), BF),
+        ],
         6 * slots * width * hid,
         got_grad,
         weights,
         gate_pre,
         up_pre,
-    )
-    partial = lax.dot_general(
-        rows_in, pre_grads, (((0,), (0,)), ((), ())), preferred_element_type=F32
-    )[None]
+        turned,
+        far=(1, 2, 3, 4),
+        far_outs=(1, 2),
+    )
+    dp = lax.axis_size("dp")
+    taken = lax.ppermute(give, "dp", [(i, i ^ 1) for i in range(dp)])
+    pair = (keep.astype(F32) + taken.astype(F32)).astype(BF)
     summed = lax.psum_scatter(
-        partial.astype(BF), "dp", scatter_dimension=1, tiled=True
-    ).astype(F32)
+        pair,
+        "dp",
+        scatter_dimension=0,
+        tiled=True,
+        axis_index_groups=[[i + c for i in range(0, dp, 2)] for c in range(2)],
+    ).astype(F32)[None]
+    (send_back,) = call(
+        backward_rows,
+        [(send, BF)],
+        [((width, 2 * hid), BF), ((slots - send[0], width), BF)],
+        4 * slots * width * hid,
+        pre_grads,
+        weights,
+        far=(1,),
+    )
     got_out, send_back = lax.optimization_barrier((got_out, send_back))
     got_back = exchange(send_back)
     mixed, gate_grad = call(
@@ -320,7 +425,9 @@
         got_out,
         out_grad,
     )
-    got_back, summed = lax.optimization_barrier((got_back, (summed[:, :, :hid], summed[:, :, hid:])))
+    experts_t, summed = lax.optimization_barrier(
+        (experts_t, (summed[:, :, :hid], summed[:, :, hid:]))
+    )
     (token_grad,) = call(
         combine_grads, [((toks, width), BF)], [], 4 * toks * send[0] * width, experts_t, got_back
     )

time: 210 us -> 206 us (0.981); the launches traced: 209 us -> 203 us
  waiting for transfers between devices: 123 us -> 109 us
  Pallas kernels: 16.4 us -> 28.7 us
  local copies, waits for them, and re-layouts: 16.1 us -> 8.95 us
  other arithmetic: 0.77 us -> 5.63 us
  matrix products: 4.35 us -> 0 us
    reduce_scatter x1, waiting for transfers between devices: 38.9 us -> 24 us  [on_device(): lax.psum_scatter(pair, 'dp', scatter_dimension=0, tiled=True, axis_index_...]
    pallas_call x6 -> x7, Pallas kernels: 16.4 us -> 28.7 us  [call(): pl.pallas_call(body, out_shape=[jax.ShapeDtypeStruct(s, d) for s, d in ou...]
    unnamed x37 -> x27, local copies, waits for them, and re-layouts: 14.3 us -> 8.12 us
    dot_general x1 -> x0, matrix products: 4.35 us -> none  [on_device(): lax.dot_general(rows_in, pre_grads, (((0,), (0,)), ((), ())), preferred_e...]
    convert_element_type x0 -> x1, other arithmetic: none -> 3.87 us  [on_device(): pair = (keep.astype(F32) + taken.astype(F32)).astype(BF)]
  transfers between devices with their start and end apart: 6 -> 7, of which waited for: 4 -> 5; matrix products, arithmetic and copies ran while one was open for 3% -> 3% of each run, Pallas kernels for 5% -> 12%
where the time goes in v3:
time: 206 us; the launch traced here: 203 us
  waiting for transfers between devices  109 us (53%)
  starting transfers between devices  35.7 us (17%)
  Pallas kernels  28.7 us (14%)
  between operations  14.2 us (7%)
  local copies, waits for them, and re-layouts  8.95 us (4%)
  other arithmetic  5.63 us (3%)
    all_to_all x4, waiting for transfers between devices, exchange(): lax.all_to_all(rows.reshape(count, 8, send[1]), 'expert', split_axis=0, c...  85.3 us
    all_to_all x4, starting transfers between devices, exchange(): lax.all_to_all(rows.reshape(count, 8, send[1]), 'expert', split_axis=0, c...  33.7 us
    pallas_call x7, Pallas kernels, call(): pl.pallas_call(body, out_shape=[jax.ShapeDtypeStruct(s, d) for s, d in ou...  28.7 us
    reduce_scatter x1, waiting for transfers between devices, on_device(): lax.psum_scatter(pair, 'dp', scatter_dimension=0, tiled=True, axis_index_...  24 us
    unnamed x27, local copies, waits for them, and re-layouts  8.12 us
  transfers between devices with their start and end apart: 7, of which 5 were waited for; matrix products, arithmetic and copies ran while one was open for 3% of the time, Pallas kernels for 12%

profile of v3, /device:TPU:6, one launch (start us, length us, event | category | flops | bytes accessed | tf_op | source)
XLA Modules:
  0.0 202.6 jit_solution(13626552975681018407)
XLA Ops:
  7.2 0.0 all-gather.2.cloned.1.call-start
  7.2 0.0 copy-start.5
  7.2 1.0 copy-done.5
  8.3 0.0 copy-start.6
  8.3 0.7 copy-done.6
  8.9 0.0 copy-start.10
  8.9 2.1 %shard_map.110 = bf16[256,3072]{1,0:T(8,128)(2,1)} custom-call(s32[2,128]{1,0:T(2,128)S(1)} %bitcast.20, bf16[128,2048]{1,0:T(8,128)(2,1)S(1)} %copy-done.5), custom_call_target="tpu_custom_call" | custom-call | flops 201326592 | bytes 2098176 | tf_op jit(solution)/shard_map/pallas_call | solution.py:322
  11.0 0.0 copy-done.10
  11.0 0.0 copy-done.11
  11.0 0.0 copy-done.12
  11.0 0.0 copy-start.7
  11.0 0.0 copy-start.8
  11.0 0.8 pad_maximum_fusion
  11.8 0.0 all-gather.2.cloned.1.call-update
  11.8 10.2 %all-to-all-start = ((bf16[32,8,3072]{2,1,0:T(8,128)(2,1)}), bf16[32,8,3072]{2,1,0:T(8,128)(2,1)S(1)}, u32[]{:S(2)}, u32[]{:S(2)}) async-start(bf16[32,8,3072]{2,1,0:T(8,128)(2,1)} %bitcast.2), calls=%async_computation | async-start | bytes 3145728 | tf_op jit(solution)/shard_map/all_to_all | solution.py:345
  22.1 0.0 copy-done.4
  22.1 0.0 copy-done.7
  22.1 0.0 copy-done.8
  22.1 2.0 shard_map.111
  24.2 35.0 %all-to-all-done = bf16[32,8,3072]{2,1,0:T(8,128)(2,1)S(1)} async-done(((bf16[32,8,3072]{2,1,0:T(8,128)(2,1)}), bf16[32,8,3072]{2,1,0:T(8,128)(2,1)S(1)}, u32[]{:S(2)}, u32[]{:S(2)}) %all-to-all-start) | async-done | bytes 1572896 | tf_op jit(solution)/shard_map/all_to_all | solution.py:345
  59.2 7.9 %all-to-all-start.1 = ((bf16[32,8,3072]{2,1,0:T(8,128)(2,1)}), bf16[32,8,3072]{2,1,0:T(8,128)(2,1)}, u32[]{:S(2)}, u32[]{:S(2)}) async-start(bf16[32,8,3072]{2,1,0:T(8,128)(2,1)} %bitcast.4), calls=%async_computation.1 | async-start | bytes 3145728 | tf_op jit(solution)/shard_map/all_to_all | solution.py:345
  67.1 0.0 all-gather.2.cloned.1.call-done
  67.1 0.0 copy-start
  67.2 2.8 %copy-done = bf16[1,2048,1536]{2,1,0:T(8,128)(2,1)S(1)} copy-done((bf16[1,2048,1536]{2,1,0:T(8,128)(2,1)S(1)}, bf16[1,2048,1536]{2,1,0:T(8,128)(2,1)}, u32[]{:S(2)}) %copy-start) | copy-done | bytes 6291480
  69.9 4.6 %shard_map.112 = (bf16[256,3072]{1,0:T(8,128)(2,1)}, bf16[384,2048]{1,0:T(8,128)(2,1)S(1)}, f32[384,512]{1,0:T(8,128)S(1)}, f32[384,512]{1,0:T(8,128)S(1)}) custom-call(s32[1]{0:T(128)} %bitcast.6.core_ref, bf16[256,3072]{1,0:T(8,128)(2,1)S(1)} %bitcast.18, bf16[2048,1536]{1,0:T(8,128)(2,1)S(1)} %bitcast.17), custom_call_target="tpu_custom_call" | custom-call | flops 2415919104 | bytes 12582916 | tf_op jit(solution)/shard_map/pallas_call | solution.py:322
  74.6 1.2 copy-done.1
  75.8 0.9 copy-done.2
  76.7 0.9 copy-done.3
  77.5 26.3 %all-to-all-done.1 = bf16[32,8,3072]{2,1,0:T(8,128)(2,1)} async-done(((bf16[32,8,3072]{2,1,0:T(8,128)(2,1)}), bf16[32,8,3072]{2,1,0:T(8,128)(2,1)}, u32[]{:S(2)}, u32[]{:S(2)}) %all-to-all-start.1) | async-done | bytes 1572896 | tf_op jit(solution)/shard_map/all_to_all | solution.py:345
  103.9 7.7 %all-to-all-start.2 = ((bf16[32,8,3072]{2,1,0:T(8,128)(2,1)}), bf16[32,8,3072]{2,1,0:T(8,128)(2,1)S(1)}, u32[]{:S(2)}, u32[]{:S(2)}) async-start(bf16[32,8,3072]{2,1,0:T(8,128)(2,1)} %bitcast.8), calls=%async_computation.2 | async-start | bytes 3145728 | tf_op jit(solution)/shard_map/all_to_all | solution.py:345
  111.6 0.0 reduce-scatter.2.cloned.1.call-start
  111.7 8.7 %shard_map.113 = (bf16[384,1024]{1,0:T(8,128)(2,1)}, bf16[1024,1024]{1,0:T(8,128)(2,1)}, bf16[1024,1024]{1,0:T(8,128)(2,1)}) custom-call(bf16[256,3072]{1,0:T(8,128)(2,1)} %bitcast.5.got_ref, bf16[2048,1536]{1,0:T(8,128)(2,1)} %bitcast.15, f32[384,512]{1,0:T(8,128)} %copy-done.2, f32[384,512]{1,0:T(8,128)} %copy-done.3, bf16[384,2048]{1,0:T(8,128)(2,1)} %copy-done.1), custom_call_target="tpu_custom_call" | custom-call | flops 2415919104 | bytes 15990784 | tf_op jit(solution)/shard_map/pallas_call | solution.py:322
  120.4 1.9 collective-permute-start
  122.3 0.0 copy-start.9
  122.3 6.5 %shard_map.114 = bf16[256,3072]{1,0:T(8,128)(2,1)} custom-call(bf16[384,1024]{1,0:T(8,128)(2,1)} %get-tuple-element.39.pre_ref, bf16[2048,1536]{1,0:T(8,128)(2,1)} %bitcast.16), custom_call_target="tpu_custom_call" | custom-call | flops 1610612736 | bytes 8650752 | tf_op jit(solution)/shard_map/pallas_call | solution.py:322
  128.8 0.0 collective-permute-done
  128.8 0.0 copy-done.9
  128.8 3.9 %add_convert_fusion = bf16[1024,1024]{1,0:T(8,128)(2,1)} fusion(bf16[1024,1024]{1,0:T(8,128)(2,1)} %collective-permute-done, bf16[1024,1024]{1,0:T(8,128)(2,1)S(1)} %copy-done.9), kind=kLoop, calls=%fused_computation | loop fusion | flops 4194304 | bytes 6291456 | tf_op jit(solution)/shard_map/convert_element_type | solution.py:399
  132.7 0.0 reduce-scatter.2.cloned.1.call-update
  132.7 15.6 %all-to-all-done.2 = bf16[32,8,3072]{2,1,0:T(8,128)(2,1)S(1)} async-done(((bf16[32,8,3072]{2,1,0:T(8,128)(2,1)}), bf16[32,8,3072]{2,1,0:T(8,128)(2,1)S(1)}, u32[]{:S(2)}, u32[]{:S(2)}) %all-to-all-start.2) | async-done | bytes 1572896 | tf_op jit(solution)/shard_map/all_to_all | solution.py:345
  148.3 7.8 %all-to-all-start.3 = ((bf16[32,8,3072]{2,1,0:T(8,128)(2,1)}), bf16[32,8,3072]{2,1,0:T(8,128)(2,1)}, u32[]{:S(2)}, u32[]{:S(2)}) async-start(bf16[32,8,3072]{2,1,0:T(8,128)(2,1)} %bitcast.26), calls=%async_computation.4 | async-start | bytes 3145728 | tf_op jit(solution)/shard_map/all_to_all | solution.py:345
  156.1 1.9 shard_map.115
  158.0 0.6 copy.12
  158.6 24.0 %reduce-scatter.2.cloned.1.call-done = bf16[128,1024]{1,0:T(8,128)(2,1)} async-done(((bf16[1024,1024]{1,0:T(8,128)(2,1)}), bf16[128,1024]{1,0:T(8,128)(2,1)}) %reduce-scatter.2.cloned.1.call-update) | async-done | bytes 262160 | tf_op jit(solution)/shard_map/reduce_scatter | solution.py:400
  182.6 1.0 bitcast_convert_fusion
  183.6 0.8 fusion
  184.5 8.4 %all-to-all-done.3 = bf16[32,8,3072]{2,1,0:T(8,128)(2,1)} async-done(((bf16[32,8,3072]{2,1,0:T(8,128)(2,1)}), bf16[32,8,3072]{2,1,0:T(8,128)(2,1)}, u32[]{:S(2)}, u32[]{:S(2)}) %all-to-all-start.3) | async-done | bytes 1572896 | tf_op jit(solution)/shard_map/all_to_all | solution.py:345
  192.9 2.9 %shard_map.116 = bf16[128,2048]{1,0:T(8,128)(2,1)} custom-call(s32[2,128]{1,0:T(2,128)S(1)} %bitcast.23, bf16[256,3072]{1,0:T(8,128)(2,1)} %bitcast.13.got_ref), custom_call_target="tpu_custom_call" | custom-call | flops 268435456 | bytes 2098176 | tf_op jit(solution)/shard_map/pallas_call | solution.py:322
  (6 shorter events, 0.0 us)
Async XLA Ops:
  7.2 60.0 %all-gather.2.cloned.1.call-start = ((), (), s32[]{:S(2)}) async-start(), calls=%async_computation.5 | async-start | bytes 6684672 | tf_op jit(solution)/shard_map/all_gather | solution.py:358
  7.2 1.0 copy-start.5
  8.3 0.7 copy-start.6
  8.9 2.1 %copy-start.10 = (bf16[1,128,512]{2,1,0:T(8,128)(2,1)S(1)}, bf16[1,128,512]{2,1,0:T(8,128)(2,1)}, u32[]{:S(2)}) copy-start(bf16[1,128,512]{2,1,0:T(8,128)(2,1)} %param.12) | copy-start | bytes 393220
  8.9 2.1 %copy-start.11 = (bf16[1,128,512]{2,1,0:T(8,128)(2,1)S(1)}, bf16[1,128,512]{2,1,0:T(8,128)(2,1)}, u32[]{:S(2)}) copy-start(bf16[1,128,512]{2,1,0:T(8,128)(2,1)} %param.11) | copy-start | bytes 393220
  8.9 2.1 %copy-start.12 = (bf16[1,128,512]{2,1,0:T(8,128)(2,1)S(1)}, bf16[1,128,512]{2,1,0:T(8,128)(2,1)}, u32[]{:S(2)}) copy-start(bf16[1,128,512]{2,1,0:T(8,128)(2,1)} %param.10) | copy-start | bytes 393220
  11.0 11.1 %copy-start.4 = (bf16[128,2048]{1,0:T(8,128)(2,1)S(1)}, bf16[128,2048]{1,0:T(8,128)(2,1)}, u32[]{:S(2)}) copy-start(bf16[128,2048]{1,0:T(8,128)(2,1)} %grad_ref.1) | copy-start | bytes 1572868
  11.0 11.1 %copy-start.7 = (s32[128,2]{0,1:T(2,128)S(1)}, s32[128,2]{0,1:T(2,128)}, u32[]{:S(2)}) copy-start(s32[128,2]{0,1:T(2,128)} %param.9) | copy-start | bytes 3076
  11.0 11.1 %copy-start.8 = (f32[128,2]{0,1:T(2,128)S(1)}, f32[128,2]{0,1:T(2,128)}, u32[]{:S(2)}) copy-start(f32[128,2]{0,1:T(2,128)} %param.8) | copy-start | bytes 3076
  11.8 47.3 %all-to-all-start = ((bf16[32,8,3072]{2,1,0:T(8,128)(2,1)}), bf16[32,8,3072]{2,1,0:T(8,128)(2,1)S(1)}, u32[]{:S(2)}, u32[]{:S(2)}) async-start(bf16[32,8,3072]{2,1,0:T(8,128)(2,1)} %bitcast.2), calls=%async_computation | async-start | bytes 3145728 | tf_op jit(solution)/shard_map/all_to_all | solution.py:345
  59.2 44.7 %all-to-all-start.1 = ((bf16[32,8,3072]{2,1,0:T(8,128)(2,1)}), bf16[32,8,3072]{2,1,0:T(8,128)(2,1)}, u32[]{:S(2)}, u32[]{:S(2)}) async-start(bf16[32,8,3072]{2,1,0:T(8,128)(2,1)} %bitcast.4), calls=%async_computation.1 | async-start | bytes 3145728 | tf_op jit(solution)/shard_map/all_to_all | solution.py:345
  67.1 2.8 %copy-start = (bf16[1,2048,1536]{2,1,0:T(8,128)(2,1)S(1)}, bf16[1,2048,1536]{2,1,0:T(8,128)(2,1)}, u32[]{:S(2)}) copy-start(bf16[1,2048,1536]{2,1,0:T(8,128)(2,1)} %all-gather.2.cloned.1.call-done) | copy-start | bytes 18874372
  74.6 1.2 copy-start.1
  75.8 0.9 copy-start.2
  76.6 0.9 copy-start.3
  103.9 44.5 %all-to-all-start.2 = ((bf16[32,8,3072]{2,1,0:T(8,128)(2,1)}), bf16[32,8,3072]{2,1,0:T(8,128)(2,1)S(1)}, u32[]{:S(2)}, u32[]{:S(2)}) async-start(bf16[32,8,3072]{2,1,0:T(8,128)(2,1)} %bitcast.8), calls=%async_computation.2 | async-start | bytes 3145728 | tf_op jit(solution)/shard_map/all_to_all | solution.py:345
  111.6 71.0 %reduce-scatter.2.cloned.1.call-start = ((), (), s32[]{:S(2)}) async-start(), calls=%async_computation.6 | async-start | bytes 2359296 | tf_op jit(solution)/shard_map/reduce_scatter | solution.py:400
  120.4 8.4 %collective-permute-start = (bf16[1024,1024]{1,0:T(8,128)(2,1)}, bf16[1024,1024]{1,0:T(8,128)(2,1)}, u32[]{:S(2)}, u32[]{:S(2)}) collective-permute-start(bf16[1024,1024]{1,0:T(8,128)(2,1)} %get-tuple-element.43), channel_id=1, source_target_pairs={{0,32},{32,0},{64,96},{96,64},{128,160},{160,128},{192,224},{224,1... | collective-permute-start | bytes 6291464 | tf_op jit(solution)/shard_map/ppermute | solution.py:398
  122.3 6.5 %copy-start.9 = (bf16[1024,1024]{1,0:T(8,128)(2,1)S(1)}, bf16[1024,1024]{1,0:T(8,128)(2,1)}, u32[]{:S(2)}) copy-start(bf16[1024,1024]{1,0:T(8,128)(2,1)} %get-tuple-element.42) | copy-start | bytes 6291460
  148.3 44.6 %all-to-all-start.3 = ((bf16[32,8,3072]{2,1,0:T(8,128)(2,1)}), bf16[32,8,3072]{2,1,0:T(8,128)(2,1)}, u32[]{:S(2)}, u32[]{:S(2)}) async-start(bf16[32,8,3072]{2,1,0:T(8,128)(2,1)} %bitcast.26), calls=%async_computation.4 | async-start | bytes 3145728 | tf_op jit(solution)/shard_map/all_to_all | solution.py:345
Sparse Core Ops, SparseCore 0:
  12.0 54.0 all-gather.1
  132.9 49.7 reduce-scatter.1

commit v4 on v3

--- a/solution.py
+++ b/solution.py
@@ -10,6 +10,8 @@
 BF = jnp.bfloat16
 F32 = jnp.float32
 TILE = 512
+AXIS = {}
+EARLY = (3, 4, 5)
 
 
 def iota(shape, axis):
@@ -173,19 +175,37 @@
         ).astype(BF)
 
 
-def split_rows(got_ref, rows_ref):
+def turned_blocks(place_ref, width, size):
+    z, core = place_ref[0], place_ref[1]
+    chips = AXIS["dp"] // 2
+    block = width // (2 * chips)
+    size = min(size, block)
+    pairs = []
+    for side, owner in enumerate((core, 1 - core)):
+        for k in range(chips):
+            shard = 2 * lax.rem(z + (chips - k), chips) + owner
+            for c in range(0, block, size):
+                column = pl.multiple_of(shard * block + c, 128)
+                pairs.append((side * (width // 2) + k * block + c, column))
+    return size, pairs
+
+
+def split_rows(place_ref, got_ref, rows_ref, tail_ref):
     count = got_ref.shape[0]
     width = rows_ref.shape[1]
     half = width // 2
     tail = count // 2
-    rows_ref[0:count, :] = got_ref[:, 0:width]
     row, col = iota((tail, count), 0), iota((tail, count), 1)
     for h in range(2):
         pick = one_hot(col == (row >> 2) * 8 + h * 4 + (row & 3))
         for c in range(0, half, TILE):
-            rows_ref[count : count + tail, h * half + c : h * half + c + TILE] = dot(
+            tail_ref[:, h * half + c : h * half + c + TILE] = dot(
                 pick, got_ref[:, width + c : width + c + TILE]
             ).astype(BF)
+    size, pairs = turned_blocks(place_ref, width, TILE)
+    for to, column in pairs:
+        rows_ref[0:count, to : to + size] = got_ref[:, pl.ds(column, size)]
+        rows_ref[count:, to : to + size] = tail_ref[:, pl.ds(column, size)]
 
 
 def tail_spread(count):
@@ -194,10 +214,13 @@
     return [one_hot(row == (col >> 2) * 8 + h * 4 + (col & 3)) for h in range(2)]
 
 
-def store_rows(product, send_ref, tail_ref, width, at, size):
+def store_rows(place_ref, product, send_ref, tail_ref, width, at):
     count = send_ref.shape[0]
-    send_ref[:, at : at + size] = product[0:count]
-    tail_ref[:, at : at + size] = product[count:]
+    size, pairs = turned_blocks(place_ref, width, 256)
+    for to, column in pairs:
+        if at <= to < at + 256:
+            send_ref[:, pl.ds(column, size)] = product[0:count, to - at : to - at + size]
+            tail_ref[:, pl.ds(column, size)] = product[count:, to - at : to - at + size]
 
 
 def flush_tail(send_ref, tail_ref, width):
@@ -211,34 +234,37 @@
         ).astype(BF)
 
 
+def dot_turned(rows_ref, mine_ref, other_ref, columns):
+    half = mine_ref.shape[0]
+    return dot(rows_ref[:, 0:half], mine_ref[:, columns]) + dot(
+        rows_ref[:, half:], other_ref[:, columns]
+    )
+
+
 def forward_rows(
-    block, core_ref, got_ref, weights_ref, send_ref, turned_ref, gate_ref, up_ref, rows_ref, hidden_ref, tail_ref
+    place_ref, got_ref, mine_ref, other_ref, send_ref, rows_ref, gate_ref, up_ref, hidden_ref, tail_ref
 ):
     width = rows_ref.shape[1]
+    half = width // 2
     hid = gate_ref.shape[1]
-    split_rows(got_ref, rows_ref)
+    split_rows(place_ref, got_ref, rows_ref, tail_ref)
     for c in range(0, hid, 256):
-        gate = dot(rows_ref[...], weights_ref[:, c : c + 256])
-        up = dot(rows_ref[...], weights_ref[:, hid + c : hid + c + 256])
+        gate = dot_turned(rows_ref, mine_ref, other_ref, slice(c, c + 256))
+        up = dot_turned(rows_ref, mine_ref, other_ref, slice(hid + c, hid + c + 256))
         gate_ref[:, c : c + 256] = gate
         up_ref[:, c : c + 256] = up
         hidden_ref[:, c : c + 256] = (gate * jax.nn.sigmoid(gate) * up).astype(BF)
-    for c in range(0, width, 256):
-        product = dot_cols(hidden_ref[...], weights_ref[c : c + 256, 2 * hid : 3 * hid]).astype(BF)
-        store_rows(product, send_ref, tail_ref, width, c, 256)
+    for side, weights_ref in enumerate((mine_ref, other_ref)):
+        for c in range(0, half, 256):
+            product = dot_cols(hidden_ref[...], weights_ref[c : c + 256, 2 * hid : 3 * hid])
+            store_rows(place_ref, product.astype(BF), send_ref, tail_ref, width, side * half + c)
     flush_tail(send_ref, tail_ref, width)
-    core = core_ref[0]
-    for side, owner in enumerate((core, 1 - core)):
-        for c in range(0, width // 2, block):
-            at = pl.multiple_of(2 * c + owner * block, 128)
-            to = side * (width // 2) + c
-            turned_ref[:, to : to + block] = rows_ref[:, pl.ds(at, block)]
 
 
 def backward_hidden(
-    got_ref, weights_ref, gate_ref, up_ref, turned_ref,
+    place_ref, got_ref, mine_ref, other_ref, gate_ref, up_ref, turned_ref,
     pre_ref, keep_ref, give_ref,
-    rows_ref, down_in, gate_in, up_in, turned_in, sums_ref, sems, out_sems,
+    rows_ref, mine_in, other_in, gate_in, up_in, turned_in, sums_ref, tail_ref, sems, out_sems,
 ):
     width = rows_ref.shape[1]
     hid = gate_ref.shape[1]
@@ -246,7 +272,8 @@
         pltpu.make_async_copy(source, target, sems.at[i])
         for i, (source, target) in enumerate(
             (
-                (weights_ref.at[:, pl.ds(2 * hid, hid)], down_in),
+                (mine_ref.at[:, pl.ds(2 * hid, hid)], mine_in),
+                (other_ref.at[:, pl.ds(2 * hid, hid)], other_in),
                 (gate_ref, gate_in),
                 (up_ref, up_in),
                 (turned_ref, turned_in),
@@ -255,16 +282,16 @@
     ]
     for copy in copies:
         copy.start()
-    split_rows(got_ref, rows_ref)
-    for copy in copies[:3]:
+    split_rows(place_ref, got_ref, rows_ref, tail_ref)
+    for copy in copies[:4]:
         copy.wait()
     for c in range(0, hid, 256):
-        grad = dot(rows_ref[...], down_in[:, c : c + 256])
+        grad = dot_turned(rows_ref, mine_in, other_in, slice(c, c + 256))
         gate, up = gate_in[:, c : c + 256], up_in[:, c : c + 256]
         sigma = jax.nn.sigmoid(gate)
         pre_ref[:, hid + c : hid + c + 256] = (grad * gate * sigma).astype(BF)
         pre_ref[:, c : c + 256] = (grad * up * sigma * (1.0 + gate * (1.0 - sigma))).astype(BF)
-    copies[3].wait()
+    copies[4].wait()
     leaving = []
     for side, out_ref in ((1, give_ref), (0, keep_ref)):
         for c in range(0, width // 2, 256):
@@ -285,27 +312,27 @@
         copy.wait()
 
 
-def backward_rows(pre_ref, weights_ref, send_ref, both_in, tail_ref, sems):
-    width = weights_ref.shape[0]
+def backward_rows(place_ref, pre_ref, mine_ref, other_ref, send_ref, both_in, tail_ref, sems):
+    half = mine_ref.shape[0]
     both = pre_ref.shape[1]
-    parts = 4
-    size = width // parts
-    copies = [
-        pltpu.make_async_copy(
-            weights_ref.at[pl.ds(i * size, size), pl.ds(0, both)],
-            both_in.at[pl.ds(i * size, size)],
-            sems.at[i],
+    size = half // 2
+    copies = []
+    for i in range(4):
+        source = (mine_ref, other_ref)[i // 2]
+        copies.append(
+            pltpu.make_async_copy(
+                source.at[pl.ds(i % 2 * size, size), pl.ds(0, both)],
+                both_in.at[pl.ds(i * size, size)],
+                sems.at[i],
+            )
         )
-        for i in range(parts)
-    ]
-    for copy in copies:
-        copy.start()
-    for i in range(parts):
+        copies[-1].start()
+    for i in range(4):
         copies[i].wait()
         for c in range(i * size, (i + 1) * size, 256):
             product = dot_cols(pre_ref[...], both_in[c : c + 256, :]).astype(BF)
-            store_rows(product, send_ref, tail_ref, width, c, 256)
-    flush_tail(send_ref, tail_ref, width)
+            store_rows(place_ref, product, send_ref, tail_ref, 2 * half, c)
+    flush_tail(send_ref, tail_ref, 2 * half)
 
 
 def call(body, outs, scratch, flops, *args, far=(), far_outs=(), scalars=()):
@@ -316,7 +343,7 @@
     ]
     held = [pltpu.VMEM(*s) for s in scratch]
     if far:
-        held.append(pltpu.SemaphoreType.DMA((4,)))
+        held.append(pltpu.SemaphoreType.DMA((5,)))
     if far_outs:
         held.append(pltpu.SemaphoreType.DMA((8,)))
     return pl.pallas_call(
@@ -334,6 +361,7 @@
 
 
 def on_device(tokens, gates, experts, gate_weight, up_weight, down_weight, out_grad):
+    AXIS["dp"] = lax.axis_size("dp")
     toks, width = tokens.shape
     hid = gate_weight.shape[2]
     count = lax.axis_size("expert") * gate_weight.shape[0]
@@ -355,20 +383,32 @@
     pack_flops = 2 * send[0] * toks * send[1]
     (send_tok,) = call(pack_tokens, [(send, BF)], [], pack_flops, experts_t, tokens)
     shards, send_tok = lax.optimization_barrier(((gate_weight, up_weight, down_weight), send_tok))
-    weights = lax.all_gather(jnp.concatenate(shards, axis=2), "dp", axis=1, tiled=True)[0]
+    dp = lax.axis_size("dp")
+    chips = dp // 2
+    swap = [(i, i ^ 1) for i in range(dp)]
+
+    def along(rows, steps):
+        pairs = [(z * 2 + c, (z + steps) % chips * 2 + c) for z in range(chips) for c in range(2)]
+        return lax.ppermute(rows, "dp", pairs)
+
+    shard = jnp.concatenate(shards, axis=2)[0]
+    mine = jnp.concatenate([shard] + [along(shard, k) for k in range(1, chips)], axis=0)
+    other = lax.ppermute(mine, "dp", swap)
     (send_grad,) = call(pack_grads, [(send, BF)], [], pack_flops, experts_t, gates_t, out_grad)
     got_tok = exchange(send_tok)
     got_tok, send_grad = lax.optimization_barrier((got_tok, send_grad))
     got_grad = exchange(send_grad)
-    core = (lax.axis_index("dp") % 2).astype(jnp.int32)[None]
+    index = lax.axis_index("dp")
+    place = jnp.stack([index // 2, index % 2]).astype(jnp.int32)
     send_out, turned, gate_pre, up_pre = call(
-        functools.partial(forward_rows, width // lax.axis_size("dp")),
+        forward_rows,
         [(send, BF), ((slots, width), BF), ((slots, hid), F32), ((slots, hid), F32)],
-        [((slots, width), BF), ((slots, hid), BF), ((slots - send[0], width), BF)],
+        [((slots, hid), BF), ((slots - send[0], width), BF)],
         6 * slots * width * hid,
-        core,
+        place,
         got_tok,
-        weights,
+        mine,
+        other,
         scalars=(0,),
     )
     got_grad, send_out = lax.optimization_barrier((got_grad, send_out))
@@ -379,41 +419,50 @@
         [((slots, 2 * hid), BF), (half, BF), (half, BF)],
         [
             ((slots, width), BF),
-            ((width, hid), BF),
+            ((width // 2, hid), BF),
+            ((width // 2, hid), BF),
             ((slots, hid), F32),
             ((slots, hid), F32),
             ((slots, width), BF),
             ((width, 2 * hid), BF),
+            ((slots - send[0], width), BF),
         ],
         6 * slots * width * hid,
+        place,
         got_grad,
-        weights,
+        mine,
+        other,
         gate_pre,
         up_pre,
         turned,
-        far=(1, 2, 3, 4),
+        far=(2, 3, 4, 5, 6),
         far_outs=(1, 2),
-    )
-    dp = lax.axis_size("dp")
-    taken = lax.ppermute(give, "dp", [(i, i ^ 1) for i in range(dp)])
-    pair = (keep.astype(F32) + taken.astype(F32)).astype(BF)
-    summed = lax.psum_scatter(
-        pair,
-        "dp",
-        scatter_dimension=0,
-        tiled=True,
-        axis_index_groups=[[i + c for i in range(0, dp, 2)] for c in range(2)],
-    ).astype(F32)[None]
+        scalars=(0,),
+    )
+    taken = lax.ppermute(give, "dp", swap)
+    pair = (keep.astype(F32) + taken.astype(F32)).astype(BF).reshape(chips, width // dp, 2 * hid)
+    parts = {k: along(pair[k], -k) for k in range(1, chips) if k in EARLY}
+    late = [pair[k] for k in range(1, chips) if k not in EARLY]
     (send_back,) = call(
         backward_rows,
         [(send, BF)],
         [((width, 2 * hid), BF), ((slots - send[0], width), BF)],
         4 * slots * width * hid,
+        place,
         pre_grads,
-        weights,
-        far=(1,),
-    )
-    got_out, send_back = lax.optimization_barrier((got_out, send_back))
+        mine,
+        other,
+        far=(2, 3),
+        scalars=(0,),
+    )
+    got_out, send_back, late = lax.optimization_barrier((got_out, send_back, late))
+    for k in range(1, chips):
+        if k not in EARLY:
+            parts[k] = along(late.pop(0), -k)
+    summed = pair[0].astype(F32)
+    for k in range(1, chips):
+        summed = summed + parts[k].astype(F32)
+    summed = summed[None]
     got_back = exchange(send_back)
     mixed, gate_grad = call(
         combine_out,

time: 206 us -> 252 us (1.22)
  the two profiles are of different devices: /device:TPU:6 before, /device:TPU:136 now
where the time goes in v4:
time: 252 us; the launch traced here: 251 us
  waiting for transfers between devices  109 us (43%)
  starting transfers between devices  96.1 us (38%)
  Pallas kernels  29.2 us (12%)
  local copies, waits for them, and re-layouts  11.2 us (4%)
  other arithmetic  4.51 us (2%)
    ppermute x14, waiting for transfers between devices, along(): return lax.ppermute(rows, 'dp', pairs)  64.6 us
    ppermute x14, starting transfers between devices, along(): return lax.ppermute(rows, 'dp', pairs)  55.9 us
    all_to_all x4, waiting for transfers between devices, exchange(): lax.all_to_all(rows.reshape(count, 8, send[1]), 'expert', split_axis=0, c...  40 us
    all_to_all x4, starting transfers between devices, exchange(): lax.all_to_all(rows.reshape(count, 8, send[1]), 'expert', split_axis=0, c...  36.4 us
    pallas_call x7, Pallas kernels, call(): pl.pallas_call(body, out_shape=[jax.ShapeDtypeStruct(s, d) for s, d in ou...  29.2 us
    unnamed x45, local copies, waits for them, and re-layouts  9.23 us
  transfers between devices with their start and end apart: 20, of which 8 were waited for; matrix products, arithmetic and copies ran while one was open for 3% of the time, Pallas kernels for 10%

profile of v4, /device:TPU:136, one launch (start us, length us, event | category | flops | bytes accessed | tf_op | source)
XLA Modules:
  0.0 251.0 jit_solution(11306149555141198273)
XLA Ops:
  0.6 1.0 copy-done.8
  1.7 0.7 copy-done.9
  2.4 2.0 shard_map.110
  4.4 10.2 %all-to-all-start = ((bf16[32,8,3072]{2,1,0:T(8,128)(2,1)}), bf16[32,8,3072]{2,1,0:T(8,128)(2,1)}, u32[]{:S(2)}, u32[]{:S(2)}) async-start(bf16[32,8,3072]{2,1,0:T(8,128)(2,1)} %bitcast.2), calls=%async_computation | async-start | bytes 3145728 | tf_op jit(solution)/shard_map/all_to_all | solution.py:373
  14.7 4.4 %collective-permute-start = (bf16[128,1536]{1,0:T(8,128)(2,1)S(1)}, bf16[128,1536]{1,0:T(8,128)(2,1)S(1)}, u32[]{:S(2)}, u32[]{:S(2)}) collective-permute-start(bf16[128,1536]{1,0:T(8,128)(2,1)S(1)} %maximum_bitcast_fusion), channel_id=1, source_target_pairs={{0,64},{32,96},{64,128},{96,160},{128,192},{160,224},{192,256},{22... | collective-permute-start | bytes 1179656 | tf_op jit(solution)/shard_map/ppermute | solution.py:392
  19.1 1.9 collective-permute-start.6
  21.1 7.3 %collective-permute-start.5 = (bf16[128,1536]{1,0:T(8,128)(2,1)S(1)}, bf16[128,1536]{1,0:T(8,128)(2,1)S(1)}, u32[]{:S(2)}, u32[]{:S(2)}) collective-permute-start(bf16[128,1536]{1,0:T(8,128)(2,1)S(1)} %maximum_bitcast_fusion), channel_id=1, source_target_pairs={{0,384},{32,416},{64,448},{96,480},{128,0},{160,32},{192,64},{224,... | collective-permute-start | bytes 1179656 | tf_op jit(solution)/shard_map/ppermute | solution.py:392
  28.4 3.9 %collective-permute-start.4 = (bf16[128,1536]{1,0:T(8,128)(2,1)S(1)}, bf16[128,1536]{1,0:T(8,128)(2,1)S(1)}, u32[]{:S(2)}, u32[]{:S(2)}) collective-permute-start(bf16[128,1536]{1,0:T(8,128)(2,1)S(1)} %maximum_bitcast_fusion), channel_id=1, source_target_pairs={{0,320},{32,352},{64,384},{96,416},{128,448},{160,480},{192,0},{22... | collective-permute-start | bytes 1179656 | tf_op jit(solution)/shard_map/ppermute | solution.py:392
  32.3 5.5 %collective-permute-start.1 = (bf16[128,1536]{1,0:T(8,128)(2,1)S(1)}, bf16[128,1536]{1,0:T(8,128)(2,1)S(1)}, u32[]{:S(2)}, u32[]{:S(2)}) collective-permute-start(bf16[128,1536]{1,0:T(8,128)(2,1)S(1)} %maximum_bitcast_fusion), channel_id=1, source_target_pairs={{0,128},{32,160},{64,192},{96,224},{128,256},{160,288},{192,320},{... | collective-permute-start | bytes 1179656 | tf_op jit(solution)/shard_map/ppermute | solution.py:392
  37.9 1.9 collective-permute-start.2
  39.8 25.0 %collective-permute-done.1 = bf16[128,1536]{1,0:T(8,128)(2,1)S(1)} collective-permute-done((bf16[128,1536]{1,0:T(8,128)(2,1)S(1)}, bf16[128,1536]{1,0:T(8,128)(2,1)S(1)}, u32[]{:S(2)}, u32[]{:S(2)}) %collective-permute-start.1) | collective-permute-done | bytes 393248 | tf_op jit(solution)/shard_map/ppermute | solution.py:392
  64.8 1.9 collective-permute-start.3
  66.8 30.5 %collective-permute-done.2 = bf16[128,1536]{1,0:T(8,128)(2,1)S(1)} collective-permute-done((bf16[128,1536]{1,0:T(8,128)(2,1)S(1)}, bf16[128,1536]{1,0:T(8,128)(2,1)S(1)}, u32[]{:S(2)}, u32[]{:S(2)}) %collective-permute-start.2) | collective-permute-done | bytes 393248 | tf_op jit(solution)/shard_map/ppermute | solution.py:392
  97.5 1.9 collective-permute-start.7
  99.4 0.9 shard_map.111
  100.3 1.2 copy-done.1
  101.5 9.8 %all-to-all-start.1 = ((bf16[32,8,3072]{2,1,0:T(8,128)(2,1)}), bf16[32,8,3072]{2,1,0:T(8,128)(2,1)}, u32[]{:S(2)}, u32[]{:S(2)}) async-start(bf16[32,8,3072]{2,1,0:T(8,128)(2,1)} %bitcast.18), calls=%async_computation.1 | async-start | bytes 3145728 | tf_op jit(solution)/shard_map/all_to_all | solution.py:373
  111.4 6.0 %shard_map.112 = (bf16[256,3072]{1,0:T(8,128)(2,1)S(1)}, bf16[384,2048]{1,0:T(8,128)(2,1)S(1)}, f32[384,512]{1,0:T(8,128)S(1)}, f32[384,512]{1,0:T(8,128)S(1)}) custom-call(s32[2]{0:T(128)S(1)} %pad_add_fusion.place_ref, bf16[256,3072]{1,0:T(8,128)(2,1)} %bitcast.3.got_ref, bf16[1024,1536]{1,0:T(8,128)(2,1)S(1)} %constant_dynamic-update-slice_fusion.mine_ref, ...), custom_call_target="tpu_custom_call" | custom-call | flops 2415919104 | bytes 12582920 | tf_op jit(solution)/shard_map/pallas_call | solution.py:349
  117.5 1.2 copy-done.2
  118.6 1.1 copy-done.3
  119.8 0.9 copy-done.4
  120.6 0.9 copy-done.5
  121.5 29.1 %all-to-all-done.1 = bf16[32,8,3072]{2,1,0:T(8,128)(2,1)} async-done(((bf16[32,8,3072]{2,1,0:T(8,128)(2,1)}), bf16[32,8,3072]{2,1,0:T(8,128)(2,1)}, u32[]{:S(2)}, u32[]{:S(2)}) %all-to-all-start.1) | async-done | bytes 1572896 | tf_op jit(solution)/shard_map/all_to_all | solution.py:373
  150.7 6.5 %all-to-all-start.2 = ((bf16[32,8,3072]{2,1,0:T(8,128)(2,1)}), bf16[32,8,3072]{2,1,0:T(8,128)(2,1)S(1)}, u32[]{:S(2)}, u32[]{:S(2)}) async-start(bf16[32,8,3072]{2,1,0:T(8,128)(2,1)} %bitcast.20), calls=%async_computation.2 | async-start | bytes 3145728 | tf_op jit(solution)/shard_map/all_to_all | solution.py:373
  157.2 8.8 %shard_map.113 = (bf16[384,1024]{1,0:T(8,128)(2,1)}, bf16[1024,1024]{1,0:T(8,128)(2,1)}, bf16[1024,1024]{1,0:T(8,128)(2,1)}) custom-call(s32[2]{0:T(128)} %copy-done.11, bf16[256,3072]{1,0:T(8,128)(2,1)} %bitcast.5.got_ref, bf16[1024,1536]{1,0:T(8,128)(2,1)} %copy-done, bf16[1024,1536]{1,0:T(8,128)(2,1)} %collective-permute-done.7.other_ref, ...), custom_call_target="tpu_custom_call" | custom-call | flops 2415919104 | bytes 15990792 | tf_op jit(solution)/shard_map/pallas_call | solution.py:349
  166.0 1.9 collective-permute-start.8
  168.0 4.3 %collective-permute-done.8 = bf16[1024,1024]{1,0:T(8,128)(2,1)S(1)} collective-permute-done((bf16[1024,1024]{1,0:T(8,128)(2,1)}, bf16[1024,1024]{1,0:T(8,128)(2,1)S(1)}, u32[]{:S(2)}, u32[]{:S(2)}) %collective-permute-start.8) | collective-permute-done | bytes 2097184 | tf_op jit(solution)/shard_map/ppermute | solution.py:442
  172.3 2.6 %add_convert_fusion = bf16[1024,1024]{1,0:T(8,128)(2,1)S(1)} fusion(bf16[1024,1024]{1,0:T(8,128)(2,1)S(1)} %collective-permute-done.8, bf16[1024,1024]{1,0:T(8,128)(2,1)} %get-tuple-element.44), kind=kLoop, calls=%fused_computation | loop fusion | flops 4194304 | bytes 6291456 | tf_op jit(solution)/shard_map/convert_element_type | solution.py:443
  174.9 1.4 copy-done.13
  176.3 1.1 fusion
  177.3 1.9 collective-permute-start.11
  179.3 7.1 %collective-permute-start.13 = (bf16[128,1024]{1,0:T(8,128)(2,1)S(1)}, bf16[128,1024]{1,0:T(8,128)(2,1)S(1)}, u32[]{:S(2)}, u32[]{:S(2)}) collective-permute-start(bf16[128,1024]{1,0:T(8,128)(2,1)S(1)} %get-tuple-element.63), channel_id=1, source_target_pairs={{0,192},{32,224},{64,256},{96,288},{128,320},{160,352},{192,384},{... | collective-permute-start | bytes 786440 | tf_op jit(solution)/shard_map/ppermute | solution.py:392
  186.4 6.6 %shard_map.114 = bf16[256,3072]{1,0:T(8,128)(2,1)} custom-call(s32[2]{0:T(128)} %copy-done.11, bf16[384,1024]{1,0:T(8,128)(2,1)} %get-tuple-element.43.pre_ref, bf16[1024,1536]{1,0:T(8,128)(2,1)} %copy-done, bf16[1024,1536]{1,0:T(8,128)(2,1)} %collective-permute-done.7.other_ref), custom_call_target="tpu_custom_call" | custom-call | flops 1610612736 | bytes 8650760 | tf_op jit(solution)/shard_map/pallas_call | solution.py:349
  193.0 6.2 %collective-permute-start.12 = (bf16[128,1024]{1,0:T(8,128)(2,1)}, bf16[128,1024]{1,0:T(8,128)(2,1)}, u32[]{:S(2)}, u32[]{:S(2)}) collective-permute-start(bf16[128,1024]{1,0:T(8,128)(2,1)} %get-tuple-element.64), channel_id=1, source_target_pairs={{0,256},{32,288},{64,320},{96,352},{128,384},{160,416},{192,448},{... | collective-permute-start | bytes 786440 | tf_op jit(solution)/shard_map/ppermute | solution.py:392
  199.2 9.8 %all-to-all-start.3 = ((bf16[32,8,3072]{2,1,0:T(8,128)(2,1)}), bf16[32,8,3072]{2,1,0:T(8,128)(2,1)}, u32[]{:S(2)}, u32[]{:S(2)}) async-start(bf16[32,8,3072]{2,1,0:T(8,128)(2,1)} %bitcast.27), calls=%async_computation.3 | async-start | bytes 3145728 | tf_op jit(solution)/shard_map/all_to_all | solution.py:373
  209.1 1.9 collective-permute-start.9
  211.0 2.5 collective-permute-start.10
  213.5 5.5 %collective-permute-start.14 = (bf16[128,1024]{1,0:T(8,128)(2,1)}, bf16[128,1024]{1,0:T(8,128)(2,1)}, u32[]{:S(2)}, u32[]{:S(2)}) collective-permute-start(bf16[128,1024]{1,0:T(8,128)(2,1)} %get-tuple-element.50), channel_id=1, source_target_pairs={{0,128},{32,160},{64,192},{96,224},{128,256},{160,288},{192,320},{... | collective-permute-start | bytes 786440 | tf_op jit(solution)/shard_map/ppermute | solution.py:392
  219.0 3.9 %collective-permute-start.15 = (bf16[128,1024]{1,0:T(8,128)(2,1)}, bf16[128,1024]{1,0:T(8,128)(2,1)}, u32[]{:S(2)}, u32[]{:S(2)}) collective-permute-start(bf16[128,1024]{1,0:T(8,128)(2,1)} %get-tuple-element.51), channel_id=1, source_target_pairs={{0,64},{32,96},{64,128},{96,160},{128,192},{160,224},{192,256},{22... | collective-permute-start | bytes 786440 | tf_op jit(solution)/shard_map/ppermute | solution.py:392
  223.0 1.9 shard_map.115
  224.8 0.6 copy.12
  225.5 3.9 %collective-permute-done.10 = bf16[128,1024]{1,0:T(8,128)(2,1)} collective-permute-done((bf16[128,1024]{1,0:T(8,128)(2,1)}, bf16[128,1024]{1,0:T(8,128)(2,1)}, u32[]{:S(2)}, u32[]{:S(2)}) %collective-permute-start.10) | collective-permute-done | bytes 262176 | tf_op jit(solution)/shard_map/ppermute | solution.py:392
  229.4 2.1 collective-permute-done.14
  231.5 3.2 %collective-permute-done.15 = bf16[128,1024]{1,0:T(8,128)(2,1)} collective-permute-done((bf16[128,1024]{1,0:T(8,128)(2,1)}, bf16[128,1024]{1,0:T(8,128)(2,1)}, u32[]{:S(2)}, u32[]{:S(2)}) %collective-permute-start.15) | collective-permute-done | bytes 262176 | tf_op jit(solution)/shard_map/ppermute | solution.py:392
  234.6 1.8 add_bitcast_fusion
  236.5 0.8 fusion.1
  237.3 10.8 %all-to-all-done.3 = bf16[32,8,3072]{2,1,0:T(8,128)(2,1)} async-done(((bf16[32,8,3072]{2,1,0:T(8,128)(2,1)}), bf16[32,8,3072]{2,1,0:T(8,128)(2,1)}, u32[]{:S(2)}, u32[]{:S(2)}) %all-to-all-start.3) | async-done | bytes 1572896 | tf_op jit(solution)/shard_map/all_to_all | solution.py:373
  248.1 2.9 %shard_map.116 = bf16[128,2048]{1,0:T(8,128)(2,1)} custom-call(s32[2,128]{1,0:T(2,128)S(1)} %bitcast.24, bf16[256,3072]{1,0:T(8,128)(2,1)} %bitcast.13.got_ref), custom_call_target="tpu_custom_call" | custom-call | flops 268435456 | bytes 2098176 | tf_op jit(solution)/shard_map/pallas_call | solution.py:349
  (52 shorter events, 0.4 us)
Async XLA Ops:
  0.6 1.0 copy-start.8
  1.7 0.7 copy-start.9
  2.4 12.3 %copy-start.14 = (bf16[1,128,512]{2,1,0:T(8,128)(2,1)S(1)}, bf16[1,128,512]{2,1,0:T(8,128)(2,1)}, u32[]{:S(2)}) copy-start(bf16[1,128,512]{2,1,0:T(8,128)(2,1)} %param.12) | copy-start | bytes 393220
  2.4 12.3 %copy-start.15 = (bf16[1,128,512]{2,1,0:T(8,128)(2,1)S(1)}, bf16[1,128,512]{2,1,0:T(8,128)(2,1)}, u32[]{:S(2)}) copy-start(bf16[1,128,512]{2,1,0:T(8,128)(2,1)} %param.11) | copy-start | bytes 393220
  2.4 12.3 %copy-start.16 = (bf16[1,128,512]{2,1,0:T(8,128)(2,1)S(1)}, bf16[1,128,512]{2,1,0:T(8,128)(2,1)}, u32[]{:S(2)}) copy-start(bf16[1,128,512]{2,1,0:T(8,128)(2,1)} %param.10) | copy-start | bytes 393220
  4.4 97.1 %all-to-all-start = ((bf16[32,8,3072]{2,1,0:T(8,128)(2,1)}), bf16[32,8,3072]{2,1,0:T(8,128)(2,1)}, u32[]{:S(2)}, u32[]{:S(2)}) async-start(bf16[32,8,3072]{2,1,0:T(8,128)(2,1)} %bitcast.2), calls=%async_computation | async-start | bytes 3145728 | tf_op jit(solution)/shard_map/all_to_all | solution.py:373
  14.7 84.7 %copy-start.6 = (bf16[128,2048]{1,0:T(8,128)(2,1)S(1)}, bf16[128,2048]{1,0:T(8,128)(2,1)}, u32[]{:S(2)}) copy-start(bf16[128,2048]{1,0:T(8,128)(2,1)} %grad_ref.1) | copy-start | bytes 1572868
  14.7 84.7 %copy-start.10 = (s32[128,2]{0,1:T(2,128)S(1)}, s32[128,2]{0,1:T(2,128)}, u32[]{:S(2)}) copy-start(s32[128,2]{0,1:T(2,128)} %param.9) | copy-start | bytes 3076
  14.7 84.7 %copy-start.12 = (f32[128,2]{0,1:T(2,128)S(1)}, f32[128,2]{0,1:T(2,128)}, u32[]{:S(2)}) copy-start(f32[128,2]{0,1:T(2,128)} %param.8) | copy-start | bytes 3076
  14.7 23.1 %collective-permute-start = (bf16[128,1536]{1,0:T(8,128)(2,1)S(1)}, bf16[128,1536]{1,0:T(8,128)(2,1)S(1)}, u32[]{:S(2)}, u32[]{:S(2)}) collective-permute-start(bf16[128,1536]{1,0:T(8,128)(2,1)S(1)} %maximum_bitcast_fusion), channel_id=1, source_target_pairs={{0,64},{32,96},{64,128},{96,160},{128,192},{160,224},{192,256},{22... | collective-permute-start | bytes 1179656 | tf_op jit(solution)/shard_map/ppermute | solution.py:392
  19.1 78.3 %collective-permute-start.6 = (bf16[128,1536]{1,0:T(8,128)(2,1)S(1)}, bf16[128,1536]{1,0:T(8,128)(2,1)S(1)}, u32[]{:S(2)}, u32[]{:S(2)}) collective-permute-start(bf16[128,1536]{1,0:T(8,128)(2,1)S(1)} %maximum_bitcast_fusion), channel_id=1, source_target_pairs={{0,448},{32,480},{64,0},{96,32},{128,64},{160,96},{192,128},{224,1... | collective-permute-start | bytes 1179656 | tf_op jit(solution)/shard_map/ppermute | solution.py:392
  21.1 76.3 %collective-permute-start.5 = (bf16[128,1536]{1,0:T(8,128)(2,1)S(1)}, bf16[128,1536]{1,0:T(8,128)(2,1)S(1)}, u32[]{:S(2)}, u32[]{:S(2)}) collective-permute-start(bf16[128,1536]{1,0:T(8,128)(2,1)S(1)} %maximum_bitcast_fusion), channel_id=1, source_target_pairs={{0,384},{32,416},{64,448},{96,480},{128,0},{160,32},{192,64},{224,... | collective-permute-start | bytes 1179656 | tf_op jit(solution)/shard_map/ppermute | solution.py:392
  28.4 68.9 %collective-permute-start.4 = (bf16[128,1536]{1,0:T(8,128)(2,1)S(1)}, bf16[128,1536]{1,0:T(8,128)(2,1)S(1)}, u32[]{:S(2)}, u32[]{:S(2)}) collective-permute-start(bf16[128,1536]{1,0:T(8,128)(2,1)S(1)} %maximum_bitcast_fusion), channel_id=1, source_target_pairs={{0,320},{32,352},{64,384},{96,416},{128,448},{160,480},{192,0},{22... | collective-permute-start | bytes 1179656 | tf_op jit(solution)/shard_map/ppermute | solution.py:392
  32.3 32.5 %collective-permute-start.1 = (bf16[128,1536]{1,0:T(8,128)(2,1)S(1)}, bf16[128,1536]{1,0:T(8,128)(2,1)S(1)}, u32[]{:S(2)}, u32[]{:S(2)}) collective-permute-start(bf16[128,1536]{1,0:T(8,128)(2,1)S(1)} %maximum_bitcast_fusion), channel_id=1, source_target_pairs={{0,128},{32,160},{64,192},{96,224},{128,256},{160,288},{192,320},{... | collective-permute-start | bytes 1179656 | tf_op jit(solution)/shard_map/ppermute | solution.py:392
  37.9 59.4 %collective-permute-start.2 = (bf16[128,1536]{1,0:T(8,128)(2,1)S(1)}, bf16[128,1536]{1,0:T(8,128)(2,1)S(1)}, u32[]{:S(2)}, u32[]{:S(2)}) collective-permute-start(bf16[128,1536]{1,0:T(8,128)(2,1)S(1)} %maximum_bitcast_fusion), channel_id=1, source_target_pairs={{0,192},{32,224},{64,256},{96,288},{128,320},{160,352},{192,384},{... | collective-permute-start | bytes 1179656 | tf_op jit(solution)/shard_map/ppermute | solution.py:392
  64.8 32.5 %collective-permute-start.3 = (bf16[128,1536]{1,0:T(8,128)(2,1)S(1)}, bf16[128,1536]{1,0:T(8,128)(2,1)S(1)}, u32[]{:S(2)}, u32[]{:S(2)}) collective-permute-start(bf16[128,1536]{1,0:T(8,128)(2,1)S(1)} %maximum_bitcast_fusion), channel_id=1, source_target_pairs={{0,256},{32,288},{64,320},{96,352},{128,384},{160,416},{192,448},{... | collective-permute-start | bytes 1179656 | tf_op jit(solution)/shard_map/ppermute | solution.py:392
  97.5 20.0 %copy-start = (bf16[1024,1536]{1,0:T(8,128)(2,1)}, bf16[1024,1536]{1,0:T(8,128)(2,1)S(1)}, u32[]{:S(2)}) copy-start(bf16[1024,1536]{1,0:T(8,128)(2,1)S(1)} %constant_dynamic-update-slice_fusion.mine_ref) | copy-start | bytes 9437188
  97.5 14.0 %collective-permute-start.7 = (bf16[1024,1536]{1,0:T(8,128)(2,1)S(1)}, bf16[1024,1536]{1,0:T(8,128)(2,1)}, u32[]{:S(2)}, u32[]{:S(2)}) collective-permute-start(bf16[1024,1536]{1,0:T(8,128)(2,1)S(1)} %constant_dynamic-update-slice_fusion.mine_ref), channel_id=1, source_target_pairs={{0,32},{32,0},{64,96},{96,64},{128,160},{160,128},{192,224},{224,1... | collective-permute-start | bytes 9437192 | tf_op jit(solution)/shard_map/ppermute | solution.py:396
  100.3 1.2 copy-start.1
  101.5 49.2 %all-to-all-start.1 = ((bf16[32,8,3072]{2,1,0:T(8,128)(2,1)}), bf16[32,8,3072]{2,1,0:T(8,128)(2,1)}, u32[]{:S(2)}, u32[]{:S(2)}) async-start(bf16[32,8,3072]{2,1,0:T(8,128)(2,1)} %bitcast.18), calls=%async_computation.1 | async-start | bytes 3145728 | tf_op jit(solution)/shard_map/all_to_all | solution.py:373
  111.4 6.0 %copy-start.11 = (s32[2]{0:T(128)}, s32[2]{0:T(128)S(1)}, u32[]{:S(2)}) copy-start(s32[2]{0:T(128)S(1)} %pad_add_fusion.place_ref) | copy-start | bytes 28
  117.4 1.2 copy-start.2
  118.6 1.1 copy-start.3
  119.8 0.9 copy-start.4
  120.6 0.9 copy-start.5
  150.7 48.5 %all-to-all-start.2 = ((bf16[32,8,3072]{2,1,0:T(8,128)(2,1)}), bf16[32,8,3072]{2,1,0:T(8,128)(2,1)S(1)}, u32[]{:S(2)}, u32[]{:S(2)}) async-start(bf16[32,8,3072]{2,1,0:T(8,128)(2,1)} %bitcast.20), calls=%async_computation.2 | async-start | bytes 3145728 | tf_op jit(solution)/shard_map/all_to_all | solution.py:373
  166.0 6.3 %collective-permute-start.8 = (bf16[1024,1024]{1,0:T(8,128)(2,1)}, bf16[1024,1024]{1,0:T(8,128)(2,1)S(1)}, u32[]{:S(2)}, u32[]{:S(2)}) collective-permute-start(bf16[1024,1024]{1,0:T(8,128)(2,1)} %get-tuple-element.45), channel_id=1, source_target_pairs={{0,32},{32,0},{64,96},{96,64},{128,160},{160,128},{192,224},{224,1... | collective-permute-start | bytes 6291464 | tf_op jit(solution)/shard_map/ppermute | solution.py:442
  174.9 1.4 copy-start.13
  177.3 36.2 %collective-permute-start.11 = (bf16[128,1024]{1,0:T(8,128)(2,1)S(1)}, bf16[128,1024]{1,0:T(8,128)(2,1)S(1)}, u32[]{:S(2)}, u32[]{:S(2)}) collective-permute-start(bf16[128,1024]{1,0:T(8,128)(2,1)S(1)} %get-tuple-element.62), channel_id=1, source_target_pairs={{0,320},{32,352},{64,384},{96,416},{128,448},{160,480},{192,0},{22... | collective-permute-start | bytes 786440 | tf_op jit(solution)/shard_map/ppermute | solution.py:392
  179.3 39.7 %collective-permute-start.13 = (bf16[128,1024]{1,0:T(8,128)(2,1)S(1)}, bf16[128,1024]{1,0:T(8,128)(2,1)S(1)}, u32[]{:S(2)}, u32[]{:S(2)}) collective-permute-start(bf16[128,1024]{1,0:T(8,128)(2,1)S(1)} %get-tuple-element.63), channel_id=1, source_target_pairs={{0,192},{32,224},{64,256},{96,288},{128,320},{160,352},{192,384},{... | collective-permute-start | bytes 786440 | tf_op jit(solution)/shard_map/ppermute | solution.py:392
  193.0 29.9 %copy-start.7 = (bf16[128,2048]{1,0:T(8,128)(2,1)S(1)}, bf16[128,2048]{1,0:T(8,128)(2,1)}, u32[]{:S(2)}) copy-start(bf16[128,2048]{1,0:T(8,128)(2,1)} %grad_ref.1) | copy-start | bytes 1572868
  193.0 32.5 %collective-permute-start.12 = (bf16[128,1024]{1,0:T(8,128)(2,1)}, bf16[128,1024]{1,0:T(8,128)(2,1)}, u32[]{:S(2)}, u32[]{:S(2)}) collective-permute-start(bf16[128,1024]{1,0:T(8,128)(2,1)} %get-tuple-element.64), channel_id=1, source_target_pairs={{0,256},{32,288},{64,320},{96,352},{128,384},{160,416},{192,448},{... | collective-permute-start | bytes 786440 | tf_op jit(solution)/shard_map/ppermute | solution.py:392
  199.2 48.9 %all-to-all-start.3 = ((bf16[32,8,3072]{2,1,0:T(8,128)(2,1)}), bf16[32,8,3072]{2,1,0:T(8,128)(2,1)}, u32[]{:S(2)}, u32[]{:S(2)}) async-start(bf16[32,8,3072]{2,1,0:T(8,128)(2,1)} %bitcast.27), calls=%async_computation.3 | async-start | bytes 3145728 | tf_op jit(solution)/shard_map/all_to_all | solution.py:373
  209.1 16.4 %collective-permute-start.9 = (bf16[128,1024]{1,0:T(8,128)(2,1)}, bf16[128,1024]{1,0:T(8,128)(2,1)}, u32[]{:S(2)}, u32[]{:S(2)}) collective-permute-start(bf16[128,1024]{1,0:T(8,128)(2,1)} %get-tuple-element.48), channel_id=1, source_target_pairs={{0,448},{32,480},{64,0},{96,32},{128,64},{160,96},{192,128},{224,1... | collective-permute-start | bytes 786440 | tf_op jit(solution)/shard_map/ppermute | solution.py:392
  211.0 18.4 %collective-permute-start.10 = (bf16[128,1024]{1,0:T(8,128)(2,1)}, bf16[128,1024]{1,0:T(8,128)(2,1)}, u32[]{:S(2)}, u32[]{:S(2)}) collective-permute-start(bf16[128,1024]{1,0:T(8,128)(2,1)} %get-tuple-element.49), channel_id=1, source_target_pairs={{0,384},{32,416},{64,448},{96,480},{128,0},{160,32},{192,64},{224,... | collective-permute-start | bytes 786440 | tf_op jit(solution)/shard_map/ppermute | solution.py:392
  213.5 11.3 %copy-start.17 = (bf16[128,1024]{1,0:T(8,128)(2,1)}, bf16[128,1024]{1,0:T(8,128)(2,1)S(1)}, u32[]{:S(2)}) copy-start(bf16[128,1024]{1,0:T(8,128)(2,1)S(1)} %collective-permute-done.11) | copy-start | bytes 786436
  213.5 18.0 %collective-permute-start.14 = (bf16[128,1024]{1,0:T(8,128)(2,1)}, bf16[128,1024]{1,0:T(8,128)(2,1)}, u32[]{:S(2)}, u32[]{:S(2)}) collective-permute-start(bf16[128,1024]{1,0:T(8,128)(2,1)} %get-tuple-element.50), channel_id=1, source_target_pairs={{0,128},{32,160},{64,192},{96,224},{128,256},{160,288},{192,320},{... | collective-permute-start | bytes 786440 | tf_op jit(solution)/shard_map/ppermute | solution.py:392
  219.0 5.8 %copy-start.18 = (bf16[128,1024]{1,0:T(8,128)(2,1)}, bf16[128,1024]{1,0:T(8,128)(2,1)S(1)}, u32[]{:S(2)}) copy-start(bf16[128,1024]{1,0:T(8,128)(2,1)S(1)} %collective-permute-done.13) | copy-start | bytes 786436
  219.0 15.6 %collective-permute-start.15 = (bf16[128,1024]{1,0:T(8,128)(2,1)}, bf16[128,1024]{1,0:T(8,128)(2,1)}, u32[]{:S(2)}, u32[]{:S(2)}) collective-permute-start(bf16[128,1024]{1,0:T(8,128)(2,1)} %get-tuple-element.51), channel_id=1, source_target_pairs={{0,64},{32,96},{64,128},{96,160},{128,192},{160,224},{192,256},{22... | collective-permute-start | bytes 786440 | tf_op jit(solution)/shard_map/ppermute | solution.py:392

commit v5 on v4

--- a/solution.py
+++ b/solution.py
@@ -392,7 +392,12 @@
         return lax.ppermute(rows, "dp", pairs)
 
     shard = jnp.concatenate(shards, axis=2)[0]
-    mine = jnp.concatenate([shard] + [along(shard, k) for k in range(1, chips)], axis=0)
+    came = {0: shard}
+    for k in range(1, chips // 2 + 1):
+        came[k] = along(came[k - 1], 1)
+    for k in range(chips - 1, chips // 2, -1):
+        came[k] = along(came[(k + 1) % chips], -1)
+    mine = jnp.concatenate([came[k] for k in range(chips)], axis=0)
     other = lax.ppermute(mine, "dp", swap)
     (send_grad,) = call(pack_grads, [(send, BF)], [], pack_flops, experts_t, gates_t, out_grad)
     got_tok = exchange(send_tok)

time: 252 us -> 222 us (0.88)
  the two profiles are of different devices: /device:TPU:136 before, /device:TPU:6 now
where the time goes in v5:
time: 222 us; the launch traced here: 219 us
  starting transfers between devices  95.6 us (43%)
  waiting for transfers between devices  77.1 us (35%)
  Pallas kernels  29.2 us (13%)
  local copies, waits for them, and re-layouts  11.2 us (5%)
  other arithmetic  4.51 us (2%)
    ppermute x14, starting transfers between devices, along(): return lax.ppermute(rows, 'dp', pairs)  53.6 us
    all_to_all x4, starting transfers between devices, exchange(): lax.all_to_all(rows.reshape(count, 8, send[1]), 'expert', split_axis=0, c...  38.1 us
    ppermute x14, waiting for transfers between devices, along(): return lax.ppermute(rows, 'dp', pairs)  38.1 us
    all_to_all x4, waiting for transfers between devices, exchange(): lax.all_to_all(rows.reshape(count, 8, send[1]), 'expert', split_axis=0, c...  34.6 us
    pallas_call x7, Pallas kernels, call(): pl.pallas_call(body, out_shape=[jax.ShapeDtypeStruct(s, d) for s, d in ou...  29.2 us
    unnamed x45, local copies, waits for them, and re-layouts  9.23 us
  transfers between devices with their start and end apart: 20, of which 10 were waited for; matrix products, arithmetic and copies ran while one was open for 3% of the time, Pallas kernels for 11%

profile of v5, /device:TPU:6, one launch (start us, length us, event | category | flops | bytes accessed | tf_op | source)
XLA Modules:
  0.0 218.6 jit_solution(1108830908781987626)
XLA Ops:
  0.6 1.0 copy-done.8
  2.4 2.0 shard_map.110
  4.4 10.3 %all-to-all-start = ((bf16[32,8,3072]{2,1,0:T(8,128)(2,1)}), bf16[32,8,3072]{2,1,0:T(8,128)(2,1)}, u32[]{:S(2)}, u32[]{:S(2)}) async-start(bf16[32,8,3072]{2,1,0:T(8,128)(2,1)} %bitcast.2), calls=%async_computation | async-start | bytes 3145728 | tf_op jit(solution)/shard_map/all_to_all | solution.py:373
  14.8 4.4 %collective-permute-start = (bf16[128,1536]{1,0:T(8,128)(2,1)S(1)}, bf16[128,1536]{1,0:T(8,128)(2,1)S(1)}, u32[]{:S(2)}, u32[]{:S(2)}) collective-permute-start(bf16[128,1536]{1,0:T(8,128)(2,1)S(1)} %maximum_bitcast_fusion), channel_id=1, source_target_pairs={{0,64},{32,96},{64,128},{96,160},{128,192},{160,224},{192,256},{22... | collective-permute-start | bytes 1179656 | tf_op jit(solution)/shard_map/ppermute | solution.py:392
  19.2 8.6 %collective-permute-start.4 = (bf16[128,1536]{1,0:T(8,128)(2,1)S(1)}, bf16[128,1536]{1,0:T(8,128)(2,1)S(1)}, u32[]{:S(2)}, u32[]{:S(2)}) collective-permute-start(bf16[128,1536]{1,0:T(8,128)(2,1)S(1)} %maximum_bitcast_fusion), channel_id=1, source_target_pairs={{0,448},{32,480},{64,0},{96,32},{128,64},{160,96},{192,128},{224,1... | collective-permute-start | bytes 1179656 | tf_op jit(solution)/shard_map/ppermute | solution.py:392
  27.8 6.6 %collective-permute-done = bf16[128,1536]{1,0:T(8,128)(2,1)S(1)} collective-permute-done((bf16[128,1536]{1,0:T(8,128)(2,1)S(1)}, bf16[128,1536]{1,0:T(8,128)(2,1)S(1)}, u32[]{:S(2)}, u32[]{:S(2)}) %collective-permute-start) | collective-permute-done | bytes 393248 | tf_op jit(solution)/shard_map/ppermute | solution.py:392
  34.4 1.9 collective-permute-start.1
  36.3 5.1 %collective-permute-start.5 = (bf16[128,1536]{1,0:T(8,128)(2,1)S(1)}, bf16[128,1536]{1,0:T(8,128)(2,1)S(1)}, u32[]{:S(2)}, u32[]{:S(2)}) collective-permute-start(bf16[128,1536]{1,0:T(8,128)(2,1)S(1)} %collective-permute-done.4), channel_id=1, source_target_pairs={{0,448},{32,480},{64,0},{96,32},{128,64},{160,96},{192,128},{224,1... | collective-permute-start | bytes 1179656 | tf_op jit(solution)/shard_map/ppermute | solution.py:392
  41.5 5.8 %collective-permute-done.1 = bf16[128,1536]{1,0:T(8,128)(2,1)S(1)} collective-permute-done((bf16[128,1536]{1,0:T(8,128)(2,1)S(1)}, bf16[128,1536]{1,0:T(8,128)(2,1)S(1)}, u32[]{:S(2)}, u32[]{:S(2)}) %collective-permute-start.1) | collective-permute-done | bytes 393248 | tf_op jit(solution)/shard_map/ppermute | solution.py:392
  47.3 1.9 collective-permute-start.2
  49.3 5.1 %collective-permute-start.6 = (bf16[128,1536]{1,0:T(8,128)(2,1)S(1)}, bf16[128,1536]{1,0:T(8,128)(2,1)S(1)}, u32[]{:S(2)}, u32[]{:S(2)}) collective-permute-start(bf16[128,1536]{1,0:T(8,128)(2,1)S(1)} %collective-permute-done.5), channel_id=1, source_target_pairs={{0,448},{32,480},{64,0},{96,32},{128,64},{160,96},{192,128},{224,1... | collective-permute-start | bytes 1179656 | tf_op jit(solution)/shard_map/ppermute | solution.py:392
  54.4 4.9 %collective-permute-done.2 = bf16[128,1536]{1,0:T(8,128)(2,1)S(1)} collective-permute-done((bf16[128,1536]{1,0:T(8,128)(2,1)S(1)}, bf16[128,1536]{1,0:T(8,128)(2,1)S(1)}, u32[]{:S(2)}, u32[]{:S(2)}) %collective-permute-start.2) | collective-permute-done | bytes 393248 | tf_op jit(solution)/shard_map/ppermute | solution.py:392
  59.3 1.9 collective-permute-start.3
  61.3 9.1 %collective-permute-done.3 = bf16[128,1536]{1,0:T(8,128)(2,1)S(1)} collective-permute-done((bf16[128,1536]{1,0:T(8,128)(2,1)S(1)}, bf16[128,1536]{1,0:T(8,128)(2,1)S(1)}, u32[]{:S(2)}, u32[]{:S(2)}) %collective-permute-start.3) | collective-permute-done | bytes 393248 | tf_op jit(solution)/shard_map/ppermute | solution.py:392
  70.5 1.9 collective-permute-start.7
  72.5 0.9 shard_map.111
  73.4 1.2 copy-done.1
  74.6 9.8 %all-to-all-start.1 = ((bf16[32,8,3072]{2,1,0:T(8,128)(2,1)}), bf16[32,8,3072]{2,1,0:T(8,128)(2,1)}, u32[]{:S(2)}, u32[]{:S(2)}) async-start(bf16[32,8,3072]{2,1,0:T(8,128)(2,1)} %bitcast.18), calls=%async_computation.1 | async-start | bytes 3145728 | tf_op jit(solution)/shard_map/all_to_all | solution.py:373
  84.5 6.0 %shard_map.112 = (bf16[256,3072]{1,0:T(8,128)(2,1)S(1)}, bf16[384,2048]{1,0:T(8,128)(2,1)S(1)}, f32[384,512]{1,0:T(8,128)S(1)}, f32[384,512]{1,0:T(8,128)S(1)}) custom-call(s32[2]{0:T(128)S(1)} %pad_add_fusion.place_ref, bf16[256,3072]{1,0:T(8,128)(2,1)} %bitcast.3.got_ref, bf16[1024,1536]{1,0:T(8,128)(2,1)S(1)} %constant_dynamic-update-slice_fusion.mine_ref, ...), custom_call_target="tpu_custom_call" | custom-call | flops 2415919104 | bytes 12582920 | tf_op jit(solution)/shard_map/pallas_call | solution.py:349
  90.5 1.2 copy-done.2
  91.7 1.1 copy-done.3
  92.8 0.9 copy-done.4
  93.7 0.9 copy-done.5
  94.6 27.5 %all-to-all-done.1 = bf16[32,8,3072]{2,1,0:T(8,128)(2,1)} async-done(((bf16[32,8,3072]{2,1,0:T(8,128)(2,1)}), bf16[32,8,3072]{2,1,0:T(8,128)(2,1)}, u32[]{:S(2)}, u32[]{:S(2)}) %all-to-all-start.1) | async-done | bytes 1572896 | tf_op jit(solution)/shard_map/all_to_all | solution.py:373
  122.1 8.1 %all-to-all-start.2 = ((bf16[32,8,3072]{2,1,0:T(8,128)(2,1)}), bf16[32,8,3072]{2,1,0:T(8,128)(2,1)S(1)}, u32[]{:S(2)}, u32[]{:S(2)}) async-start(bf16[32,8,3072]{2,1,0:T(8,128)(2,1)} %bitcast.20), calls=%async_computation.2 | async-start | bytes 3145728 | tf_op jit(solution)/shard_map/all_to_all | solution.py:373
  130.3 8.8 %shard_map.113 = (bf16[384,1024]{1,0:T(8,128)(2,1)}, bf16[1024,1024]{1,0:T(8,128)(2,1)}, bf16[1024,1024]{1,0:T(8,128)(2,1)}) custom-call(s32[2]{0:T(128)} %copy-done.11, bf16[256,3072]{1,0:T(8,128)(2,1)} %bitcast.5.got_ref, bf16[1024,1536]{1,0:T(8,128)(2,1)} %copy-done, bf16[1024,1536]{1,0:T(8,128)(2,1)} %collective-permute-done.7.other_ref, ...), custom_call_target="tpu_custom_call" | custom-call | flops 2415919104 | bytes 15990792 | tf_op jit(solution)/shard_map/pallas_call | solution.py:349
  139.1 1.9 collective-permute-start.8
  141.0 4.3 %collective-permute-done.8 = bf16[1024,1024]{1,0:T(8,128)(2,1)S(1)} collective-permute-done((bf16[1024,1024]{1,0:T(8,128)(2,1)}, bf16[1024,1024]{1,0:T(8,128)(2,1)S(1)}, u32[]{:S(2)}, u32[]{:S(2)}) %collective-permute-start.8) | collective-permute-done | bytes 2097184 | tf_op jit(solution)/shard_map/ppermute | solution.py:447
  145.4 2.6 %add_convert_fusion = bf16[1024,1024]{1,0:T(8,128)(2,1)S(1)} fusion(bf16[1024,1024]{1,0:T(8,128)(2,1)S(1)} %collective-permute-done.8, bf16[1024,1024]{1,0:T(8,128)(2,1)} %get-tuple-element.44), kind=kLoop, calls=%fused_computation | loop fusion | flops 4194304 | bytes 6291456 | tf_op jit(solution)/shard_map/convert_element_type | solution.py:448
  147.9 1.4 copy-done.13
  149.3 1.1 fusion
  150.4 1.9 collective-permute-start.11
  152.3 5.9 %collective-permute-start.13 = (bf16[128,1024]{1,0:T(8,128)(2,1)S(1)}, bf16[128,1024]{1,0:T(8,128)(2,1)S(1)}, u32[]{:S(2)}, u32[]{:S(2)}) collective-permute-start(bf16[128,1024]{1,0:T(8,128)(2,1)S(1)} %get-tuple-element.63), channel_id=1, source_target_pairs={{0,192},{32,224},{64,256},{96,288},{128,320},{160,352},{192,384},{... | collective-permute-start | bytes 786440 | tf_op jit(solution)/shard_map/ppermute | solution.py:392
  158.2 6.6 %shard_map.114 = bf16[256,3072]{1,0:T(8,128)(2,1)} custom-call(s32[2]{0:T(128)} %copy-done.11, bf16[384,1024]{1,0:T(8,128)(2,1)} %get-tuple-element.43.pre_ref, bf16[1024,1536]{1,0:T(8,128)(2,1)} %copy-done, bf16[1024,1536]{1,0:T(8,128)(2,1)} %collective-permute-done.7.other_ref), custom_call_target="tpu_custom_call" | custom-call | flops 1610612736 | bytes 8650760 | tf_op jit(solution)/shard_map/pallas_call | solution.py:349
  164.9 4.2 %collective-permute-start.12 = (bf16[128,1024]{1,0:T(8,128)(2,1)}, bf16[128,1024]{1,0:T(8,128)(2,1)}, u32[]{:S(2)}, u32[]{:S(2)}) collective-permute-start(bf16[128,1024]{1,0:T(8,128)(2,1)} %get-tuple-element.64), channel_id=1, source_target_pairs={{0,256},{32,288},{64,320},{96,352},{128,384},{160,416},{192,448},{... | collective-permute-start | bytes 786440 | tf_op jit(solution)/shard_map/ppermute | solution.py:392
  169.2 9.8 %all-to-all-start.3 = ((bf16[32,8,3072]{2,1,0:T(8,128)(2,1)}), bf16[32,8,3072]{2,1,0:T(8,128)(2,1)}, u32[]{:S(2)}, u32[]{:S(2)}) async-start(bf16[32,8,3072]{2,1,0:T(8,128)(2,1)} %bitcast.27), calls=%async_computation.3 | async-start | bytes 3145728 | tf_op jit(solution)/shard_map/all_to_all | solution.py:373
  179.0 2.7 %collective-permute-start.9 = (bf16[128,1024]{1,0:T(8,128)(2,1)}, bf16[128,1024]{1,0:T(8,128)(2,1)}, u32[]{:S(2)}, u32[]{:S(2)}) collective-permute-start(bf16[128,1024]{1,0:T(8,128)(2,1)} %get-tuple-element.48), channel_id=1, source_target_pairs={{0,448},{32,480},{64,0},{96,32},{128,64},{160,96},{192,128},{224,1... | collective-permute-start | bytes 786440 | tf_op jit(solution)/shard_map/ppermute | solution.py:392
  181.7 4.3 %collective-permute-start.10 = (bf16[128,1024]{1,0:T(8,128)(2,1)}, bf16[128,1024]{1,0:T(8,128)(2,1)}, u32[]{:S(2)}, u32[]{:S(2)}) collective-permute-start(bf16[128,1024]{1,0:T(8,128)(2,1)} %get-tuple-element.49), channel_id=1, source_target_pairs={{0,384},{32,416},{64,448},{96,480},{128,0},{160,32},{192,64},{224,... | collective-permute-start | bytes 786440 | tf_op jit(solution)/shard_map/ppermute | solution.py:392
  186.0 2.4 %collective-permute-start.14 = (bf16[128,1024]{1,0:T(8,128)(2,1)}, bf16[128,1024]{1,0:T(8,128)(2,1)}, u32[]{:S(2)}, u32[]{:S(2)}) collective-permute-start(bf16[128,1024]{1,0:T(8,128)(2,1)} %get-tuple-element.50), channel_id=1, source_target_pairs={{0,128},{32,160},{64,192},{96,224},{128,256},{160,288},{192,320},{... | collective-permute-start | bytes 786440 | tf_op jit(solution)/shard_map/ppermute | solution.py:392
  188.5 3.2 %collective-permute-start.15 = (bf16[128,1024]{1,0:T(8,128)(2,1)}, bf16[128,1024]{1,0:T(8,128)(2,1)}, u32[]{:S(2)}, u32[]{:S(2)}) collective-permute-start(bf16[128,1024]{1,0:T(8,128)(2,1)} %get-tuple-element.51), channel_id=1, source_target_pairs={{0,64},{32,96},{64,128},{96,160},{128,192},{160,224},{192,256},{22... | collective-permute-start | bytes 786440 | tf_op jit(solution)/shard_map/ppermute | solution.py:392
  191.7 1.9 shard_map.115
  194.2 7.0 %collective-permute-done.10 = bf16[128,1024]{1,0:T(8,128)(2,1)} collective-permute-done((bf16[128,1024]{1,0:T(8,128)(2,1)}, bf16[128,1024]{1,0:T(8,128)(2,1)}, u32[]{:S(2)}, u32[]{:S(2)}) %collective-permute-start.10) | collective-permute-done | bytes 262176 | tf_op jit(solution)/shard_map/ppermute | solution.py:392
  201.2 2.7 %collective-permute-done.14 = bf16[128,1024]{1,0:T(8,128)(2,1)} collective-permute-done((bf16[128,1024]{1,0:T(8,128)(2,1)}, bf16[128,1024]{1,0:T(8,128)(2,1)}, u32[]{:S(2)}, u32[]{:S(2)}) %collective-permute-start.14) | collective-permute-done | bytes 262176 | tf_op jit(solution)/shard_map/ppermute | solution.py:392
  203.9 2.0 collective-permute-done.15
  205.9 1.8 add_bitcast_fusion
  207.7 0.8 fusion.1
  208.6 7.1 %all-to-all-done.3 = bf16[32,8,3072]{2,1,0:T(8,128)(2,1)} async-done(((bf16[32,8,3072]{2,1,0:T(8,128)(2,1)}), bf16[32,8,3072]{2,1,0:T(8,128)(2,1)}, u32[]{:S(2)}, u32[]{:S(2)}) %all-to-all-start.3) | async-done | bytes 1572896 | tf_op jit(solution)/shard_map/all_to_all | solution.py:373
  215.7 2.9 %shard_map.116 = bf16[128,2048]{1,0:T(8,128)(2,1)} custom-call(s32[2,128]{1,0:T(2,128)S(1)} %bitcast.24, bf16[256,3072]{1,0:T(8,128)(2,1)} %bitcast.13.got_ref), custom_call_target="tpu_custom_call" | custom-call | flops 268435456 | bytes 2098176 | tf_op jit(solution)/shard_map/pallas_call | solution.py:349
  (52 shorter events, 1.7 us)
Async XLA Ops:
  0.6 1.0 copy-start.8
  1.7 0.7 copy-start.9
  2.4 12.4 %copy-start.14 = (bf16[1,128,512]{2,1,0:T(8,128)(2,1)S(1)}, bf16[1,128,512]{2,1,0:T(8,128)(2,1)}, u32[]{:S(2)}) copy-start(bf16[1,128,512]{2,1,0:T(8,128)(2,1)} %param.12) | copy-start | bytes 393220
  2.4 12.4 %copy-start.15 = (bf16[1,128,512]{2,1,0:T(8,128)(2,1)S(1)}, bf16[1,128,512]{2,1,0:T(8,128)(2,1)}, u32[]{:S(2)}) copy-start(bf16[1,128,512]{2,1,0:T(8,128)(2,1)} %param.11) | copy-start | bytes 393220
  2.4 12.4 %copy-start.16 = (bf16[1,128,512]{2,1,0:T(8,128)(2,1)S(1)}, bf16[1,128,512]{2,1,0:T(8,128)(2,1)}, u32[]{:S(2)}) copy-start(bf16[1,128,512]{2,1,0:T(8,128)(2,1)} %param.10) | copy-start | bytes 393220
  4.4 70.2 %all-to-all-start = ((bf16[32,8,3072]{2,1,0:T(8,128)(2,1)}), bf16[32,8,3072]{2,1,0:T(8,128)(2,1)}, u32[]{:S(2)}, u32[]{:S(2)}) async-start(bf16[32,8,3072]{2,1,0:T(8,128)(2,1)} %bitcast.2), calls=%async_computation | async-start | bytes 3145728 | tf_op jit(solution)/shard_map/all_to_all | solution.py:373
  14.8 57.7 %copy-start.6 = (bf16[128,2048]{1,0:T(8,128)(2,1)S(1)}, bf16[128,2048]{1,0:T(8,128)(2,1)}, u32[]{:S(2)}) copy-start(bf16[128,2048]{1,0:T(8,128)(2,1)} %grad_ref.1) | copy-start | bytes 1572868
  14.8 57.7 %copy-start.10 = (s32[128,2]{0,1:T(2,128)S(1)}, s32[128,2]{0,1:T(2,128)}, u32[]{:S(2)}) copy-start(s32[128,2]{0,1:T(2,128)} %param.9) | copy-start | bytes 3076
  14.8 57.7 %copy-start.12 = (f32[128,2]{0,1:T(2,128)S(1)}, f32[128,2]{0,1:T(2,128)}, u32[]{:S(2)}) copy-start(f32[128,2]{0,1:T(2,128)} %param.8) | copy-start | bytes 3076
  14.8 19.6 %collective-permute-start = (bf16[128,1536]{1,0:T(8,128)(2,1)S(1)}, bf16[128,1536]{1,0:T(8,128)(2,1)S(1)}, u32[]{:S(2)}, u32[]{:S(2)}) collective-permute-start(bf16[128,1536]{1,0:T(8,128)(2,1)S(1)} %maximum_bitcast_fusion), channel_id=1, source_target_pairs={{0,64},{32,96},{64,128},{96,160},{128,192},{160,224},{192,256},{22... | collective-permute-start | bytes 1179656 | tf_op jit(solution)/shard_map/ppermute | solution.py:392
  19.2 17.1 %collective-permute-start.4 = (bf16[128,1536]{1,0:T(8,128)(2,1)S(1)}, bf16[128,1536]{1,0:T(8,128)(2,1)S(1)}, u32[]{:S(2)}, u32[]{:S(2)}) collective-permute-start(bf16[128,1536]{1,0:T(8,128)(2,1)S(1)} %maximum_bitcast_fusion), channel_id=1, source_target_pairs={{0,448},{32,480},{64,0},{96,32},{128,64},{160,96},{192,128},{224,1... | collective-permute-start | bytes 1179656 | tf_op jit(solution)/shard_map/ppermute | solution.py:392
  34.4 12.8 %collective-permute-start.1 = (bf16[128,1536]{1,0:T(8,128)(2,1)S(1)}, bf16[128,1536]{1,0:T(8,128)(2,1)S(1)}, u32[]{:S(2)}, u32[]{:S(2)}) collective-permute-start(bf16[128,1536]{1,0:T(8,128)(2,1)S(1)} %collective-permute-done), channel_id=1, source_target_pairs={{0,64},{32,96},{64,128},{96,160},{128,192},{160,224},{192,256},{22... | collective-permute-start | bytes 1179656 | tf_op jit(solution)/shard_map/ppermute | solution.py:392
  36.3 12.9 %collective-permute-start.5 = (bf16[128,1536]{1,0:T(8,128)(2,1)S(1)}, bf16[128,1536]{1,0:T(8,128)(2,1)S(1)}, u32[]{:S(2)}, u32[]{:S(2)}) collective-permute-start(bf16[128,1536]{1,0:T(8,128)(2,1)S(1)} %collective-permute-done.4), channel_id=1, source_target_pairs={{0,448},{32,480},{64,0},{96,32},{128,64},{160,96},{192,128},{224,1... | collective-permute-start | bytes 1179656 | tf_op jit(solution)/shard_map/ppermute | solution.py:392
  47.3 12.0 %collective-permute-start.2 = (bf16[128,1536]{1,0:T(8,128)(2,1)S(1)}, bf16[128,1536]{1,0:T(8,128)(2,1)S(1)}, u32[]{:S(2)}, u32[]{:S(2)}) collective-permute-start(bf16[128,1536]{1,0:T(8,128)(2,1)S(1)} %collective-permute-done.1), channel_id=1, source_target_pairs={{0,64},{32,96},{64,128},{96,160},{128,192},{160,224},{192,256},{22... | collective-permute-start | bytes 1179656 | tf_op jit(solution)/shard_map/ppermute | solution.py:392
  49.3 21.2 %collective-permute-start.6 = (bf16[128,1536]{1,0:T(8,128)(2,1)S(1)}, bf16[128,1536]{1,0:T(8,128)(2,1)S(1)}, u32[]{:S(2)}, u32[]{:S(2)}) collective-permute-start(bf16[128,1536]{1,0:T(8,128)(2,1)S(1)} %collective-permute-done.5), channel_id=1, source_target_pairs={{0,448},{32,480},{64,0},{96,32},{128,64},{160,96},{192,128},{224,1... | collective-permute-start | bytes 1179656 | tf_op jit(solution)/shard_map/ppermute | solution.py:392
  59.3 11.1 %collective-permute-start.3 = (bf16[128,1536]{1,0:T(8,128)(2,1)S(1)}, bf16[128,1536]{1,0:T(8,128)(2,1)S(1)}, u32[]{:S(2)}, u32[]{:S(2)}) collective-permute-start(bf16[128,1536]{1,0:T(8,128)(2,1)S(1)} %collective-permute-done.2), channel_id=1, source_target_pairs={{0,64},{32,96},{64,128},{96,160},{128,192},{160,224},{192,256},{22... | collective-permute-start | bytes 1179656 | tf_op jit(solution)/shard_map/ppermute | solution.py:392
  70.5 20.0 %copy-start = (bf16[1024,1536]{1,0:T(8,128)(2,1)}, bf16[1024,1536]{1,0:T(8,128)(2,1)S(1)}, u32[]{:S(2)}) copy-start(bf16[1024,1536]{1,0:T(8,128)(2,1)S(1)} %constant_dynamic-update-slice_fusion.mine_ref) | copy-start | bytes 9437188
  70.5 14.0 %collective-permute-start.7 = (bf16[1024,1536]{1,0:T(8,128)(2,1)S(1)}, bf16[1024,1536]{1,0:T(8,128)(2,1)}, u32[]{:S(2)}, u32[]{:S(2)}) collective-permute-start(bf16[1024,1536]{1,0:T(8,128)(2,1)S(1)} %constant_dynamic-update-slice_fusion.mine_ref), channel_id=1, source_target_pairs={{0,32},{32,0},{64,96},{96,64},{128,160},{160,128},{192,224},{224,1... | collective-permute-start | bytes 9437192 | tf_op jit(solution)/shard_map/ppermute | solution.py:401
  73.4 1.2 copy-start.1
  74.6 47.5 %all-to-all-start.1 = ((bf16[32,8,3072]{2,1,0:T(8,128)(2,1)}), bf16[32,8,3072]{2,1,0:T(8,128)(2,1)}, u32[]{:S(2)}, u32[]{:S(2)}) async-start(bf16[32,8,3072]{2,1,0:T(8,128)(2,1)} %bitcast.18), calls=%async_computation.1 | async-start | bytes 3145728 | tf_op jit(solution)/shard_map/all_to_all | solution.py:373
  84.5 6.0 %copy-start.11 = (s32[2]{0:T(128)}, s32[2]{0:T(128)S(1)}, u32[]{:S(2)}) copy-start(s32[2]{0:T(128)S(1)} %pad_add_fusion.place_ref) | copy-start | bytes 28
  90.5 1.2 copy-start.2
  91.7 1.1 copy-start.3
  92.8 0.9 copy-start.4
  93.7 0.9 copy-start.5
  122.1 47.0 %all-to-all-start.2 = ((bf16[32,8,3072]{2,1,0:T(8,128)(2,1)}), bf16[32,8,3072]{2,1,0:T(8,128)(2,1)S(1)}, u32[]{:S(2)}, u32[]{:S(2)}) async-start(bf16[32,8,3072]{2,1,0:T(8,128)(2,1)} %bitcast.20), calls=%async_computation.2 | async-start | bytes 3145728 | tf_op jit(solution)/shard_map/all_to_all | solution.py:373
  139.1 6.3 %collective-permute-start.8 = (bf16[1024,1024]{1,0:T(8,128)(2,1)}, bf16[1024,1024]{1,0:T(8,128)(2,1)S(1)}, u32[]{:S(2)}, u32[]{:S(2)}) collective-permute-start(bf16[1024,1024]{1,0:T(8,128)(2,1)} %get-tuple-element.45), channel_id=1, source_target_pairs={{0,32},{32,0},{64,96},{96,64},{128,160},{160,128},{192,224},{224,1... | collective-permute-start | bytes 6291464 | tf_op jit(solution)/shard_map/ppermute | solution.py:447
  147.9 1.4 copy-start.13
  150.4 35.6 %collective-permute-start.11 = (bf16[128,1024]{1,0:T(8,128)(2,1)S(1)}, bf16[128,1024]{1,0:T(8,128)(2,1)S(1)}, u32[]{:S(2)}, u32[]{:S(2)}) collective-permute-start(bf16[128,1024]{1,0:T(8,128)(2,1)S(1)} %get-tuple-element.62), channel_id=1, source_target_pairs={{0,320},{32,352},{64,384},{96,416},{128,448},{160,480},{192,0},{22... | collective-permute-start | bytes 786440 | tf_op jit(solution)/shard_map/ppermute | solution.py:392
  152.3 36.1 %collective-permute-start.13 = (bf16[128,1024]{1,0:T(8,128)(2,1)S(1)}, bf16[128,1024]{1,0:T(8,128)(2,1)S(1)}, u32[]{:S(2)}, u32[]{:S(2)}) collective-permute-start(bf16[128,1024]{1,0:T(8,128)(2,1)S(1)} %get-tuple-element.63), channel_id=1, source_target_pairs={{0,192},{32,224},{64,256},{96,288},{128,320},{160,352},{192,384},{... | collective-permute-start | bytes 786440 | tf_op jit(solution)/shard_map/ppermute | solution.py:392
  164.9 26.8 %copy-start.7 = (bf16[128,2048]{1,0:T(8,128)(2,1)S(1)}, bf16[128,2048]{1,0:T(8,128)(2,1)}, u32[]{:S(2)}) copy-start(bf16[128,2048]{1,0:T(8,128)(2,1)} %grad_ref.1) | copy-start | bytes 1572868
  164.9 29.3 %collective-permute-start.12 = (bf16[128,1024]{1,0:T(8,128)(2,1)}, bf16[128,1024]{1,0:T(8,128)(2,1)}, u32[]{:S(2)}, u32[]{:S(2)}) collective-permute-start(bf16[128,1024]{1,0:T(8,128)(2,1)} %get-tuple-element.64), channel_id=1, source_target_pairs={{0,256},{32,288},{64,320},{96,352},{128,384},{160,416},{192,448},{... | collective-permute-start | bytes 786440 | tf_op jit(solution)/shard_map/ppermute | solution.py:392
  169.2 46.6 %all-to-all-start.3 = ((bf16[32,8,3072]{2,1,0:T(8,128)(2,1)}), bf16[32,8,3072]{2,1,0:T(8,128)(2,1)}, u32[]{:S(2)}, u32[]{:S(2)}) async-start(bf16[32,8,3072]{2,1,0:T(8,128)(2,1)} %bitcast.27), calls=%async_computation.3 | async-start | bytes 3145728 | tf_op jit(solution)/shard_map/all_to_all | solution.py:373
  179.0 15.2 %collective-permute-start.9 = (bf16[128,1024]{1,0:T(8,128)(2,1)}, bf16[128,1024]{1,0:T(8,128)(2,1)}, u32[]{:S(2)}, u32[]{:S(2)}) collective-permute-start(bf16[128,1024]{1,0:T(8,128)(2,1)} %get-tuple-element.48), channel_id=1, source_target_pairs={{0,448},{32,480},{64,0},{96,32},{128,64},{160,96},{192,128},{224,1... | collective-permute-start | bytes 786440 | tf_op jit(solution)/shard_map/ppermute | solution.py:392
  181.7 19.5 %collective-permute-start.10 = (bf16[128,1024]{1,0:T(8,128)(2,1)}, bf16[128,1024]{1,0:T(8,128)(2,1)}, u32[]{:S(2)}, u32[]{:S(2)}) collective-permute-start(bf16[128,1024]{1,0:T(8,128)(2,1)} %get-tuple-element.49), channel_id=1, source_target_pairs={{0,384},{32,416},{64,448},{96,480},{128,0},{160,32},{192,64},{224,... | collective-permute-start | bytes 786440 | tf_op jit(solution)/shard_map/ppermute | solution.py:392
  186.0 7.6 %copy-start.17 = (bf16[128,1024]{1,0:T(8,128)(2,1)}, bf16[128,1024]{1,0:T(8,128)(2,1)S(1)}, u32[]{:S(2)}) copy-start(bf16[128,1024]{1,0:T(8,128)(2,1)S(1)} %collective-permute-done.11) | copy-start | bytes 786436
  186.0 17.9 %collective-permute-start.14 = (bf16[128,1024]{1,0:T(8,128)(2,1)}, bf16[128,1024]{1,0:T(8,128)(2,1)}, u32[]{:S(2)}, u32[]{:S(2)}) collective-permute-start(bf16[128,1024]{1,0:T(8,128)(2,1)} %get-tuple-element.50), channel_id=1, source_target_pairs={{0,128},{32,160},{64,192},{96,224},{128,256},{160,288},{192,320},{... | collective-permute-start | bytes 786440 | tf_op jit(solution)/shard_map/ppermute | solution.py:392
  188.5 5.1 %copy-start.18 = (bf16[128,1024]{1,0:T(8,128)(2,1)}, bf16[128,1024]{1,0:T(8,128)(2,1)S(1)}, u32[]{:S(2)}) copy-start(bf16[128,1024]{1,0:T(8,128)(2,1)S(1)} %collective-permute-done.13) | copy-start | bytes 786436
  188.5 17.4 %collective-permute-start.15 = (bf16[128,1024]{1,0:T(8,128)(2,1)}, bf16[128,1024]{1,0:T(8,128)(2,1)}, u32[]{:S(2)}, u32[]{:S(2)}) collective-permute-start(bf16[128,1024]{1,0:T(8,128)(2,1)} %get-tuple-element.51), channel_id=1, source_target_pairs={{0,64},{32,96},{64,128},{96,160},{128,192},{160,224},{192,256},{22... | collective-permute-start | bytes 786440 | tf_op jit(solution)/shard_map/ppermute | solution.py:392

commit v6 on v5

--- a/solution.py
+++ b/solution.py
@@ -398,7 +398,7 @@
     for k in range(chips - 1, chips // 2, -1):
         came[k] = along(came[(k + 1) % chips], -1)
     mine = jnp.concatenate([came[k] for k in range(chips)], axis=0)
-    other = lax.ppermute(mine, "dp", swap)
+    other = jnp.concatenate([lax.ppermute(came[k], "dp", swap) for k in range(chips)], axis=0)
     (send_grad,) = call(pack_grads, [(send, BF)], [], pack_flops, experts_t, gates_t, out_grad)
     got_tok = exchange(send_tok)
     got_tok, send_grad = lax.optimization_barrier((got_tok, send_grad))

time: 222 us -> 211 us (0.950)
  waiting for transfers between devices: 77.1 us -> 33.2 us
  starting transfers between devices: 95.6 us -> 112 us
  local copies, waits for them, and re-layouts: 11.2 us -> 25.7 us
    all_to_all x4, waiting for transfers between devices: 34.6 us -> 4.57 us  [exchange(): lax.all_to_all(rows.reshape(count, 8, send[1]), 'expert', split_axis=0, c...]
    ppermute x1 -> x8, starting transfers between devices: 1.92 us -> 16 us  [on_device(): lax.ppermute(came[k], 'dp', swap)]
    ppermute x14, waiting for transfers between devices: 38.1 us -> 24.2 us  [along(): return lax.ppermute(rows, 'dp', pairs)]
    unnamed x45 -> x52, local copies, waits for them, and re-layouts: 9.23 us -> 22 us
  transfers between devices with their start and end apart: 20 -> 27, of which waited for: 10 -> 10; matrix products, arithmetic and copies ran while one was open for 3% -> 11% of each run, Pallas kernels for 11% -> 12%
where the time goes in v6:
time: 211 us; the launch traced here: 208 us
  starting transfers between devices  112 us (53%)
  waiting for transfers between devices  33.2 us (16%)
  Pallas kernels  30.4 us (14%)
  local copies, waits for them, and re-layouts  25.7 us (12%)
  other arithmetic  5.25 us (2%)
    ppermute x14, starting transfers between devices, along(): return lax.ppermute(rows, 'dp', pairs)  54.1 us
    all_to_all x4, starting transfers between devices, exchange(): lax.all_to_all(rows.reshape(count, 8, send[1]), 'expert', split_axis=0, c...  39.8 us
    pallas_call x7, Pallas kernels, call(): pl.pallas_call(body, out_shape=[jax.ShapeDtypeStruct(s, d) for s, d in ou...  30.4 us
    ppermute x14, waiting for transfers between devices, along(): return lax.ppermute(rows, 'dp', pairs)  24.2 us
    unnamed x52, local copies, waits for them, and re-layouts  22 us
    ppermute x8, starting transfers between devices, on_device(): lax.ppermute(came[k], 'dp', swap)  16 us
    all_to_all x4, waiting for transfers between devices, exchange(): lax.all_to_all(rows.reshape(count, 8, send[1]), 'expert', split_axis=0, c...  4.57 us
    ppermute x1, waiting for transfers between devices, on_device(): taken = lax.ppermute(give, 'dp', swap)  4.34 us
  transfers between devices with their start and end apart: 27, of which 10 were waited for; matrix products, arithmetic and copies ran while one was open for 11% of the time, Pallas kernels for 12%

profile of v6, /device:TPU:6, one launch (start us, length us, event | category | flops | bytes accessed | tf_op | source)
XLA Modules:
  0.0 207.6 jit_solution(3048945056467567471)
XLA Ops:
  2.4 2.1 shard_map.110
  4.5 10.3 %all-to-all-start = ((bf16[32,8,3072]{2,1,0:T(8,128)(2,1)}), bf16[32,8,3072]{2,1,0:T(8,128)(2,1)}, u32[]{:S(2)}, u32[]{:S(2)}) async-start(bf16[32,8,3072]{2,1,0:T(8,128)(2,1)} %bitcast.2), calls=%async_computation | async-start | bytes 3145728 | tf_op jit(solution)/shard_map/all_to_all | solution.py:373
  14.9 10.9 %collective-permute-start.4 = (bf16[128,1536]{1,0:T(8,128)(2,1)S(1)}, bf16[128,1536]{1,0:T(8,128)(2,1)S(1)}, u32[]{:S(2)}, u32[]{:S(2)}) collective-permute-start(bf16[128,1536]{1,0:T(8,128)(2,1)S(1)} %maximum_bitcast_fusion), channel_id=1, source_target_pairs={{0,448},{32,480},{64,0},{96,32},{128,64},{160,96},{192,128},{224,1... | collective-permute-start | bytes 1179656 | tf_op jit(solution)/shard_map/ppermute | solution.py:392
  25.8 1.9 collective-permute-start
  27.7 1.9 collective-permute-start.7
  33.6 1.9 collective-permute-start.14
  35.5 5.6 %collective-permute-start.5 = (bf16[128,1536]{1,0:T(8,128)(2,1)S(1)}, bf16[128,1536]{1,0:T(8,128)(2,1)}, u32[]{:S(2)}, u32[]{:S(2)}) collective-permute-start(bf16[128,1536]{1,0:T(8,128)(2,1)S(1)} %collective-permute-done.4), channel_id=1, source_target_pairs={{0,448},{32,480},{64,0},{96,32},{128,64},{160,96},{192,128},{224,1... | collective-permute-start | bytes 1179656 | tf_op jit(solution)/shard_map/ppermute | solution.py:392
  41.1 2.1 %collective-permute-start.8 = (bf16[128,1536]{1,0:T(8,128)(2,1)}, bf16[128,1536]{1,0:T(8,128)(2,1)}, u32[]{:S(2)}, u32[]{:S(2)}) collective-permute-start(bf16[128,1536]{1,0:T(8,128)(2,1)} %collective-permute-done), channel_id=1, source_target_pairs={{0,32},{32,0},{64,96},{96,64},{128,160},{160,128},{192,224},{224,1... | collective-permute-start | bytes 1179656 | tf_op jit(solution)/shard_map/ppermute | solution.py:401
  43.3 1.9 collective-permute-start.1
  46.2 1.8 constant_dynamic-update-slice_fusion.6
  48.0 2.1 %collective-permute-done.5 = bf16[128,1536]{1,0:T(8,128)(2,1)} collective-permute-done((bf16[128,1536]{1,0:T(8,128)(2,1)S(1)}, bf16[128,1536]{1,0:T(8,128)(2,1)}, u32[]{:S(2)}, u32[]{:S(2)}) %collective-permute-start.5) | collective-permute-done | bytes 393248 | tf_op jit(solution)/shard_map/ppermute | solution.py:392
  50.1 1.9 collective-permute-start.13
  52.1 5.7 %collective-permute-start.6 = (bf16[128,1536]{1,0:T(8,128)(2,1)}, bf16[128,1536]{1,0:T(8,128)(2,1)}, u32[]{:S(2)}, u32[]{:S(2)}) collective-permute-start(bf16[128,1536]{1,0:T(8,128)(2,1)} %collective-permute-done.5), channel_id=1, source_target_pairs={{0,448},{32,480},{64,0},{96,32},{128,64},{160,96},{192,128},{224,1... | collective-permute-start | bytes 1179656 | tf_op jit(solution)/shard_map/ppermute | solution.py:392
  58.0 1.9 collective-permute-start.2
  59.9 1.8 constant_dynamic-update-slice_fusion.5
  61.7 9.8 %all-to-all-start.1 = ((bf16[32,8,3072]{2,1,0:T(8,128)(2,1)}), bf16[32,8,3072]{2,1,0:T(8,128)(2,1)}, u32[]{:S(2)}, u32[]{:S(2)}) async-start(bf16[32,8,3072]{2,1,0:T(8,128)(2,1)} %bitcast.18), calls=%async_computation.1 | async-start | bytes 3145728 | tf_op jit(solution)/shard_map/all_to_all | solution.py:373
  71.6 1.9 collective-permute-start.9
  74.6 1.9 collective-permute-start.3
  76.5 1.8 constant_dynamic-update-slice_fusion.4
  78.3 2.4 %collective-permute-start.10 = (bf16[128,1536]{1,0:T(8,128)(2,1)}, bf16[128,1536]{1,0:T(8,128)(2,1)S(1)}, u32[]{:S(2)}, u32[]{:S(2)}) collective-permute-start(bf16[128,1536]{1,0:T(8,128)(2,1)} %collective-permute-done.2), channel_id=1, source_target_pairs={{0,32},{32,0},{64,96},{96,64},{128,160},{160,128},{192,224},{224,1... | collective-permute-start | bytes 1179656 | tf_op jit(solution)/shard_map/ppermute | solution.py:401
  80.7 1.9 collective-permute-start.12
  82.6 7.0 %collective-permute-done.3 = bf16[128,1536]{1,0:T(8,128)(2,1)S(1)} collective-permute-done((bf16[128,1536]{1,0:T(8,128)(2,1)}, bf16[128,1536]{1,0:T(8,128)(2,1)S(1)}, u32[]{:S(2)}, u32[]{:S(2)}) %collective-permute-start.3) | collective-permute-done | bytes 393248 | tf_op jit(solution)/shard_map/ppermute | solution.py:392
  89.7 1.9 collective-permute-start.11
  92.4 1.8 constant_dynamic-update-slice_fusion.2
  94.2 1.8 constant_dynamic-update-slice_fusion.1
  98.9 7.2 %shard_map.112 = (bf16[256,3072]{1,0:T(8,128)(2,1)S(1)}, bf16[384,2048]{1,0:T(8,128)(2,1)S(1)}, f32[384,512]{1,0:T(8,128)S(1)}, f32[384,512]{1,0:T(8,128)S(1)}) custom-call(s32[2]{0:T(128)S(1)} %pad_add_fusion.place_ref, bf16[256,3072]{1,0:T(8,128)(2,1)} %bitcast.3.got_ref, bf16[1024,1536]{1,0:T(8,128)(2,1)} %constant_dynamic-update-slice_fusion.mine_ref, ...), custom_call_target="tpu_custom_call" | custom-call | flops 2415919104 | bytes 12582920 | tf_op jit(solution)/shard_map/pallas_call | solution.py:349
  110.2 9.8 %all-to-all-start.2 = ((bf16[32,8,3072]{2,1,0:T(8,128)(2,1)}), bf16[32,8,3072]{2,1,0:T(8,128)(2,1)S(1)}, u32[]{:S(2)}, u32[]{:S(2)}) async-start(bf16[32,8,3072]{2,1,0:T(8,128)(2,1)} %bitcast.20), calls=%async_computation.2 | async-start | bytes 3145728 | tf_op jit(solution)/shard_map/all_to_all | solution.py:373
  120.0 8.9 %shard_map.113 = (bf16[384,1024]{1,0:T(8,128)(2,1)}, bf16[1024,1024]{1,0:T(8,128)(2,1)}, bf16[1024,1024]{1,0:T(8,128)(2,1)}) custom-call(s32[2]{0:T(128)} %copy-done.11, bf16[256,3072]{1,0:T(8,128)(2,1)} %bitcast.5.got_ref, bf16[1024,1536]{1,0:T(8,128)(2,1)} %constant_dynamic-update-slice_fusion.mine_ref, bf16[1024,1536]{1,0:T(8,128)(2,1)} %copy-done, ...), custom_call_target="tpu_custom_call" | custom-call | flops 2415919104 | bytes 15990792 | tf_op jit(solution)/shard_map/pallas_call | solution.py:349
  128.9 1.9 collective-permute-start.15
  130.8 4.3 %collective-permute-done.15 = bf16[1024,1024]{1,0:T(8,128)(2,1)S(1)} collective-permute-done((bf16[1024,1024]{1,0:T(8,128)(2,1)}, bf16[1024,1024]{1,0:T(8,128)(2,1)S(1)}, u32[]{:S(2)}, u32[]{:S(2)}) %collective-permute-start.15) | collective-permute-done | bytes 2097184 | tf_op jit(solution)/shard_map/ppermute | solution.py:447
  135.2 2.6 %add_convert_fusion = bf16[1024,1024]{1,0:T(8,128)(2,1)S(1)} fusion(bf16[1024,1024]{1,0:T(8,128)(2,1)S(1)} %collective-permute-done.15, bf16[1024,1024]{1,0:T(8,128)(2,1)} %get-tuple-element.44), kind=kLoop, calls=%fused_computation | loop fusion | flops 4194304 | bytes 6291456 | tf_op jit(solution)/shard_map/convert_element_type | solution.py:448
  137.7 1.4 copy-done.13
  140.2 1.9 collective-permute-start.18
  142.1 5.9 %collective-permute-start.20 = (bf16[128,1024]{1,0:T(8,128)(2,1)S(1)}, bf16[128,1024]{1,0:T(8,128)(2,1)S(1)}, u32[]{:S(2)}, u32[]{:S(2)}) collective-permute-start(bf16[128,1024]{1,0:T(8,128)(2,1)S(1)} %get-tuple-element.63), channel_id=1, source_target_pairs={{0,192},{32,224},{64,256},{96,288},{128,320},{160,352},{192,384},{... | collective-permute-start | bytes 786440 | tf_op jit(solution)/shard_map/ppermute | solution.py:392
  148.0 6.6 %shard_map.114 = bf16[256,3072]{1,0:T(8,128)(2,1)} custom-call(s32[2]{0:T(128)} %copy-done.11, bf16[384,1024]{1,0:T(8,128)(2,1)} %get-tuple-element.43.pre_ref, bf16[1024,1536]{1,0:T(8,128)(2,1)} %constant_dynamic-update-slice_fusion.mine_ref, bf16[1024,1536]{1,0:T(8,128)(2,1)} %copy-done), custom_call_target="tpu_custom_call" | custom-call | flops 1610612736 | bytes 8650760 | tf_op jit(solution)/shard_map/pallas_call | solution.py:349
  154.6 3.2 %collective-permute-start.19 = (bf16[128,1024]{1,0:T(8,128)(2,1)}, bf16[128,1024]{1,0:T(8,128)(2,1)}, u32[]{:S(2)}, u32[]{:S(2)}) collective-permute-start(bf16[128,1024]{1,0:T(8,128)(2,1)} %get-tuple-element.64), channel_id=1, source_target_pairs={{0,256},{32,288},{64,320},{96,352},{128,384},{160,416},{192,448},{... | collective-permute-start | bytes 786440 | tf_op jit(solution)/shard_map/ppermute | solution.py:392
  157.9 9.9 %all-to-all-start.3 = ((bf16[32,8,3072]{2,1,0:T(8,128)(2,1)}), bf16[32,8,3072]{2,1,0:T(8,128)(2,1)}, u32[]{:S(2)}, u32[]{:S(2)}) async-start(bf16[32,8,3072]{2,1,0:T(8,128)(2,1)} %bitcast.27), calls=%async_computation.3 | async-start | bytes 3145728 | tf_op jit(solution)/shard_map/all_to_all | solution.py:373
  167.7 3.9 %collective-permute-start.16 = (bf16[128,1024]{1,0:T(8,128)(2,1)}, bf16[128,1024]{1,0:T(8,128)(2,1)}, u32[]{:S(2)}, u32[]{:S(2)}) collective-permute-start(bf16[128,1024]{1,0:T(8,128)(2,1)} %get-tuple-element.48), channel_id=1, source_target_pairs={{0,448},{32,480},{64,0},{96,32},{128,64},{160,96},{192,128},{224,1... | collective-permute-start | bytes 786440 | tf_op jit(solution)/shard_map/ppermute | solution.py:392
  171.7 3.7 %collective-permute-start.17 = (bf16[128,1024]{1,0:T(8,128)(2,1)}, bf16[128,1024]{1,0:T(8,128)(2,1)}, u32[]{:S(2)}, u32[]{:S(2)}) collective-permute-start(bf16[128,1024]{1,0:T(8,128)(2,1)} %get-tuple-element.49), channel_id=1, source_target_pairs={{0,384},{32,416},{64,448},{96,480},{128,0},{160,32},{192,64},{224,... | collective-permute-start | bytes 786440 | tf_op jit(solution)/shard_map/ppermute | solution.py:392
  175.4 3.0 %collective-permute-start.21 = (bf16[128,1024]{1,0:T(8,128)(2,1)}, bf16[128,1024]{1,0:T(8,128)(2,1)}, u32[]{:S(2)}, u32[]{:S(2)}) collective-permute-start(bf16[128,1024]{1,0:T(8,128)(2,1)} %get-tuple-element.50), channel_id=1, source_target_pairs={{0,128},{32,160},{64,192},{96,224},{128,256},{160,288},{192,320},{... | collective-permute-start | bytes 786440 | tf_op jit(solution)/shard_map/ppermute | solution.py:392
  178.5 2.6 %collective-permute-start.22 = (bf16[128,1024]{1,0:T(8,128)(2,1)}, bf16[128,1024]{1,0:T(8,128)(2,1)}, u32[]{:S(2)}, u32[]{:S(2)}) collective-permute-start(bf16[128,1024]{1,0:T(8,128)(2,1)} %get-tuple-element.51), channel_id=1, source_target_pairs={{0,64},{32,96},{64,128},{96,160},{128,192},{160,224},{192,256},{22... | collective-permute-start | bytes 786440 | tf_op jit(solution)/shard_map/ppermute | solution.py:392
  181.0 1.9 shard_map.115
  184.0 7.8 %collective-permute-done.17 = bf16[128,1024]{1,0:T(8,128)(2,1)} collective-permute-done((bf16[128,1024]{1,0:T(8,128)(2,1)}, bf16[128,1024]{1,0:T(8,128)(2,1)}, u32[]{:S(2)}, u32[]{:S(2)}) %collective-permute-start.17) | collective-permute-done | bytes 262176 | tf_op jit(solution)/shard_map/ppermute | solution.py:392
  191.8 2.5 %collective-permute-done.21 = bf16[128,1024]{1,0:T(8,128)(2,1)} collective-permute-done((bf16[128,1024]{1,0:T(8,128)(2,1)}, bf16[128,1024]{1,0:T(8,128)(2,1)}, u32[]{:S(2)}, u32[]{:S(2)}) %collective-permute-start.21) | collective-permute-done | bytes 262176 | tf_op jit(solution)/shard_map/ppermute | solution.py:392
  194.3 3.1 %collective-permute-done.22 = bf16[128,1024]{1,0:T(8,128)(2,1)} collective-permute-done((bf16[128,1024]{1,0:T(8,128)(2,1)}, bf16[128,1024]{1,0:T(8,128)(2,1)}, u32[]{:S(2)}, u32[]{:S(2)}) %collective-permute-start.22) | collective-permute-done | bytes 262176 | tf_op jit(solution)/shard_map/ppermute | solution.py:392
  197.4 1.8 add_bitcast_fusion
  200.1 4.6 %all-to-all-done.3 = bf16[32,8,3072]{2,1,0:T(8,128)(2,1)} async-done(((bf16[32,8,3072]{2,1,0:T(8,128)(2,1)}), bf16[32,8,3072]{2,1,0:T(8,128)(2,1)}, u32[]{:S(2)}, u32[]{:S(2)}) %all-to-all-start.3) | async-done | bytes 1572896 | tf_op jit(solution)/shard_map/all_to_all | solution.py:373
  204.7 2.9 %shard_map.116 = bf16[128,2048]{1,0:T(8,128)(2,1)} custom-call(s32[2,128]{1,0:T(2,128)S(1)} %bitcast.24, bf16[256,3072]{1,0:T(8,128)(2,1)} %bitcast.13.got_ref), custom_call_target="tpu_custom_call" | custom-call | flops 268435456 | bytes 2098176 | tf_op jit(solution)/shard_map/pallas_call | solution.py:349
  (74 shorter events, 18.9 us)
Async XLA Ops:
  0.6 29.1 %copy-start.6 = (bf16[128,2048]{1,0:T(8,128)(2,1)S(1)}, bf16[128,2048]{1,0:T(8,128)(2,1)}, u32[]{:S(2)}) copy-start(bf16[128,2048]{1,0:T(8,128)(2,1)} %grad_ref.1) | copy-start | bytes 1572868
  0.6 1.1 copy-start.8
  1.7 0.7 copy-start.9
  2.4 12.4 %copy-start.14 = (bf16[1,128,512]{2,1,0:T(8,128)(2,1)S(1)}, bf16[1,128,512]{2,1,0:T(8,128)(2,1)}, u32[]{:S(2)}) copy-start(bf16[1,128,512]{2,1,0:T(8,128)(2,1)} %param.12) | copy-start | bytes 393220
  2.4 12.4 %copy-start.15 = (bf16[1,128,512]{2,1,0:T(8,128)(2,1)S(1)}, bf16[1,128,512]{2,1,0:T(8,128)(2,1)}, u32[]{:S(2)}) copy-start(bf16[1,128,512]{2,1,0:T(8,128)(2,1)} %param.11) | copy-start | bytes 393220
  2.4 12.4 %copy-start.16 = (bf16[1,128,512]{2,1,0:T(8,128)(2,1)S(1)}, bf16[1,128,512]{2,1,0:T(8,128)(2,1)}, u32[]{:S(2)}) copy-start(bf16[1,128,512]{2,1,0:T(8,128)(2,1)} %param.10) | copy-start | bytes 393220
  2.4 27.3 %copy-start.10 = (s32[128,2]{0,1:T(2,128)S(1)}, s32[128,2]{0,1:T(2,128)}, u32[]{:S(2)}) copy-start(s32[128,2]{0,1:T(2,128)} %param.9) | copy-start | bytes 3076
  2.4 27.3 %copy-start.12 = (f32[128,2]{0,1:T(2,128)S(1)}, f32[128,2]{0,1:T(2,128)}, u32[]{:S(2)}) copy-start(f32[128,2]{0,1:T(2,128)} %param.8) | copy-start | bytes 3076
  4.5 57.2 %all-to-all-start = ((bf16[32,8,3072]{2,1,0:T(8,128)(2,1)}), bf16[32,8,3072]{2,1,0:T(8,128)(2,1)}, u32[]{:S(2)}, u32[]{:S(2)}) async-start(bf16[32,8,3072]{2,1,0:T(8,128)(2,1)} %bitcast.2), calls=%async_computation | async-start | bytes 3145728 | tf_op jit(solution)/shard_map/all_to_all | solution.py:373
  14.9 18.7 %collective-permute-start.4 = (bf16[128,1536]{1,0:T(8,128)(2,1)S(1)}, bf16[128,1536]{1,0:T(8,128)(2,1)S(1)}, u32[]{:S(2)}, u32[]{:S(2)}) collective-permute-start(bf16[128,1536]{1,0:T(8,128)(2,1)S(1)} %maximum_bitcast_fusion), channel_id=1, source_target_pairs={{0,448},{32,480},{64,0},{96,32},{128,64},{160,96},{192,128},{224,1... | collective-permute-start | bytes 1179656 | tf_op jit(solution)/shard_map/ppermute | solution.py:392
  25.8 15.3 %collective-permute-start = (bf16[128,1536]{1,0:T(8,128)(2,1)S(1)}, bf16[128,1536]{1,0:T(8,128)(2,1)}, u32[]{:S(2)}, u32[]{:S(2)}) collective-permute-start(bf16[128,1536]{1,0:T(8,128)(2,1)S(1)} %maximum_bitcast_fusion), channel_id=1, source_target_pairs={{0,64},{32,96},{64,128},{96,160},{128,192},{160,224},{192,256},{22... | collective-permute-start | bytes 1179656 | tf_op jit(solution)/shard_map/ppermute | solution.py:392
  27.7 17.5 %collective-permute-start.7 = (bf16[128,1536]{1,0:T(8,128)(2,1)S(1)}, bf16[128,1536]{1,0:T(8,128)(2,1)}, u32[]{:S(2)}, u32[]{:S(2)}) collective-permute-start(bf16[128,1536]{1,0:T(8,128)(2,1)S(1)} %maximum_bitcast_fusion), channel_id=1, source_target_pairs={{0,32},{32,0},{64,96},{96,64},{128,160},{160,128},{192,224},{224,1... | collective-permute-start | bytes 1179656 | tf_op jit(solution)/shard_map/ppermute | solution.py:401
  30.6 1.2 copy-start.1
  31.9 67.0 %copy-start.11 = (s32[2]{0:T(128)}, s32[2]{0:T(128)S(1)}, u32[]{:S(2)}) copy-start(s32[2]{0:T(128)S(1)} %pad_add_fusion.place_ref) | copy-start | bytes 28
  33.6 64.3 %collective-permute-start.14 = (bf16[128,1536]{1,0:T(8,128)(2,1)S(1)}, bf16[128,1536]{1,0:T(8,128)(2,1)}, u32[]{:S(2)}, u32[]{:S(2)}) collective-permute-start(bf16[128,1536]{1,0:T(8,128)(2,1)S(1)} %collective-permute-done.4), channel_id=1, source_target_pairs={{0,32},{32,0},{64,96},{96,64},{128,160},{160,128},{192,224},{224,1... | collective-permute-start | bytes 1179656 | tf_op jit(solution)/shard_map/ppermute | solution.py:401
  35.5 14.6 %collective-permute-start.5 = (bf16[128,1536]{1,0:T(8,128)(2,1)S(1)}, bf16[128,1536]{1,0:T(8,128)(2,1)}, u32[]{:S(2)}, u32[]{:S(2)}) collective-permute-start(bf16[128,1536]{1,0:T(8,128)(2,1)S(1)} %collective-permute-done.4), channel_id=1, source_target_pairs={{0,448},{32,480},{64,0},{96,32},{128,64},{160,96},{192,128},{224,1... | collective-permute-start | bytes 1179656 | tf_op jit(solution)/shard_map/ppermute | solution.py:392
  41.1 30.5 %collective-permute-start.8 = (bf16[128,1536]{1,0:T(8,128)(2,1)}, bf16[128,1536]{1,0:T(8,128)(2,1)}, u32[]{:S(2)}, u32[]{:S(2)}) collective-permute-start(bf16[128,1536]{1,0:T(8,128)(2,1)} %collective-permute-done), channel_id=1, source_target_pairs={{0,32},{32,0},{64,96},{96,64},{128,160},{160,128},{192,224},{224,1... | collective-permute-start | bytes 1179656 | tf_op jit(solution)/shard_map/ppermute | solution.py:401
  43.3 14.7 %collective-permute-start.1 = (bf16[128,1536]{1,0:T(8,128)(2,1)}, bf16[128,1536]{1,0:T(8,128)(2,1)}, u32[]{:S(2)}, u32[]{:S(2)}) collective-permute-start(bf16[128,1536]{1,0:T(8,128)(2,1)} %collective-permute-done), channel_id=1, source_target_pairs={{0,64},{32,96},{64,128},{96,160},{128,192},{160,224},{192,256},{22... | collective-permute-start | bytes 1179656 | tf_op jit(solution)/shard_map/ppermute | solution.py:392
  50.1 46.7 %collective-permute-start.13 = (bf16[128,1536]{1,0:T(8,128)(2,1)}, bf16[128,1536]{1,0:T(8,128)(2,1)}, u32[]{:S(2)}, u32[]{:S(2)}) collective-permute-start(bf16[128,1536]{1,0:T(8,128)(2,1)} %collective-permute-done.5), channel_id=1, source_target_pairs={{0,32},{32,0},{64,96},{96,64},{128,160},{160,128},{192,224},{224,1... | collective-permute-start | bytes 1179656 | tf_op jit(solution)/shard_map/ppermute | solution.py:401
  52.1 26.2 %collective-permute-start.6 = (bf16[128,1536]{1,0:T(8,128)(2,1)}, bf16[128,1536]{1,0:T(8,128)(2,1)}, u32[]{:S(2)}, u32[]{:S(2)}) collective-permute-start(bf16[128,1536]{1,0:T(8,128)(2,1)} %collective-permute-done.5), channel_id=1, source_target_pairs={{0,448},{32,480},{64,0},{96,32},{128,64},{160,96},{192,128},{224,1... | collective-permute-start | bytes 1179656 | tf_op jit(solution)/shard_map/ppermute | solution.py:392
  58.0 16.5 %collective-permute-start.2 = (bf16[128,1536]{1,0:T(8,128)(2,1)}, bf16[128,1536]{1,0:T(8,128)(2,1)}, u32[]{:S(2)}, u32[]{:S(2)}) collective-permute-start(bf16[128,1536]{1,0:T(8,128)(2,1)} %collective-permute-done.1), channel_id=1, source_target_pairs={{0,64},{32,96},{64,128},{96,160},{128,192},{160,224},{192,256},{22... | collective-permute-start | bytes 1179656 | tf_op jit(solution)/shard_map/ppermute | solution.py:392
  61.7 48.5 %all-to-all-start.1 = ((bf16[32,8,3072]{2,1,0:T(8,128)(2,1)}), bf16[32,8,3072]{2,1,0:T(8,128)(2,1)}, u32[]{:S(2)}, u32[]{:S(2)}) async-start(bf16[32,8,3072]{2,1,0:T(8,128)(2,1)} %bitcast.18), calls=%async_computation.1 | async-start | bytes 3145728 | tf_op jit(solution)/shard_map/all_to_all | solution.py:373
  71.6 9.1 %collective-permute-start.9 = (bf16[128,1536]{1,0:T(8,128)(2,1)}, bf16[128,1536]{1,0:T(8,128)(2,1)S(1)}, u32[]{:S(2)}, u32[]{:S(2)}) collective-permute-start(bf16[128,1536]{1,0:T(8,128)(2,1)} %collective-permute-done.1), channel_id=1, source_target_pairs={{0,32},{32,0},{64,96},{96,64},{128,160},{160,128},{192,224},{224,1... | collective-permute-start | bytes 1179656 | tf_op jit(solution)/shard_map/ppermute | solution.py:401
  74.6 15.1 %collective-permute-start.3 = (bf16[128,1536]{1,0:T(8,128)(2,1)}, bf16[128,1536]{1,0:T(8,128)(2,1)S(1)}, u32[]{:S(2)}, u32[]{:S(2)}) collective-permute-start(bf16[128,1536]{1,0:T(8,128)(2,1)} %collective-permute-done.2), channel_id=1, source_target_pairs={{0,64},{32,96},{64,128},{96,160},{128,192},{160,224},{192,256},{22... | collective-permute-start | bytes 1179656 | tf_op jit(solution)/shard_map/ppermute | solution.py:392
  78.3 18.4 %collective-permute-start.10 = (bf16[128,1536]{1,0:T(8,128)(2,1)}, bf16[128,1536]{1,0:T(8,128)(2,1)S(1)}, u32[]{:S(2)}, u32[]{:S(2)}) collective-permute-start(bf16[128,1536]{1,0:T(8,128)(2,1)} %collective-permute-done.2), channel_id=1, source_target_pairs={{0,32},{32,0},{64,96},{96,64},{128,160},{160,128},{192,224},{224,1... | collective-permute-start | bytes 1179656 | tf_op jit(solution)/shard_map/ppermute | solution.py:401
  80.7 16.1 %collective-permute-start.12 = (bf16[128,1536]{1,0:T(8,128)(2,1)}, bf16[128,1536]{1,0:T(8,128)(2,1)S(1)}, u32[]{:S(2)}, u32[]{:S(2)}) collective-permute-start(bf16[128,1536]{1,0:T(8,128)(2,1)} %collective-permute-done.6), channel_id=1, source_target_pairs={{0,32},{32,0},{64,96},{96,64},{128,160},{160,128},{192,224},{224,1... | collective-permute-start | bytes 1179656 | tf_op jit(solution)/shard_map/ppermute | solution.py:401
  89.7 7.1 %collective-permute-start.11 = (bf16[128,1536]{1,0:T(8,128)(2,1)S(1)}, bf16[128,1536]{1,0:T(8,128)(2,1)S(1)}, u32[]{:S(2)}, u32[]{:S(2)}) collective-permute-start(bf16[128,1536]{1,0:T(8,128)(2,1)S(1)} %collective-permute-done.3), channel_id=1, source_target_pairs={{0,32},{32,0},{64,96},{96,64},{128,160},{160,128},{192,224},{224,1... | collective-permute-start | bytes 1179656 | tf_op jit(solution)/shard_map/ppermute | solution.py:401
  98.9 7.2 %copy-start = (bf16[1024,1536]{1,0:T(8,128)(2,1)}, bf16[1024,1536]{1,0:T(8,128)(2,1)S(1)}, u32[]{:S(2)}) copy-start(bf16[1024,1536]{1,0:T(8,128)(2,1)S(1)} %constant_dynamic-update-slice_fusion.8.other_ref) | copy-start | bytes 9437188
  106.1 1.2 copy-start.2
  107.3 1.2 copy-start.3
  108.4 0.9 copy-start.4
  109.4 0.9 copy-start.5
  110.2 47.6 %all-to-all-start.2 = ((bf16[32,8,3072]{2,1,0:T(8,128)(2,1)}), bf16[32,8,3072]{2,1,0:T(8,128)(2,1)S(1)}, u32[]{:S(2)}, u32[]{:S(2)}) async-start(bf16[32,8,3072]{2,1,0:T(8,128)(2,1)} %bitcast.20), calls=%async_computation.2 | async-start | bytes 3145728 | tf_op jit(solution)/shard_map/all_to_all | solution.py:373
  128.9 6.3 %collective-permute-start.15 = (bf16[1024,1024]{1,0:T(8,128)(2,1)}, bf16[1024,1024]{1,0:T(8,128)(2,1)S(1)}, u32[]{:S(2)}, u32[]{:S(2)}) collective-permute-start(bf16[1024,1024]{1,0:T(8,128)(2,1)} %get-tuple-element.45), channel_id=1, source_target_pairs={{0,32},{32,0},{64,96},{96,64},{128,160},{160,128},{192,224},{224,1... | collective-permute-start | bytes 6291464 | tf_op jit(solution)/shard_map/ppermute | solution.py:447
  137.7 1.4 copy-start.13
  140.2 35.2 %collective-permute-start.18 = (bf16[128,1024]{1,0:T(8,128)(2,1)S(1)}, bf16[128,1024]{1,0:T(8,128)(2,1)S(1)}, u32[]{:S(2)}, u32[]{:S(2)}) collective-permute-start(bf16[128,1024]{1,0:T(8,128)(2,1)S(1)} %get-tuple-element.62), channel_id=1, source_target_pairs={{0,320},{32,352},{64,384},{96,416},{128,448},{160,480},{192,0},{22... | collective-permute-start | bytes 786440 | tf_op jit(solution)/shard_map/ppermute | solution.py:392
  142.1 36.3 %collective-permute-start.20 = (bf16[128,1024]{1,0:T(8,128)(2,1)S(1)}, bf16[128,1024]{1,0:T(8,128)(2,1)S(1)}, u32[]{:S(2)}, u32[]{:S(2)}) collective-permute-start(bf16[128,1024]{1,0:T(8,128)(2,1)S(1)} %get-tuple-element.63), channel_id=1, source_target_pairs={{0,192},{32,224},{64,256},{96,288},{128,320},{160,352},{192,384},{... | collective-permute-start | bytes 786440 | tf_op jit(solution)/shard_map/ppermute | solution.py:392
  154.6 26.4 %copy-start.7 = (bf16[128,2048]{1,0:T(8,128)(2,1)S(1)}, bf16[128,2048]{1,0:T(8,128)(2,1)}, u32[]{:S(2)}) copy-start(bf16[128,2048]{1,0:T(8,128)(2,1)} %grad_ref.1) | copy-start | bytes 1572868
  154.6 28.9 %collective-permute-start.19 = (bf16[128,1024]{1,0:T(8,128)(2,1)}, bf16[128,1024]{1,0:T(8,128)(2,1)}, u32[]{:S(2)}, u32[]{:S(2)}) collective-permute-start(bf16[128,1024]{1,0:T(8,128)(2,1)} %get-tuple-element.64), channel_id=1, source_target_pairs={{0,256},{32,288},{64,320},{96,352},{128,384},{160,416},{192,448},{... | collective-permute-start | bytes 786440 | tf_op jit(solution)/shard_map/ppermute | solution.py:392
  157.9 46.8 %all-to-all-start.3 = ((bf16[32,8,3072]{2,1,0:T(8,128)(2,1)}), bf16[32,8,3072]{2,1,0:T(8,128)(2,1)}, u32[]{:S(2)}, u32[]{:S(2)}) async-start(bf16[32,8,3072]{2,1,0:T(8,128)(2,1)} %bitcast.27), calls=%async_computation.3 | async-start | bytes 3145728 | tf_op jit(solution)/shard_map/all_to_all | solution.py:373
  167.7 16.3 %collective-permute-start.16 = (bf16[128,1024]{1,0:T(8,128)(2,1)}, bf16[128,1024]{1,0:T(8,128)(2,1)}, u32[]{:S(2)}, u32[]{:S(2)}) collective-permute-start(bf16[128,1024]{1,0:T(8,128)(2,1)} %get-tuple-element.48), channel_id=1, source_target_pairs={{0,448},{32,480},{64,0},{96,32},{128,64},{160,96},{192,128},{224,1... | collective-permute-start | bytes 786440 | tf_op jit(solution)/shard_map/ppermute | solution.py:392
  171.7 20.1 %collective-permute-start.17 = (bf16[128,1024]{1,0:T(8,128)(2,1)}, bf16[128,1024]{1,0:T(8,128)(2,1)}, u32[]{:S(2)}, u32[]{:S(2)}) collective-permute-start(bf16[128,1024]{1,0:T(8,128)(2,1)} %get-tuple-element.49), channel_id=1, source_target_pairs={{0,384},{32,416},{64,448},{96,480},{128,0},{160,32},{192,64},{224,... | collective-permute-start | bytes 786440 | tf_op jit(solution)/shard_map/ppermute | solution.py:392
  175.4 7.5 %copy-start.17 = (bf16[128,1024]{1,0:T(8,128)(2,1)}, bf16[128,1024]{1,0:T(8,128)(2,1)S(1)}, u32[]{:S(2)}) copy-start(bf16[128,1024]{1,0:T(8,128)(2,1)S(1)} %collective-permute-done.18) | copy-start | bytes 786436
  175.4 18.9 %collective-permute-start.21 = (bf16[128,1024]{1,0:T(8,128)(2,1)}, bf16[128,1024]{1,0:T(8,128)(2,1)}, u32[]{:S(2)}, u32[]{:S(2)}) collective-permute-start(bf16[128,1024]{1,0:T(8,128)(2,1)} %get-tuple-element.50), channel_id=1, source_target_pairs={{0,128},{32,160},{64,192},{96,224},{128,256},{160,288},{192,320},{... | collective-permute-start | bytes 786440 | tf_op jit(solution)/shard_map/ppermute | solution.py:392
  178.4 4.5 %copy-start.18 = (bf16[128,1024]{1,0:T(8,128)(2,1)}, bf16[128,1024]{1,0:T(8,128)(2,1)S(1)}, u32[]{:S(2)}) copy-start(bf16[128,1024]{1,0:T(8,128)(2,1)S(1)} %collective-permute-done.20) | copy-start | bytes 786436
  178.5 19.0 %collective-permute-start.22 = (bf16[128,1024]{1,0:T(8,128)(2,1)}, bf16[128,1024]{1,0:T(8,128)(2,1)}, u32[]{:S(2)}, u32[]{:S(2)}) collective-permute-start(bf16[128,1024]{1,0:T(8,128)(2,1)} %get-tuple-element.51), channel_id=1, source_target_pairs={{0,64},{32,96},{64,128},{96,160},{128,192},{160,224},{192,256},{22... | collective-permute-start | bytes 786440 | tf_op jit(solution)/shard_map/ppermute | solution.py:392

commit v7 on v3

--- a/solution.py
+++ b/solution.py
@@ -80,19 +80,29 @@
     return jnp.where(both, 1.0, 0.0).astype(BF)
 
 
-def pack_tokens(experts_ref, rows_ref, out_ref):
+def pack_tokens(experts_ref, rows_ref, out_ref, rows_in, sems):
     count = out_ref.shape[0] // 8
     width = rows_ref.shape[1]
     half = width // 2
+    copies = [
+        pltpu.make_async_copy(
+            rows_ref.at[:, pl.ds(i * half, half)], rows_in.at[:, pl.ds(i * half, half)], sems.at[i]
+        )
+        for i in range(2)
+    ]
+    for copy in copies:
+        copy.start()
     first, second = send_masks(experts_ref, count)
     wide = one_hot(first[0], second[0])
     halves = [one_hot(first[1 + h], second[1 + h]) for h in range(2)]
-    for c in range(0, width, TILE):
-        out_ref[:, c : c + TILE] = dot(wide, rows_ref[:, c : c + TILE]).astype(BF)
+    for i in range(2):
+        copies[i].wait()
+        for c in range(i * half, (i + 1) * half, TILE):
+            out_ref[:, c : c + TILE] = dot(wide, rows_in[:, c : c + TILE]).astype(BF)
     for c in range(0, half, TILE):
         out_ref[:, width + c : width + c + TILE] = (
-            dot(halves[0], rows_ref[:, c : c + TILE])
-            + dot(halves[1], rows_ref[:, half + c : half + c + TILE])
+            dot(halves[0], rows_in[:, c : c + TILE])
+            + dot(halves[1], rows_in[:, half + c : half + c + TILE])
         ).astype(BF)
 
 
@@ -159,18 +169,31 @@
     gate_grad_ref[...] = jnp.where(lane == 0, sums[0], sums[1])
 
 
-def combine_grads(experts_ref, got_ref, out_ref):
+def combine_grads(experts_ref, got_ref, out_ref, got_in, sems):
     count = got_ref.shape[0] // 8
     width = out_ref.shape[1]
     half = width // 2
+    pieces = ((width, half), (0, half), (half, half))
+    copies = [
+        pltpu.make_async_copy(
+            got_ref.at[:, pl.ds(at, size)], got_in.at[:, pl.ds(at, size)], sems.at[i]
+        )
+        for i, (at, size) in enumerate(pieces)
+    ]
+    for copy in copies:
+        copy.start()
     first, second = fetch_masks(experts_ref, count)
     wide = one_hot(first[0], second[0])
     halves = [one_hot(first[1 + h], second[1 + h]) for h in range(2)]
-    for c in range(0, width, TILE):
-        low = width + c % half
-        out_ref[:, c : c + TILE] = (
-            dot(wide, got_ref[:, c : c + TILE]) + dot(halves[c // half], got_ref[:, low : low + TILE])
-        ).astype(BF)
+    copies[0].wait()
+    for h in range(2):
+        copies[1 + h].wait()
+        for c in range(0, half, TILE):
+            at = h * half + c
+            out_ref[:, at : at + TILE] = (
+                dot(wide, got_in[:, at : at + TILE])
+                + dot(halves[h], got_in[:, width + c : width + c + TILE])
+            ).astype(BF)
 
 
 def split_rows(got_ref, rows_ref):
@@ -353,7 +376,9 @@
         return moved.reshape(send)
 
     pack_flops = 2 * send[0] * toks * send[1]
-    (send_tok,) = call(pack_tokens, [(send, BF)], [], pack_flops, experts_t, tokens)
+    (send_tok,) = call(
+        pack_tokens, [(send, BF)], [((toks, width), BF)], pack_flops, experts_t, tokens, far=(1,)
+    )
     shards, send_tok = lax.optimization_barrier(((gate_weight, up_weight, down_weight), send_tok))
     weights = lax.all_gather(jnp.concatenate(shards, axis=2), "dp", axis=1, tiled=True)[0]
     (send_grad,) = call(pack_grads, [(send, BF)], [], pack_flops, experts_t, gates_t, out_grad)
@@ -429,7 +454,13 @@
         (experts_t, (summed[:, :, :hid], summed[:, :, hid:]))
     )
     (token_grad,) = call(
-        combine_grads, [((toks, width), BF)], [], 4 * toks * send[0] * width, experts_t, got_back
+        combine_grads,
+        [((toks, width), BF)],
+        [(send, BF)],
+        4 * toks * send[0] * width,
+        experts_t,
+        got_back,
+        far=(1,),
     )
     return (mixed, token_grad, gate_grad, *summed)
 

time: 206 us -> 206 us (level)
  Pallas kernels: 28.7 us -> 30.9 us
    pallas_call x7, Pallas kernels: 28.7 us -> 30.9 us  [call(): pl.pallas_call(body, out_shape=[jax.ShapeDtypeStruct(s, d) for s, d in ou...]
    unnamed x27 -> x23, local copies, waits for them, and re-layouts: 8.12 us -> 6.4 us
where the time goes in v7:
time: 206 us; the launch traced here: 203 us
  waiting for transfers between devices  109 us (53%)
  starting transfers between devices  35.7 us (17%)
  Pallas kernels  30.9 us (15%)
  between operations  14.3 us (7%)
  local copies, waits for them, and re-layouts  7.22 us (4%)
  other arithmetic  5.64 us (3%)
    all_to_all x4, waiting for transfers between devices, exchange(): lax.all_to_all(rows.reshape(count, 8, send[1]), 'expert', split_axis=0, c...  85.3 us
    all_to_all x4, starting transfers between devices, exchange(): lax.all_to_all(rows.reshape(count, 8, send[1]), 'expert', split_axis=0, c...  33.7 us
    pallas_call x7, Pallas kernels, call(): pl.pallas_call(body, out_shape=[jax.ShapeDtypeStruct(s, d) for s, d in ou...  30.9 us
    reduce_scatter x1, waiting for transfers between devices, on_device(): lax.psum_scatter(pair, 'dp', scatter_dimension=0, tiled=True, axis_index_...  24 us
    unnamed x23, local copies, waits for them, and re-layouts  6.4 us
  transfers between devices with their start and end apart: 7, of which 5 were waited for; matrix products, arithmetic and copies ran while one was open for 3% of the time, Pallas kernels for 12%

profile of v7, /device:TPU:6, one launch (start us, length us, event | category | flops | bytes accessed | tf_op | source)
XLA Modules:
  0.0 203.1 jit_solution(17994983343496369947)
XLA Ops:
  7.2 0.0 copy-start.8
  7.2 0.0 copy-start.9
  7.2 0.0 copy-start.10
  7.2 0.0 all-gather.2.cloned.1.call-start
  7.2 3.8 %shard_map.110 = bf16[256,3072]{1,0:T(8,128)(2,1)} custom-call(s32[2,128]{1,0:T(2,128)} %bitcast.20, bf16[128,2048]{1,0:T(8,128)(2,1)} %rows_ref.2), custom_call_target="tpu_custom_call" | custom-call | flops 201326592 | bytes 2098176 | tf_op jit(solution)/shard_map/pallas_call | solution.py:345
  11.1 0.0 copy-done.8
  11.1 0.0 copy-done.9
  11.1 0.0 copy-done.10
  11.1 0.0 copy-start.4
  11.1 0.0 copy-start.5
  11.1 0.0 copy-start.6
  11.1 0.8 pad_maximum_fusion
  11.9 0.0 all-gather.2.cloned.1.call-update
  11.9 10.3 %all-to-all-start = ((bf16[32,8,3072]{2,1,0:T(8,128)(2,1)}), bf16[32,8,3072]{2,1,0:T(8,128)(2,1)S(1)}, u32[]{:S(2)}, u32[]{:S(2)}) async-start(bf16[32,8,3072]{2,1,0:T(8,128)(2,1)} %bitcast.26), calls=%async_computation | async-start | bytes 3145728 | tf_op jit(solution)/shard_map/all_to_all | solution.py:368
  22.2 0.0 copy-done.4
  22.2 0.0 copy-done.5
  22.2 0.0 copy-done.6
  22.2 2.0 shard_map.111
  24.2 35.0 %all-to-all-done = bf16[32,8,3072]{2,1,0:T(8,128)(2,1)S(1)} async-done(((bf16[32,8,3072]{2,1,0:T(8,128)(2,1)}), bf16[32,8,3072]{2,1,0:T(8,128)(2,1)S(1)}, u32[]{:S(2)}, u32[]{:S(2)}) %all-to-all-start) | async-done | bytes 1572896 | tf_op jit(solution)/shard_map/all_to_all | solution.py:368
  59.3 7.9 %all-to-all-start.1 = ((bf16[32,8,3072]{2,1,0:T(8,128)(2,1)}), bf16[32,8,3072]{2,1,0:T(8,128)(2,1)}, u32[]{:S(2)}, u32[]{:S(2)}) async-start(bf16[32,8,3072]{2,1,0:T(8,128)(2,1)} %bitcast.4), calls=%async_computation.1 | async-start | bytes 3145728 | tf_op jit(solution)/shard_map/all_to_all | solution.py:368
  67.2 0.0 all-gather.2.cloned.1.call-done
  67.2 0.0 copy-start
  67.2 2.8 %copy-done = bf16[1,2048,1536]{2,1,0:T(8,128)(2,1)S(1)} copy-done((bf16[1,2048,1536]{2,1,0:T(8,128)(2,1)S(1)}, bf16[1,2048,1536]{2,1,0:T(8,128)(2,1)}, u32[]{:S(2)}) %copy-start) | copy-done | bytes 6291480
  70.0 4.6 %shard_map.112 = (bf16[256,3072]{1,0:T(8,128)(2,1)}, bf16[384,2048]{1,0:T(8,128)(2,1)S(1)}, f32[384,512]{1,0:T(8,128)S(1)}, f32[384,512]{1,0:T(8,128)S(1)}) custom-call(s32[1]{0:T(128)} %bitcast.6.core_ref, bf16[256,3072]{1,0:T(8,128)(2,1)S(1)} %bitcast.18, bf16[2048,1536]{1,0:T(8,128)(2,1)S(1)} %bitcast.17), custom_call_target="tpu_custom_call" | custom-call | flops 2415919104 | bytes 12582916 | tf_op jit(solution)/shard_map/pallas_call | solution.py:345
  74.6 0.0 copy-start.1
  74.6 1.2 copy-done.1
  75.8 0.9 copy-done.2
  76.7 0.9 copy-done.3
  77.6 26.3 %all-to-all-done.1 = bf16[32,8,3072]{2,1,0:T(8,128)(2,1)} async-done(((bf16[32,8,3072]{2,1,0:T(8,128)(2,1)}), bf16[32,8,3072]{2,1,0:T(8,128)(2,1)}, u32[]{:S(2)}, u32[]{:S(2)}) %all-to-all-start.1) | async-done | bytes 1572896 | tf_op jit(solution)/shard_map/all_to_all | solution.py:368
  103.9 7.7 %all-to-all-start.2 = ((bf16[32,8,3072]{2,1,0:T(8,128)(2,1)}), bf16[32,8,3072]{2,1,0:T(8,128)(2,1)S(1)}, u32[]{:S(2)}, u32[]{:S(2)}) async-start(bf16[32,8,3072]{2,1,0:T(8,128)(2,1)} %bitcast.8), calls=%async_computation.2 | async-start | bytes 3145728 | tf_op jit(solution)/shard_map/all_to_all | solution.py:368
  111.7 0.0 reduce-scatter.2.cloned.1.call-start
  111.7 8.7 %shard_map.113 = (bf16[384,1024]{1,0:T(8,128)(2,1)}, bf16[1024,1024]{1,0:T(8,128)(2,1)}, bf16[1024,1024]{1,0:T(8,128)(2,1)}) custom-call(bf16[256,3072]{1,0:T(8,128)(2,1)} %bitcast.5.got_ref, bf16[2048,1536]{1,0:T(8,128)(2,1)} %bitcast.15, f32[384,512]{1,0:T(8,128)} %copy-done.2, f32[384,512]{1,0:T(8,128)} %copy-done.3, bf16[384,2048]{1,0:T(8,128)(2,1)} %copy-done.1), custom_call_target="tpu_custom_call" | custom-call | flops 2415919104 | bytes 15990784 | tf_op jit(solution)/shard_map/pallas_call | solution.py:345
  120.5 1.9 collective-permute-start
  122.4 0.0 copy-start.7
  122.4 6.5 %shard_map.114 = bf16[256,3072]{1,0:T(8,128)(2,1)} custom-call(bf16[384,1024]{1,0:T(8,128)(2,1)} %get-tuple-element.39.pre_ref, bf16[2048,1536]{1,0:T(8,128)(2,1)} %bitcast.16), custom_call_target="tpu_custom_call" | custom-call | flops 1610612736 | bytes 8650752 | tf_op jit(solution)/shard_map/pallas_call | solution.py:345
  128.9 0.0 collective-permute-done
  128.9 0.0 copy-done.7
  128.9 3.9 %add_convert_fusion = bf16[1024,1024]{1,0:T(8,128)(2,1)} fusion(bf16[1024,1024]{1,0:T(8,128)(2,1)} %collective-permute-done, bf16[1024,1024]{1,0:T(8,128)(2,1)S(1)} %copy-done.7), kind=kLoop, calls=%fused_computation | loop fusion | flops 4194304 | bytes 6291456 | tf_op jit(solution)/shard_map/convert_element_type | solution.py:424
  132.8 0.0 reduce-scatter.2.cloned.1.call-update
  132.8 15.5 %all-to-all-done.2 = bf16[32,8,3072]{2,1,0:T(8,128)(2,1)S(1)} async-done(((bf16[32,8,3072]{2,1,0:T(8,128)(2,1)}), bf16[32,8,3072]{2,1,0:T(8,128)(2,1)S(1)}, u32[]{:S(2)}, u32[]{:S(2)}) %all-to-all-start.2) | async-done | bytes 1572896 | tf_op jit(solution)/shard_map/all_to_all | solution.py:368
  148.4 7.8 %all-to-all-start.3 = ((bf16[32,8,3072]{2,1,0:T(8,128)(2,1)}), bf16[32,8,3072]{2,1,0:T(8,128)(2,1)}, u32[]{:S(2)}, u32[]{:S(2)}) async-start(bf16[32,8,3072]{2,1,0:T(8,128)(2,1)} %bitcast.27), calls=%async_computation.4 | async-start | bytes 3145728 | tf_op jit(solution)/shard_map/all_to_all | solution.py:368
  156.2 1.9 shard_map.115
  158.1 0.6 copy.12
  158.7 24.0 %reduce-scatter.2.cloned.1.call-done = bf16[128,1024]{1,0:T(8,128)(2,1)} async-done(((bf16[1024,1024]{1,0:T(8,128)(2,1)}), bf16[128,1024]{1,0:T(8,128)(2,1)}) %reduce-scatter.2.cloned.1.call-update) | async-done | bytes 262160 | tf_op jit(solution)/shard_map/reduce_scatter | solution.py:425
  182.7 1.0 bitcast_convert_fusion
  183.7 0.8 fusion
  184.6 8.4 %all-to-all-done.3 = bf16[32,8,3072]{2,1,0:T(8,128)(2,1)} async-done(((bf16[32,8,3072]{2,1,0:T(8,128)(2,1)}), bf16[32,8,3072]{2,1,0:T(8,128)(2,1)}, u32[]{:S(2)}, u32[]{:S(2)}) %all-to-all-start.3) | async-done | bytes 1572896 | tf_op jit(solution)/shard_map/all_to_all | solution.py:368
  192.9 3.3 %shard_map.116 = bf16[128,2048]{1,0:T(8,128)(2,1)} custom-call(s32[2,128]{1,0:T(2,128)} %bitcast.21, bf16[256,3072]{1,0:T(8,128)(2,1)} %bitcast.13.got_ref), custom_call_target="tpu_custom_call" | custom-call | flops 268435456 | bytes 2098176 | tf_op jit(solution)/shard_map/pallas_call | solution.py:345
  (2 shorter events, 0.0 us)
Async XLA Ops:
  7.2 3.9 %copy-start.8 = (bf16[1,128,512]{2,1,0:T(8,128)(2,1)S(1)}, bf16[1,128,512]{2,1,0:T(8,128)(2,1)}, u32[]{:S(2)}) copy-start(bf16[1,128,512]{2,1,0:T(8,128)(2,1)} %param.12) | copy-start | bytes 393220
  7.2 3.9 %copy-start.9 = (bf16[1,128,512]{2,1,0:T(8,128)(2,1)S(1)}, bf16[1,128,512]{2,1,0:T(8,128)(2,1)}, u32[]{:S(2)}) copy-start(bf16[1,128,512]{2,1,0:T(8,128)(2,1)} %param.11) | copy-start | bytes 393220
  7.2 3.9 %copy-start.10 = (bf16[1,128,512]{2,1,0:T(8,128)(2,1)S(1)}, bf16[1,128,512]{2,1,0:T(8,128)(2,1)}, u32[]{:S(2)}) copy-start(bf16[1,128,512]{2,1,0:T(8,128)(2,1)} %param.10) | copy-start | bytes 393220
  7.2 60.0 %all-gather.2.cloned.1.call-start = ((), (), s32[]{:S(2)}) async-start(), calls=%async_computation.5 | async-start | bytes 6684672 | tf_op jit(solution)/shard_map/all_gather | solution.py:383
  11.1 11.1 %copy-start.4 = (bf16[128,2048]{1,0:T(8,128)(2,1)S(1)}, bf16[128,2048]{1,0:T(8,128)(2,1)}, u32[]{:S(2)}) copy-start(bf16[128,2048]{1,0:T(8,128)(2,1)} %grad_ref.1) | copy-start | bytes 1572868
  11.1 11.1 %copy-start.5 = (s32[128,2]{0,1:T(2,128)S(1)}, s32[128,2]{0,1:T(2,128)}, u32[]{:S(2)}) copy-start(s32[128,2]{0,1:T(2,128)} %param.9) | copy-start | bytes 3076
  11.1 11.1 %copy-start.6 = (f32[128,2]{0,1:T(2,128)S(1)}, f32[128,2]{0,1:T(2,128)}, u32[]{:S(2)}) copy-start(f32[128,2]{0,1:T(2,128)} %param.8) | copy-start | bytes 3076
  11.9 47.3 %all-to-all-start = ((bf16[32,8,3072]{2,1,0:T(8,128)(2,1)}), bf16[32,8,3072]{2,1,0:T(8,128)(2,1)S(1)}, u32[]{:S(2)}, u32[]{:S(2)}) async-start(bf16[32,8,3072]{2,1,0:T(8,128)(2,1)} %bitcast.26), calls=%async_computation | async-start | bytes 3145728 | tf_op jit(solution)/shard_map/all_to_all | solution.py:368
  59.3 44.7 %all-to-all-start.1 = ((bf16[32,8,3072]{2,1,0:T(8,128)(2,1)}), bf16[32,8,3072]{2,1,0:T(8,128)(2,1)}, u32[]{:S(2)}, u32[]{:S(2)}) async-start(bf16[32,8,3072]{2,1,0:T(8,128)(2,1)} %bitcast.4), calls=%async_computation.1 | async-start | bytes 3145728 | tf_op jit(solution)/shard_map/all_to_all | solution.py:368
  67.2 2.8 %copy-start = (bf16[1,2048,1536]{2,1,0:T(8,128)(2,1)S(1)}, bf16[1,2048,1536]{2,1,0:T(8,128)(2,1)}, u32[]{:S(2)}) copy-start(bf16[1,2048,1536]{2,1,0:T(8,128)(2,1)} %all-gather.2.cloned.1.call-done) | copy-start | bytes 18874372
  74.6 1.2 copy-start.1
  75.8 0.9 copy-start.2
  76.7 0.9 copy-start.3
  103.9 44.5 %all-to-all-start.2 = ((bf16[32,8,3072]{2,1,0:T(8,128)(2,1)}), bf16[32,8,3072]{2,1,0:T(8,128)(2,1)S(1)}, u32[]{:S(2)}, u32[]{:S(2)}) async-start(bf16[32,8,3072]{2,1,0:T(8,128)(2,1)} %bitcast.8), calls=%async_computation.2 | async-start | bytes 3145728 | tf_op jit(solution)/shard_map/all_to_all | solution.py:368
  111.7 71.1 %reduce-scatter.2.cloned.1.call-start = ((), (), s32[]{:S(2)}) async-start(), calls=%async_computation.6 | async-start | bytes 2359296 | tf_op jit(solution)/shard_map/reduce_scatter | solution.py:425
  120.5 8.4 %collective-permute-start = (bf16[1024,1024]{1,0:T(8,128)(2,1)}, bf16[1024,1024]{1,0:T(8,128)(2,1)}, u32[]{:S(2)}, u32[]{:S(2)}) collective-permute-start(bf16[1024,1024]{1,0:T(8,128)(2,1)} %get-tuple-element.43), channel_id=1, source_target_pairs={{0,32},{32,0},{64,96},{96,64},{128,160},{160,128},{192,224},{224,1... | collective-permute-start | bytes 6291464 | tf_op jit(solution)/shard_map/ppermute | solution.py:423
  122.4 6.5 %copy-start.7 = (bf16[1024,1024]{1,0:T(8,128)(2,1)S(1)}, bf16[1024,1024]{1,0:T(8,128)(2,1)}, u32[]{:S(2)}) copy-start(bf16[1024,1024]{1,0:T(8,128)(2,1)} %get-tuple-element.42) | copy-start | bytes 6291460
  148.4 44.6 %all-to-all-start.3 = ((bf16[32,8,3072]{2,1,0:T(8,128)(2,1)}), bf16[32,8,3072]{2,1,0:T(8,128)(2,1)}, u32[]{:S(2)}, u32[]{:S(2)}) async-start(bf16[32,8,3072]{2,1,0:T(8,128)(2,1)} %bitcast.27), calls=%async_computation.4 | async-start | bytes 3145728 | tf_op jit(solution)/shard_map/all_to_all | solution.py:368
Sparse Core Ops, SparseCore 0:
  12.0 54.0 all-gather.1
  133.0 49.7 reduce-scatter.1

commit v8 on v3

--- a/solution.py
+++ b/solution.py
@@ -24,8 +24,12 @@
     return lax.dot_general(left, right, (((1,), (1,)), ((), ())), preferred_element_type=F32)
 
 
+NEAR_FIRST = (0, 1, 7, 2, 6, 3, 5, 4)
+
+
 def turn(expert):
-    return (expert & 3) * 8 + (expert >> 2)
+    y = expert >> 2
+    return (expert & 3) * 8 + jnp.where(y > 4, 16 - 2 * y, jnp.maximum(2 * y - 1, 0))
 
 
 def pick_ranks(experts_ref, count):
@@ -348,7 +352,7 @@
             split_axis=0,
             concat_axis=0,
             tiled=True,
-            axis_index_groups=[[y * 4 + x for x in range(4) for y in range(8)]],
+            axis_index_groups=[[y * 4 + x for x in range(4) for y in NEAR_FIRST]],
         )
         return moved.reshape(send)
 

time: 206 us -> 205 us (level)
  starting transfers between devices: 35.7 us -> 33.2 us
    all_to_all x4, starting transfers between devices: 33.7 us -> 31.2 us  [exchange(): lax.all_to_all(rows.reshape(count, 8, send[1]), 'expert', split_axis=0, c...]
where the time goes in v8:
time: 205 us; the launch traced here: 201 us
  waiting for transfers between devices  110 us (54%)
  starting transfers between devices  33.2 us (16%)
  Pallas kernels  28.8 us (14%)
  between operations  14.2 us (7%)
  local copies, waits for them, and re-layouts  8.95 us (4%)
  other arithmetic  5.63 us (3%)
    all_to_all x4, waiting for transfers between devices, exchange(): lax.all_to_all(rows.reshape(count, 8, send[1]), 'expert', split_axis=0, c...  85.4 us
    all_to_all x4, starting transfers between devices, exchange(): lax.all_to_all(rows.reshape(count, 8, send[1]), 'expert', split_axis=0, c...  31.2 us
    pallas_call x7, Pallas kernels, call(): pl.pallas_call(body, out_shape=[jax.ShapeDtypeStruct(s, d) for s, d in ou...  28.8 us
    reduce_scatter x1, waiting for transfers between devices, on_device(): lax.psum_scatter(pair, 'dp', scatter_dimension=0, tiled=True, axis_index_...  24.8 us
    unnamed x27, local copies, waits for them, and re-layouts  8.12 us
  transfers between devices with their start and end apart: 7, of which 5 were waited for; matrix products, arithmetic and copies ran while one was open for 3% of the time, Pallas kernels for 12%

profile of v8, /device:TPU:6, one launch (start us, length us, event | category | flops | bytes accessed | tf_op | source)
XLA Modules:
  0.0 201.1 jit_solution(2741800345325138273)
XLA Ops:
  7.2 0.0 all-gather.2.cloned.1.call-start
  7.2 0.0 copy-start.5
  7.2 1.0 copy-done.5
  8.3 0.0 copy-start.6
  8.3 0.7 copy-done.6
  8.9 0.0 copy-start.10
  8.9 2.1 %shard_map.110 = bf16[256,3072]{1,0:T(8,128)(2,1)} custom-call(s32[2,128]{1,0:T(2,128)S(1)} %bitcast.20, bf16[128,2048]{1,0:T(8,128)(2,1)S(1)} %copy-done.5), custom_call_target="tpu_custom_call" | custom-call | flops 201326592 | bytes 2098176 | tf_op jit(solution)/shard_map/pallas_call | solution.py:326
  11.0 0.0 copy-done.10
  11.0 0.0 copy-done.11
  11.0 0.0 copy-done.12
  11.0 0.0 copy-start.7
  11.0 0.0 copy-start.8
  11.0 0.8 pad_maximum_fusion
  11.8 0.0 all-gather.2.cloned.1.call-update
  11.8 10.2 %all-to-all-start = ((bf16[32,8,3072]{2,1,0:T(8,128)(2,1)}), bf16[32,8,3072]{2,1,0:T(8,128)(2,1)S(1)}, u32[]{:S(2)}, u32[]{:S(2)}) async-start(bf16[32,8,3072]{2,1,0:T(8,128)(2,1)} %bitcast.2), calls=%async_computation | async-start | bytes 3145728 | tf_op jit(solution)/shard_map/all_to_all | solution.py:349
  22.1 0.0 copy-done.4
  22.1 0.0 copy-done.7
  22.1 0.0 copy-done.8
  22.1 2.0 %shard_map.111 = bf16[256,3072]{1,0:T(8,128)(2,1)} custom-call(s32[2,128]{1,0:T(2,128)S(1)} %bitcast.21, f32[2,128]{1,0:T(2,128)S(1)} %bitcast.24, bf16[128,2048]{1,0:T(8,128)(2,1)S(1)} %copy-done.4), custom_call_target="tpu_custom_call" | custom-call | flops 201326592 | bytes 2099200 | tf_op jit(solution)/shard_map/pallas_call | solution.py:326
  24.2 35.6 %all-to-all-done = bf16[32,8,3072]{2,1,0:T(8,128)(2,1)S(1)} async-done(((bf16[32,8,3072]{2,1,0:T(8,128)(2,1)}), bf16[32,8,3072]{2,1,0:T(8,128)(2,1)S(1)}, u32[]{:S(2)}, u32[]{:S(2)}) %all-to-all-start) | async-done | bytes 1572896 | tf_op jit(solution)/shard_map/all_to_all | solution.py:349
  59.8 6.8 %all-to-all-start.1 = ((bf16[32,8,3072]{2,1,0:T(8,128)(2,1)}), bf16[32,8,3072]{2,1,0:T(8,128)(2,1)}, u32[]{:S(2)}, u32[]{:S(2)}) async-start(bf16[32,8,3072]{2,1,0:T(8,128)(2,1)} %bitcast.4), calls=%async_computation.1 | async-start | bytes 3145728 | tf_op jit(solution)/shard_map/all_to_all | solution.py:349
  66.6 0.0 all-gather.2.cloned.1.call-done
  66.6 0.0 copy-start
  66.6 2.8 %copy-done = bf16[1,2048,1536]{2,1,0:T(8,128)(2,1)S(1)} copy-done((bf16[1,2048,1536]{2,1,0:T(8,128)(2,1)S(1)}, bf16[1,2048,1536]{2,1,0:T(8,128)(2,1)}, u32[]{:S(2)}) %copy-start) | copy-done | bytes 6291480
  69.4 4.6 %shard_map.112 = (bf16[256,3072]{1,0:T(8,128)(2,1)}, bf16[384,2048]{1,0:T(8,128)(2,1)S(1)}, f32[384,512]{1,0:T(8,128)S(1)}, f32[384,512]{1,0:T(8,128)S(1)}) custom-call(s32[1]{0:T(128)} %bitcast.6.core_ref, bf16[256,3072]{1,0:T(8,128)(2,1)S(1)} %bitcast.18, bf16[2048,1536]{1,0:T(8,128)(2,1)S(1)} %bitcast.17), custom_call_target="tpu_custom_call" | custom-call | flops 2415919104 | bytes 12582916 | tf_op jit(solution)/shard_map/pallas_call | solution.py:326
  74.1 1.2 copy-done.1
  75.2 0.9 copy-done.2
  76.1 0.9 copy-done.3
  77.0 26.5 %all-to-all-done.1 = bf16[32,8,3072]{2,1,0:T(8,128)(2,1)} async-done(((bf16[32,8,3072]{2,1,0:T(8,128)(2,1)}), bf16[32,8,3072]{2,1,0:T(8,128)(2,1)}, u32[]{:S(2)}, u32[]{:S(2)}) %all-to-all-start.1) | async-done | bytes 1572896 | tf_op jit(solution)/shard_map/all_to_all | solution.py:349
  103.5 7.1 %all-to-all-start.2 = ((bf16[32,8,3072]{2,1,0:T(8,128)(2,1)}), bf16[32,8,3072]{2,1,0:T(8,128)(2,1)S(1)}, u32[]{:S(2)}, u32[]{:S(2)}) async-start(bf16[32,8,3072]{2,1,0:T(8,128)(2,1)} %bitcast.8), calls=%async_computation.2 | async-start | bytes 3145728 | tf_op jit(solution)/shard_map/all_to_all | solution.py:349
  110.6 0.0 reduce-scatter.2.cloned.1.call-start
  110.6 8.7 %shard_map.113 = (bf16[384,1024]{1,0:T(8,128)(2,1)}, bf16[1024,1024]{1,0:T(8,128)(2,1)}, bf16[1024,1024]{1,0:T(8,128)(2,1)}) custom-call(bf16[256,3072]{1,0:T(8,128)(2,1)} %bitcast.5.got_ref, bf16[2048,1536]{1,0:T(8,128)(2,1)} %bitcast.15, f32[384,512]{1,0:T(8,128)} %copy-done.2, f32[384,512]{1,0:T(8,128)} %copy-done.3, bf16[384,2048]{1,0:T(8,128)(2,1)} %copy-done.1), custom_call_target="tpu_custom_call" | custom-call | flops 2415919104 | bytes 15990784 | tf_op jit(solution)/shard_map/pallas_call | solution.py:326
  119.4 1.9 collective-permute-start
  121.3 0.0 copy-start.9
  121.3 6.5 %shard_map.114 = bf16[256,3072]{1,0:T(8,128)(2,1)} custom-call(bf16[384,1024]{1,0:T(8,128)(2,1)} %get-tuple-element.39.pre_ref, bf16[2048,1536]{1,0:T(8,128)(2,1)} %bitcast.16), custom_call_target="tpu_custom_call" | custom-call | flops 1610612736 | bytes 8650752 | tf_op jit(solution)/shard_map/pallas_call | solution.py:326
  127.8 0.0 collective-permute-done
  127.8 0.0 copy-done.9
  127.8 3.9 %add_convert_fusion = bf16[1024,1024]{1,0:T(8,128)(2,1)} fusion(bf16[1024,1024]{1,0:T(8,128)(2,1)} %collective-permute-done, bf16[1024,1024]{1,0:T(8,128)(2,1)S(1)} %copy-done.9), kind=kLoop, calls=%fused_computation | loop fusion | flops 4194304 | bytes 6291456 | tf_op jit(solution)/shard_map/convert_element_type | solution.py:403
  131.7 0.0 reduce-scatter.2.cloned.1.call-update
  131.7 15.6 %all-to-all-done.2 = bf16[32,8,3072]{2,1,0:T(8,128)(2,1)S(1)} async-done(((bf16[32,8,3072]{2,1,0:T(8,128)(2,1)}), bf16[32,8,3072]{2,1,0:T(8,128)(2,1)S(1)}, u32[]{:S(2)}, u32[]{:S(2)}) %all-to-all-start.2) | async-done | bytes 1572896 | tf_op jit(solution)/shard_map/all_to_all | solution.py:349
  147.4 7.1 %all-to-all-start.3 = ((bf16[32,8,3072]{2,1,0:T(8,128)(2,1)}), bf16[32,8,3072]{2,1,0:T(8,128)(2,1)}, u32[]{:S(2)}, u32[]{:S(2)}) async-start(bf16[32,8,3072]{2,1,0:T(8,128)(2,1)} %bitcast.26), calls=%async_computation.4 | async-start | bytes 3145728 | tf_op jit(solution)/shard_map/all_to_all | solution.py:349
  154.5 1.9 shard_map.115
  156.4 0.6 copy.12
  157.0 24.8 %reduce-scatter.2.cloned.1.call-done = bf16[128,1024]{1,0:T(8,128)(2,1)} async-done(((bf16[1024,1024]{1,0:T(8,128)(2,1)}), bf16[128,1024]{1,0:T(8,128)(2,1)}) %reduce-scatter.2.cloned.1.call-update) | async-done | bytes 262160 | tf_op jit(solution)/shard_map/reduce_scatter | solution.py:404
  181.8 1.0 bitcast_convert_fusion
  182.8 0.8 fusion
  183.6 7.7 %all-to-all-done.3 = bf16[32,8,3072]{2,1,0:T(8,128)(2,1)} async-done(((bf16[32,8,3072]{2,1,0:T(8,128)(2,1)}), bf16[32,8,3072]{2,1,0:T(8,128)(2,1)}, u32[]{:S(2)}, u32[]{:S(2)}) %all-to-all-start.3) | async-done | bytes 1572896 | tf_op jit(solution)/shard_map/all_to_all | solution.py:349
  191.3 2.9 %shard_map.116 = bf16[128,2048]{1,0:T(8,128)(2,1)} custom-call(s32[2,128]{1,0:T(2,128)S(1)} %bitcast.23, bf16[256,3072]{1,0:T(8,128)(2,1)} %bitcast.13.got_ref), custom_call_target="tpu_custom_call" | custom-call | flops 268435456 | bytes 2098176 | tf_op jit(solution)/shard_map/pallas_call | solution.py:326
  (6 shorter events, 0.0 us)
Async XLA Ops:
  7.2 59.5 %all-gather.2.cloned.1.call-start = ((), (), s32[]{:S(2)}) async-start(), calls=%async_computation.5 | async-start | bytes 6684672 | tf_op jit(solution)/shard_map/all_gather | solution.py:362
  7.2 1.0 copy-start.5
  8.3 0.7 copy-start.6
  8.9 2.1 %copy-start.10 = (bf16[1,128,512]{2,1,0:T(8,128)(2,1)S(1)}, bf16[1,128,512]{2,1,0:T(8,128)(2,1)}, u32[]{:S(2)}) copy-start(bf16[1,128,512]{2,1,0:T(8,128)(2,1)} %param.12) | copy-start | bytes 393220
  8.9 2.1 %copy-start.11 = (bf16[1,128,512]{2,1,0:T(8,128)(2,1)S(1)}, bf16[1,128,512]{2,1,0:T(8,128)(2,1)}, u32[]{:S(2)}) copy-start(bf16[1,128,512]{2,1,0:T(8,128)(2,1)} %param.11) | copy-start | bytes 393220
  8.9 2.1 %copy-start.12 = (bf16[1,128,512]{2,1,0:T(8,128)(2,1)S(1)}, bf16[1,128,512]{2,1,0:T(8,128)(2,1)}, u32[]{:S(2)}) copy-start(bf16[1,128,512]{2,1,0:T(8,128)(2,1)} %param.10) | copy-start | bytes 393220
  11.0 11.1 %copy-start.4 = (bf16[128,2048]{1,0:T(8,128)(2,1)S(1)}, bf16[128,2048]{1,0:T(8,128)(2,1)}, u32[]{:S(2)}) copy-start(bf16[128,2048]{1,0:T(8,128)(2,1)} %grad_ref.1) | copy-start | bytes 1572868
  11.0 11.1 %copy-start.7 = (s32[128,2]{0,1:T(2,128)S(1)}, s32[128,2]{0,1:T(2,128)}, u32[]{:S(2)}) copy-start(s32[128,2]{0,1:T(2,128)} %param.9) | copy-start | bytes 3076
  11.0 11.1 %copy-start.8 = (f32[128,2]{0,1:T(2,128)S(1)}, f32[128,2]{0,1:T(2,128)}, u32[]{:S(2)}) copy-start(f32[128,2]{0,1:T(2,128)} %param.8) | copy-start | bytes 3076
  11.8 48.0 %all-to-all-start = ((bf16[32,8,3072]{2,1,0:T(8,128)(2,1)}), bf16[32,8,3072]{2,1,0:T(8,128)(2,1)S(1)}, u32[]{:S(2)}, u32[]{:S(2)}) async-start(bf16[32,8,3072]{2,1,0:T(8,128)(2,1)} %bitcast.2), calls=%async_computation | async-start | bytes 3145728 | tf_op jit(solution)/shard_map/all_to_all | solution.py:349
  59.8 43.7 %all-to-all-start.1 = ((bf16[32,8,3072]{2,1,0:T(8,128)(2,1)}), bf16[32,8,3072]{2,1,0:T(8,128)(2,1)}, u32[]{:S(2)}, u32[]{:S(2)}) async-start(bf16[32,8,3072]{2,1,0:T(8,128)(2,1)} %bitcast.4), calls=%async_computation.1 | async-start | bytes 3145728 | tf_op jit(solution)/shard_map/all_to_all | solution.py:349
  66.6 2.8 %copy-start = (bf16[1,2048,1536]{2,1,0:T(8,128)(2,1)S(1)}, bf16[1,2048,1536]{2,1,0:T(8,128)(2,1)}, u32[]{:S(2)}) copy-start(bf16[1,2048,1536]{2,1,0:T(8,128)(2,1)} %all-gather.2.cloned.1.call-done) | copy-start | bytes 18874372
  74.1 1.2 copy-start.1
  75.2 0.9 copy-start.2
  76.1 0.9 copy-start.3
  103.5 43.8 %all-to-all-start.2 = ((bf16[32,8,3072]{2,1,0:T(8,128)(2,1)}), bf16[32,8,3072]{2,1,0:T(8,128)(2,1)S(1)}, u32[]{:S(2)}, u32[]{:S(2)}) async-start(bf16[32,8,3072]{2,1,0:T(8,128)(2,1)} %bitcast.8), calls=%async_computation.2 | async-start | bytes 3145728 | tf_op jit(solution)/shard_map/all_to_all | solution.py:349
  110.6 71.2 %reduce-scatter.2.cloned.1.call-start = ((), (), s32[]{:S(2)}) async-start(), calls=%async_computation.6 | async-start | bytes 2359296 | tf_op jit(solution)/shard_map/reduce_scatter | solution.py:404
  119.4 8.4 %collective-permute-start = (bf16[1024,1024]{1,0:T(8,128)(2,1)}, bf16[1024,1024]{1,0:T(8,128)(2,1)}, u32[]{:S(2)}, u32[]{:S(2)}) collective-permute-start(bf16[1024,1024]{1,0:T(8,128)(2,1)} %get-tuple-element.43), channel_id=1, source_target_pairs={{0,32},{32,0},{64,96},{96,64},{128,160},{160,128},{192,224},{224,1... | collective-permute-start | bytes 6291464 | tf_op jit(solution)/shard_map/ppermute | solution.py:402
  121.3 6.5 %copy-start.9 = (bf16[1024,1024]{1,0:T(8,128)(2,1)S(1)}, bf16[1024,1024]{1,0:T(8,128)(2,1)}, u32[]{:S(2)}) copy-start(bf16[1024,1024]{1,0:T(8,128)(2,1)} %get-tuple-element.42) | copy-start | bytes 6291460
  147.4 44.0 %all-to-all-start.3 = ((bf16[32,8,3072]{2,1,0:T(8,128)(2,1)}), bf16[32,8,3072]{2,1,0:T(8,128)(2,1)}, u32[]{:S(2)}, u32[]{:S(2)}) async-start(bf16[32,8,3072]{2,1,0:T(8,128)(2,1)} %bitcast.26), calls=%async_computation.4 | async-start | bytes 3145728 | tf_op jit(solution)/shard_map/all_to_all | solution.py:349
Sparse Core Ops, SparseCore 0:
  12.0 54.0 all-gather.1
  131.8 49.9 reduce-scatter.1
